TPU v7x, 256 devices: a whole 4x4x8 slice. The times are simulated.
256 devices in a mesh: ctx: 64 (over x, y_hi, z), tp: 4 (over y_lo, core).
Axes of the slice: x: 4, y: 4 (y_hi: 2, y_lo: 2; y = y_hi * 2 + y_lo), z: 8, core: 2. Of those that a mesh axis runs over, the one named last changes fastest.
Arguments:
- queries: bfloat16 [16384, 2048], P('ctx', 'tp'), may hold values from -6 to 6
- keys: bfloat16 [16384, 2048], P('ctx', 'tp'), may hold values from -6 to 6
- values: bfloat16 [16384, 2048], P('ctx', 'tp'), may hold values from -6 to 6
- out_grad: bfloat16 [16384, 4096], P('ctx', 'tp'), may hold values from -6 to 6
- w_out: bfloat16 [2048, 4096], P('tp'), may hold values from -0.09375 to 0.09375
- offsets: int32 [16, 3], P('tp'), may hold values from 0 to 3, as said below
Outputs:
- query_grad: bfloat16 [16384, 2048], P('ctx', 'tp')
- key_grad: bfloat16 [16384, 2048], P('ctx', 'tp')
- value_grad: bfloat16 [16384, 2048], P('ctx', 'tp')
Inputs may be any that keep to these rules, and one draw needn't show every extreme that they name: offsets[h, l] lies between 0 and 2^l - 1.
All inputs are finite; a program needn't handle non-finite values.
Results may differ from a plain program's by a relative error of at most 0.017.
Values may be sent and summed in bfloat16 or wider, within the bound.
No kernel may reach another device: no remote copies, remote signals or barrier semaphores. Data moves between devices by JAX's collectives and lax.ppermute only.
A program may use at most 64 MiB of HBM per device.

v0:
```python
from functools import reduce
import math

import jax
import jax.numpy as jnp
from jax import lax
from jax.sharding import PartitionSpec as P

LEVELS = 3
KEYS_SEG = 1024


NEGATIVE_FILL = -1e30


def for_sending(array):

    def short(part):
        return part.astype(jnp.bfloat16) if part.dtype == jnp.float32 else part

    return jax.tree.map(short, array)


def passed_along(block, axis, distance):
    devices = range(lax.axis_size(axis))
    route = [((i - distance) % len(devices), i) for i in devices]
    return lax.ppermute(block, axis, route)


def pick_table(offset_col, stride):
    return lax.broadcasted_iota(jnp.int32, (stride, offset_col.shape[0]), 0) == offset_col[None, :]


def pack_rows(whole, pick):
    stride = pick.shape[0]
    grouped = whole.reshape((whole.shape[0] // stride, stride) + whole.shape[1:])
    chosen = pick.reshape((1,) + pick.shape + (1,) * (whole.ndim - 2))
    return jnp.sum(jnp.where(chosen, grouped, jnp.zeros((), whole.dtype)), axis=1)


def spread_rows(packed, pick, fill_value):
    stride = pick.shape[0]
    chosen = pick.reshape((1,) + pick.shape + (1,) * (packed.ndim - 2))
    spread = jnp.where(chosen, packed[:, None], jnp.asarray(fill_value, packed.dtype))
    return spread.reshape((packed.shape[0] * stride,) + packed.shape[1:])


def linked_pairs(offset_col, stride, segment, query_start, key_start, row_count):
    tok_rows = row_count * stride
    total_rows = tok_rows * lax.axis_size("ctx")
    rotation = 2 * tok_rows
    lanes = lax.broadcasted_iota(jnp.int32, (row_count,), 0) * stride
    query_pos = (
        query_start + lanes[None, :, None] + offset_col[:, None, None] - rotation
    ) % total_rows
    key_pos = (key_start + lanes[None, None, :] + offset_col[:, None, None] - rotation) % total_rows
    return (query_pos // segment == key_pos // segment) & (key_pos <= query_pos)


def forward_tile(running, query_pack, key_pair, linked, score_scale):
    row_top, row_total, accumulated = running
    scores = (
        jnp.einsum("ahd,bhd->hab", query_pack, key_pair[0], preferred_element_type=jnp.float32)
        * score_scale
    )
    scores = jnp.where(linked, scores, NEGATIVE_FILL)
    new_top = jnp.maximum(row_top, jnp.max(scores, axis=2).T)
    weights = jnp.where(linked, jnp.exp(scores - new_top.T[:, :, None]), 0.0)
    factor = jnp.exp(row_top - new_top)
    row_total = row_total * factor + jnp.sum(weights, axis=2).T
    weights_high = weights.astype(jnp.bfloat16)
    weights_rest = (weights - weights_high.astype(jnp.float32)).astype(jnp.bfloat16)
    product = jnp.einsum(
        "hab,bhd->ahd", weights_high, key_pair[1], preferred_element_type=jnp.float32
    )
    product = product + jnp.einsum(
        "hab,bhd->ahd", weights_rest, key_pair[1], preferred_element_type=jnp.float32
    )
    accumulated = accumulated * factor[:, :, None] + product
    return (new_top, row_total, accumulated)


def tile_grads(query_side, key_pair, linked, score_scale):
    query_pack, grad_pack, log_pack, delta_pack = query_side
    scores = (
        jnp.einsum("ahd,bhd->hab", query_pack, key_pair[0], preferred_element_type=jnp.float32)
        * score_scale
    )
    scores = jnp.where(linked, scores, NEGATIVE_FILL)
    weights = jnp.where(linked, jnp.exp(scores - log_pack.T[:, :, None]), 0.0)
    prob_grad = jnp.einsum(
        "ahd,bhd->hab", grad_pack, key_pair[1], preferred_element_type=jnp.float32
    )
    score_grad = (weights * (prob_grad - delta_pack.T[:, :, None])).astype(jnp.bfloat16)
    return (weights.astype(jnp.bfloat16), score_grad)


def forward_relay(
    running, query_pack, key_pair, offset_col, stride, segment, relay_turns, score_scale
):
    row_count = query_pack.shape[0]
    tok_rows = row_count * stride
    axis_size = lax.axis_size("ctx")
    device_index = lax.axis_index("ctx")
    stored = (
        jnp.zeros((max(relay_turns, 1),) + key_pair[0].shape, key_pair[0].dtype),
        jnp.zeros((max(relay_turns, 1),) + key_pair[1].shape, key_pair[1].dtype),
    )

    def forward_turn_body(turn_num, carried):
        packet, running, stored = carried
        packet = jax.tree.map(
            lambda part, own: part.astype(own.dtype),
            passed_along(for_sending(packet), "ctx", 1),
            packet,
        )
        key_start = (device_index - turn_num) % axis_size * tok_rows
        linked = linked_pairs(
            offset_col, stride, segment, device_index * tok_rows, key_start, row_count
        )
        running = forward_tile(running, query_pack, packet, linked, score_scale)
        return (packet, running, stored)

    packet, running, stored = lax.fori_loop(
        1, relay_turns + 1, forward_turn_body, (key_pair, running, stored)
    )
    return (running, stored)


def keys_pass(query_side, key_pair, offset_col, stride, segment, relay_turns, score_scale):
    query_pack, grad_pack = (query_side[0], query_side[1])
    row_count = query_pack.shape[0]
    tok_rows = row_count * stride
    axis_size = lax.axis_size("ctx")
    device_index = lax.axis_index("ctx")
    own_start = device_index * tok_rows
    weights_low, score_grad = tile_grads(
        query_side,
        key_pair,
        linked_pairs(offset_col, stride, segment, own_start, own_start, row_count),
        score_scale,
    )
    level_q = jnp.einsum(
        "hab,bhd->ahd", score_grad, key_pair[0], preferred_element_type=jnp.float32
    )
    partial_value = (
        jnp.einsum("hab,ahd->bhd", score_grad, query_pack, preferred_element_type=jnp.float32),
        jnp.einsum("hab,ahd->bhd", weights_low, grad_pack, preferred_element_type=jnp.float32),
    )

    def keys_turn_body(turn_num, carried):
        packet, partial_value, level_q = carried
        packet = jax.tree.map(
            lambda part, own: part.astype(own.dtype),
            passed_along(for_sending(packet), "ctx", 1),
            packet,
        )
        partial_value = jax.tree.map(
            lambda part, own: part.astype(own.dtype),
            passed_along(for_sending(partial_value), "ctx", 1),
            partial_value,
        )
        key_start = (device_index - turn_num) % axis_size * tok_rows
        weights_low, score_grad = tile_grads(
            query_side,
            packet,
            linked_pairs(offset_col, stride, segment, own_start, key_start, row_count),
            score_scale,
        )
        level_q = level_q + jnp.einsum(
            "hab,bhd->ahd", score_grad, packet[0], preferred_element_type=jnp.float32
        )
        partial_value = (
            partial_value[0]
            + jnp.einsum(
                "hab,ahd->bhd", score_grad, query_pack, preferred_element_type=jnp.float32
            ),
            partial_value[1]
            + jnp.einsum(
                "hab,ahd->bhd", weights_low, grad_pack, preferred_element_type=jnp.float32
            ),
        )
        return (packet, partial_value, level_q)

    packet, partial_value, level_q = lax.fori_loop(
        1, relay_turns + 1, keys_turn_body, (key_pair, partial_value, level_q)
    )
    partial_value = (
        passed_along(partial_value[0].astype(jnp.bfloat16), "ctx", -relay_turns).astype(
            jnp.float32
        ),
        passed_along(partial_value[1].astype(jnp.bfloat16), "ctx", -relay_turns).astype(
            jnp.float32
        ),
    )
    return (level_q, partial_value[0], partial_value[1])


def local(queries, keys, values, out_grad, w_out, offsets):
    tok_rows = queries.shape[0]
    head_count = offsets.shape[0]
    head_width = queries.shape[1] // head_count
    axis_size = lax.axis_size("ctx")
    device_index = lax.axis_index("ctx")
    keys_seg = KEYS_SEG
    score_scale = 1.0 / math.sqrt(head_width)
    own_start = device_index * tok_rows
    query_rows = queries.reshape(tok_rows, head_count, head_width)
    key_rows = keys.reshape(tok_rows, head_count, head_width)
    value_rows = values.reshape(tok_rows, head_count, head_width)
    grad_out = jnp.einsum(
        "td,fd->tf",
        lax.all_gather(out_grad, "tp", axis=1, tiled=True),
        w_out,
        preferred_element_type=jnp.float32,
    )
    grad_rows = grad_out.astype(jnp.bfloat16).reshape(tok_rows, head_count, head_width)
    level_data = []
    for level_num in range(LEVELS):
        stride = 2**level_num
        segment = min(keys_seg * stride, tok_rows * axis_size)
        row_count = tok_rows // stride
        relay_turns = min(max(segment // tok_rows, 1), axis_size) - 1
        offset_col = offsets[:, level_num]
        pick = pick_table(offset_col, stride)
        query_pack = pack_rows(query_rows, pick)
        key_pair = (pack_rows(key_rows, pick), pack_rows(value_rows, pick))
        running = (
            jnp.full((row_count, head_count), NEGATIVE_FILL, jnp.float32),
            jnp.zeros((row_count, head_count), jnp.float32),
            jnp.zeros((row_count, head_count, head_width), jnp.float32),
        )
        linked = linked_pairs(offset_col, stride, segment, own_start, own_start, row_count)
        running = forward_tile(running, query_pack, key_pair, linked, score_scale)
        running, stored = forward_relay(
            running, query_pack, key_pair, offset_col, stride, segment, relay_turns, score_scale
        )
        level_data.append(
            (stride, segment, relay_turns, offset_col, pick, query_pack, key_pair, running, stored)
        )
    tops = [spread_rows(entry[7][0], entry[4], NEGATIVE_FILL) for entry in level_data]
    row_top = reduce(jnp.maximum, tops)
    row_total = jnp.zeros((tok_rows, head_count), jnp.float32)
    out_sum = jnp.zeros((tok_rows, head_count, head_width), jnp.float32)
    for entry, level_top in zip(level_data, tops):
        factor = jnp.exp(level_top - row_top)
        row_total = row_total + spread_rows(entry[7][1], entry[4], 0.0) * factor
        out_sum = out_sum + spread_rows(entry[7][2], entry[4], 0.0) * factor[:, :, None]
    log_total = row_top + jnp.log(row_total)
    attn_out = out_sum / row_total[:, :, None]
    delta_rows = jnp.sum(grad_rows.astype(jnp.float32) * attn_out, axis=2)
    grad_q = jnp.zeros((tok_rows, head_count, head_width), jnp.float32)
    grad_k = jnp.zeros((tok_rows, head_count, head_width), jnp.float32)
    grad_v = jnp.zeros((tok_rows, head_count, head_width), jnp.float32)
    for (
        stride,
        segment,
        relay_turns,
        offset_col,
        pick,
        query_pack,
        key_pair,
        running,
        stored,
    ) in level_data:
        query_side = (
            query_pack,
            pack_rows(grad_rows, pick),
            pack_rows(log_total, pick),
            pack_rows(delta_rows, pick),
        )
        level_q, level_k, level_v = keys_pass(
            query_side, key_pair, offset_col, stride, segment, relay_turns, score_scale
        )
        grad_q = grad_q + spread_rows(level_q, pick, 0.0)
        grad_k = grad_k + spread_rows(level_k, pick, 0.0)
        grad_v = grad_v + spread_rows(level_v, pick, 0.0)
    flat_width = head_count * head_width
    return (
        (grad_q * score_scale).reshape(tok_rows, flat_width).astype(jnp.bfloat16),
        (grad_k * score_scale).reshape(tok_rows, flat_width).astype(jnp.bfloat16),
        grad_v.reshape(tok_rows, flat_width).astype(jnp.bfloat16),
    )


def solution(mesh):
    return jax.shard_map(
        local,
        mesh=mesh,
        in_specs=(
            P("ctx", "tp"),
            P("ctx", "tp"),
            P("ctx", "tp"),
            P("ctx", "tp"),
            P("tp", None),
            P("tp", None),
        ),
        out_specs=(P("ctx", "tp"), P("ctx", "tp"), P("ctx", "tp")),
        check_vma=False,
    )
```

profile of v0, /device:TPU:8, one launch (start us, length us, event | category | flops | bytes accessed | tf_op | source)
XLA Modules:
  0.0 897.6 jit_solution(7576920657588802797)
XLA Ops:
  20.9 21.8 %all-gather.2.cloned.1.call-done = bf16[256,4096]{1,0:T(8,128)(2,1)} async-done(((bf16[256,1024]{1,0:T(8,128)(2,1)}), bf16[256,4096]{1,0:T(8,128)(2,1)}) %all-gather.2.cloned.1.call-update) | async-done | bytes 2097168 | tf_op jit(solution)/shard_map/all_gather | solution.py:213
  69.5 71.6 %while.144 = (s32[]{:T(128)}, bf16[256,4,128]{2,0,1:T(8,128)(2,1)}, bf16[256,4,128]{2,0,1:T(8,128)(2,1)}, f32[256,4]{0,1:T(4,128)S(1)}, f32[256,4]{0,1:T(4,128)S...) while((s32[]{:T(128)}, bf16[256,4,128]{2,0,1:T(8,128)(2,1)}, ...), condition=%wide.region_5.6_spmd, body=%wide.region_2.5_spmd.sunk | while | flops 208857616 | bytes 10641786 | solution.py:124
  74.0 10.9 %collective-permute-done = bf16[256,4,128]{2,0,1:T(8,128)(2,1)S(1)} collective-permute-done((bf16[256,4,128]{2,0,1:T(8,128)(2,1)}, bf16[256,4,128]{2,0,1:T(8,128)(2,1)S(1)}, u32[]{:S(2)}, u32[]{:S(2)}) %collective-permute-start) | collective-permute-done | bytes 262176 | tf_op jit(solution)/shard_map/while/body/eval_jaxpr/ppermute | solution.py:27
  95.3 14.3 %collective-permute-done = bf16[256,4,128]{2,0,1:T(8,128)(2,1)S(1)} collective-permute-done((bf16[256,4,128]{2,0,1:T(8,128)(2,1)}, bf16[256,4,128]{2,0,1:T(8,128)(2,1)S(1)}, u32[]{:S(2)}, u32[]{:S(2)}) %collective-permute-start) | collective-permute-done | bytes 262176 | tf_op jit(solution)/shard_map/while/body/eval_jaxpr/ppermute | solution.py:27
  119.1 14.3 %collective-permute-done = bf16[256,4,128]{2,0,1:T(8,128)(2,1)S(1)} collective-permute-done((bf16[256,4,128]{2,0,1:T(8,128)(2,1)}, bf16[256,4,128]{2,0,1:T(8,128)(2,1)S(1)}, u32[]{:S(2)}, u32[]{:S(2)}) %collective-permute-start) | collective-permute-done | bytes 262176 | tf_op jit(solution)/shard_map/while/body/eval_jaxpr/ppermute | solution.py:27
  141.9 173.4 %while.146 = (s32[]{:T(128)}, bf16[64,4,128]{2,0,1:T(8,128)(2,1)S(1)}, bf16[64,4,128]{2,0,1:T(8,128)(2,1)S(1)}, f32[64,4]{0,1:T(4,128)S(1)}, f32[64,4]{0,1:T(4,1...) while((s32[]{:T(128)}, ...), condition=%wide.region_23.24_spmd, body=%wide.region_20.23_spmd.sunk | while | flops 13138703 | bytes 1874298 | solution.py:124
  223.9 9.8 %collective-permute-done.4 = bf16[64,4,128]{2,0,1:T(8,128)(2,1)S(1)} collective-permute-done((bf16[64,4,128]{2,0,1:T(8,128)(2,1)S(1)}, bf16[64,4,128]{2,0,1:T(8,128)(2,1)S(1)}, u32[]{:S(2)}, u32[]{:S(2)}) %collective-permute-start.4) | collective-permute-done | bytes 65568 | tf_op jit(solution)/shard_map/while/body/eval_jaxpr/ppermute | solution.py:27
  318.2 98.9 %while.145 = (s32[]{:T(128)}, bf16[128,4,128]{2,0,1:T(8,128)(2,1)S(1)}, bf16[128,4,128]{2,0,1:T(8,128)(2,1)S(1)}, f32[128,4]{0,1:T(4,128)S(1)}, f32[128,4]{0,1:T...) while((s32[]{:T(128)}, ...), condition=%wide.region_14.15_spmd, body=%wide.region_11.14_spmd.sunk | while | flops 52327952 | bytes 4272506 | solution.py:124
  319.3 9.8 %collective-permute-done.2 = bf16[128,4,128]{2,0,1:T(8,128)(2,1)S(1)} collective-permute-done((bf16[128,4,128]{2,0,1:T(8,128)(2,1)S(1)}, bf16[128,4,128]{2,0,1:T(8,128)(2,1)S(1)}, u32[]{:S(2)}, u32[]{:S(2)}) %collective-permute-start.2) | collective-permute-done | bytes 131104 | tf_op jit(solution)/shard_map/while/body/eval_jaxpr/ppermute | solution.py:27
  333.3 9.8 %collective-permute-done.2 = bf16[128,4,128]{2,0,1:T(8,128)(2,1)S(1)} collective-permute-done((bf16[128,4,128]{2,0,1:T(8,128)(2,1)S(1)}, bf16[128,4,128]{2,0,1:T(8,128)(2,1)S(1)}, u32[]{:S(2)}, u32[]{:S(2)}) %collective-permute-start.2) | collective-permute-done | bytes 131104 | tf_op jit(solution)/shard_map/while/body/eval_jaxpr/ppermute | solution.py:27
  347.4 9.8 %collective-permute-done.2 = bf16[128,4,128]{2,0,1:T(8,128)(2,1)S(1)} collective-permute-done((bf16[128,4,128]{2,0,1:T(8,128)(2,1)S(1)}, bf16[128,4,128]{2,0,1:T(8,128)(2,1)S(1)}, u32[]{:S(2)}, u32[]{:S(2)}) %collective-permute-start.2) | collective-permute-done | bytes 131104 | tf_op jit(solution)/shard_map/while/body/eval_jaxpr/ppermute | solution.py:27
  361.4 9.8 %collective-permute-done.2 = bf16[128,4,128]{2,0,1:T(8,128)(2,1)S(1)} collective-permute-done((bf16[128,4,128]{2,0,1:T(8,128)(2,1)S(1)}, bf16[128,4,128]{2,0,1:T(8,128)(2,1)S(1)}, u32[]{:S(2)}, u32[]{:S(2)}) %collective-permute-start.2) | collective-permute-done | bytes 131104 | tf_op jit(solution)/shard_map/while/body/eval_jaxpr/ppermute | solution.py:27
  375.4 9.8 %collective-permute-done.2 = bf16[128,4,128]{2,0,1:T(8,128)(2,1)S(1)} collective-permute-done((bf16[128,4,128]{2,0,1:T(8,128)(2,1)S(1)}, bf16[128,4,128]{2,0,1:T(8,128)(2,1)S(1)}, u32[]{:S(2)}, u32[]{:S(2)}) %collective-permute-start.2) | collective-permute-done | bytes 131104 | tf_op jit(solution)/shard_map/while/body/eval_jaxpr/ppermute | solution.py:27
  390.1 9.8 %collective-permute-done.2 = bf16[128,4,128]{2,0,1:T(8,128)(2,1)S(1)} collective-permute-done((bf16[128,4,128]{2,0,1:T(8,128)(2,1)S(1)}, bf16[128,4,128]{2,0,1:T(8,128)(2,1)S(1)}, u32[]{:S(2)}, u32[]{:S(2)}) %collective-permute-start.2) | collective-permute-done | bytes 131104 | tf_op jit(solution)/shard_map/while/body/eval_jaxpr/ppermute | solution.py:27
  404.1 9.8 %collective-permute-done.2 = bf16[128,4,128]{2,0,1:T(8,128)(2,1)S(1)} collective-permute-done((bf16[128,4,128]{2,0,1:T(8,128)(2,1)S(1)}, bf16[128,4,128]{2,0,1:T(8,128)(2,1)S(1)}, u32[]{:S(2)}, u32[]{:S(2)}) %collective-permute-start.2) | collective-permute-done | bytes 131104 | tf_op jit(solution)/shard_map/while/body/eval_jaxpr/ppermute | solution.py:27
  457.5 74.9 %while.147 = (s32[]{:T(128)}, bf16[256,4,128]{2,0,1:T(8,128)(2,1)S(1)}, bf16[256,4,128]{2,0,1:T(8,128)(2,1)S(1)}, bf16[256,4,128]{2,0,1:T(8,128)(2,1)}, bf16[256...) while((s32[]{:T(128)}, ...), condition=%wide.region_26.27_spmd, body=%wide.region_25.26_spmd.sunk | while | flops 339403264 | bytes 13939170 | solution.py:185
  458.7 13.9 %collective-permute-done.6 = bf16[256,4,128]{2,0,1:T(8,128)(2,1)S(1)} collective-permute-done((bf16[256,4,128]{2,0,1:T(8,128)(2,1)S(1)}, bf16[256,4,128]{2,0,1:T(8,128)(2,1)S(1)}, u32[]{:S(2)}, u32[]{:S(2)}) %collective-permute-start.6) | collective-permute-done | bytes 262176 | tf_op jit(solution)/shard_map/while/body/eval_jaxpr/ppermute | solution.py:27
  484.7 14.1 %collective-permute-done.6 = bf16[256,4,128]{2,0,1:T(8,128)(2,1)S(1)} collective-permute-done((bf16[256,4,128]{2,0,1:T(8,128)(2,1)S(1)}, bf16[256,4,128]{2,0,1:T(8,128)(2,1)S(1)}, u32[]{:S(2)}, u32[]{:S(2)}) %collective-permute-start.6) | collective-permute-done | bytes 262176 | tf_op jit(solution)/shard_map/while/body/eval_jaxpr/ppermute | solution.py:27
  510.0 11.4 %collective-permute-done.6 = bf16[256,4,128]{2,0,1:T(8,128)(2,1)S(1)} collective-permute-done((bf16[256,4,128]{2,0,1:T(8,128)(2,1)S(1)}, bf16[256,4,128]{2,0,1:T(8,128)(2,1)S(1)}, u32[]{:S(2)}, u32[]{:S(2)}) %collective-permute-start.6) | collective-permute-done | bytes 262176 | tf_op jit(solution)/shard_map/while/body/eval_jaxpr/ppermute | solution.py:27
  534.8 134.4 %while.148 = (s32[]{:T(128)}, bf16[128,4,128]{2,0,1:T(8,128)(2,1)}, bf16[128,4,128]{2,0,1:T(8,128)(2,1)S(1)}, bf16[128,4,128]{2,0,1:T(8,128)(2,1)}, bf16[128,4,1...) while((s32[]{:T(128)}, bf16[128,4,128]{2,0,1:T(8,128)(2,1)}, ...), condition=%wide.region_31.32_spmd, body=%wide.region_30.31_spmd.sunk | while | flops 85094928 | bytes 5790178 | solution.py:185
  557.4 11.4 %collective-permute-done.10 = bf16[128,4,128]{2,0,1:T(8,128)(2,1)S(1)} collective-permute-done((bf16[128,4,128]{2,0,1:T(8,128)(2,1)}, bf16[128,4,128]{2,0,1:T(8,128)(2,1)S(1)}, u32[]{:S(2)}, u32[]{:S(2)}) %collective-permute-start.10) | collective-permute-done | bytes 131104 | tf_op jit(solution)/shard_map/while/body/eval_jaxpr/ppermute | solution.py:27
  578.2 11.5 %collective-permute-done.10 = bf16[128,4,128]{2,0,1:T(8,128)(2,1)S(1)} collective-permute-done((bf16[128,4,128]{2,0,1:T(8,128)(2,1)}, bf16[128,4,128]{2,0,1:T(8,128)(2,1)S(1)}, u32[]{:S(2)}, u32[]{:S(2)}) %collective-permute-start.10) | collective-permute-done | bytes 131104 | tf_op jit(solution)/shard_map/while/body/eval_jaxpr/ppermute | solution.py:27
  598.1 11.5 %collective-permute-done.10 = bf16[128,4,128]{2,0,1:T(8,128)(2,1)S(1)} collective-permute-done((bf16[128,4,128]{2,0,1:T(8,128)(2,1)}, bf16[128,4,128]{2,0,1:T(8,128)(2,1)S(1)}, u32[]{:S(2)}, u32[]{:S(2)}) %collective-permute-start.10) | collective-permute-done | bytes 131104 | tf_op jit(solution)/shard_map/while/body/eval_jaxpr/ppermute | solution.py:27
  617.1 11.5 %collective-permute-done.10 = bf16[128,4,128]{2,0,1:T(8,128)(2,1)S(1)} collective-permute-done((bf16[128,4,128]{2,0,1:T(8,128)(2,1)}, bf16[128,4,128]{2,0,1:T(8,128)(2,1)S(1)}, u32[]{:S(2)}, u32[]{:S(2)}) %collective-permute-start.10) | collective-permute-done | bytes 131104 | tf_op jit(solution)/shard_map/while/body/eval_jaxpr/ppermute | solution.py:27
  635.2 10.1 %collective-permute-done.10 = bf16[128,4,128]{2,0,1:T(8,128)(2,1)S(1)} collective-permute-done((bf16[128,4,128]{2,0,1:T(8,128)(2,1)}, bf16[128,4,128]{2,0,1:T(8,128)(2,1)S(1)}, u32[]{:S(2)}, u32[]{:S(2)}) %collective-permute-start.10) | collective-permute-done | bytes 131104 | tf_op jit(solution)/shard_map/while/body/eval_jaxpr/ppermute | solution.py:27
  651.2 10.1 %collective-permute-done.10 = bf16[128,4,128]{2,0,1:T(8,128)(2,1)S(1)} collective-permute-done((bf16[128,4,128]{2,0,1:T(8,128)(2,1)}, bf16[128,4,128]{2,0,1:T(8,128)(2,1)S(1)}, u32[]{:S(2)}, u32[]{:S(2)}) %collective-permute-start.10) | collective-permute-done | bytes 131104 | tf_op jit(solution)/shard_map/while/body/eval_jaxpr/ppermute | solution.py:27
  669.3 194.8 %while.149 = (s32[]{:T(128)}, bf16[64,4,128]{2,0,1:T(8,128)(2,1)S(1)}, bf16[64,4,128]{2,0,1:T(8,128)(2,1)S(1)}, bf16[64,4,128]{2,0,1:T(8,128)(2,1)S(1)}, bf16[64...) while((s32[]{:T(128)}, ...), condition=%wide.region_36.37_spmd, body=%wide.region_35.36_spmd.sunk | while | flops 21395728 | bytes 2600418 | solution.py:185
  669.8 10.0 %collective-permute-done.14 = bf16[64,4,128]{2,0,1:T(8,128)(2,1)S(1)} collective-permute-done((bf16[64,4,128]{2,0,1:T(8,128)(2,1)S(1)}, bf16[64,4,128]{2,0,1:T(8,128)(2,1)S(1)}, u32[]{:S(2)}, u32[]{:S(2)}) %collective-permute-start.14) | collective-permute-done | bytes 65568 | tf_op jit(solution)/shard_map/while/body/eval_jaxpr/ppermute | solution.py:27
  695.1 9.6 %collective-permute-done.14 = bf16[64,4,128]{2,0,1:T(8,128)(2,1)S(1)} collective-permute-done((bf16[64,4,128]{2,0,1:T(8,128)(2,1)S(1)}, bf16[64,4,128]{2,0,1:T(8,128)(2,1)S(1)}, u32[]{:S(2)}, u32[]{:S(2)}) %collective-permute-start.14) | collective-permute-done | bytes 65568 | tf_op jit(solution)/shard_map/while/body/eval_jaxpr/ppermute | solution.py:27
  771.6 10.2 %collective-permute-done.14 = bf16[64,4,128]{2,0,1:T(8,128)(2,1)S(1)} collective-permute-done((bf16[64,4,128]{2,0,1:T(8,128)(2,1)S(1)}, bf16[64,4,128]{2,0,1:T(8,128)(2,1)S(1)}, u32[]{:S(2)}, u32[]{:S(2)}) %collective-permute-start.14) | collective-permute-done | bytes 65568 | tf_op jit(solution)/shard_map/while/body/eval_jaxpr/ppermute | solution.py:27
  786.8 10.3 %collective-permute-done.14 = bf16[64,4,128]{2,0,1:T(8,128)(2,1)S(1)} collective-permute-done((bf16[64,4,128]{2,0,1:T(8,128)(2,1)S(1)}, bf16[64,4,128]{2,0,1:T(8,128)(2,1)S(1)}, u32[]{:S(2)}, u32[]{:S(2)}) %collective-permute-start.14) | collective-permute-done | bytes 65568 | tf_op jit(solution)/shard_map/while/body/eval_jaxpr/ppermute | solution.py:27
  801.1 10.3 %collective-permute-done.14 = bf16[64,4,128]{2,0,1:T(8,128)(2,1)S(1)} collective-permute-done((bf16[64,4,128]{2,0,1:T(8,128)(2,1)S(1)}, bf16[64,4,128]{2,0,1:T(8,128)(2,1)S(1)}, u32[]{:S(2)}, u32[]{:S(2)}) %collective-permute-start.14) | collective-permute-done | bytes 65568 | tf_op jit(solution)/shard_map/while/body/eval_jaxpr/ppermute | solution.py:27
  (1178 shorter events, 580.2 us)
Async XLA Ops:
  7.2 35.5 %all-gather.2.cloned.1.call-start = ((), (), s32[]{:S(2)}) async-start(), calls=%async_computation | async-start | bytes 2621440 | tf_op jit(solution)/shard_map/all_gather | solution.py:213
  69.5 15.4 %collective-permute-start = (bf16[256,4,128]{2,0,1:T(8,128)(2,1)}, bf16[256,4,128]{2,0,1:T(8,128)(2,1)S(1)}, u32[]{:S(2)}, u32[]{:S(2)}) collective-permute-start(bf16[256,4,128]{2,0,1:T(8,128)(2,1)} %get-tuple-element.3054), channel_id=1, source_target_pairs={{252,0},{0,4},{4,8},{8,12},{12,16},{16,20},{20,24},{24,28},{28,32}... | collective-permute-start | bytes 786440 | tf_op jit(solution)/shard_map/while/body/eval_jaxpr/ppermute | solution.py:27
  71.8 18.5 %collective-permute-start.1 = (bf16[256,4,128]{2,0,1:T(8,128)(2,1)}, bf16[256,4,128]{2,0,1:T(8,128)(2,1)S(1)}, u32[]{:S(2)}, u32[]{:S(2)}) collective-permute-start(bf16[256,4,128]{2,0,1:T(8,128)(2,1)} %get-tuple-element.3055), channel_id=1, source_target_pairs={{252,0},{0,4},{4,8},{8,12},{12,16},{16,20},{20,24},{24,28},{28,32}... | collective-permute-start | bytes 786440 | tf_op jit(solution)/shard_map/while/body/eval_jaxpr/ppermute | solution.py:27
  94.4 15.2 %collective-permute-start = (bf16[256,4,128]{2,0,1:T(8,128)(2,1)}, bf16[256,4,128]{2,0,1:T(8,128)(2,1)S(1)}, u32[]{:S(2)}, u32[]{:S(2)}) collective-permute-start(bf16[256,4,128]{2,0,1:T(8,128)(2,1)} %get-tuple-element.3054), channel_id=1, source_target_pairs={{252,0},{0,4},{4,8},{8,12},{12,16},{16,20},{20,24},{24,28},{28,32}... | collective-permute-start | bytes 786440 | tf_op jit(solution)/shard_map/while/body/eval_jaxpr/ppermute | solution.py:27
  94.4 19.6 %collective-permute-start.1 = (bf16[256,4,128]{2,0,1:T(8,128)(2,1)}, bf16[256,4,128]{2,0,1:T(8,128)(2,1)S(1)}, u32[]{:S(2)}, u32[]{:S(2)}) collective-permute-start(bf16[256,4,128]{2,0,1:T(8,128)(2,1)} %get-tuple-element.3055), channel_id=1, source_target_pairs={{252,0},{0,4},{4,8},{8,12},{12,16},{16,20},{20,24},{24,28},{28,32}... | collective-permute-start | bytes 786440 | tf_op jit(solution)/shard_map/while/body/eval_jaxpr/ppermute | solution.py:27
  118.2 15.3 %collective-permute-start = (bf16[256,4,128]{2,0,1:T(8,128)(2,1)}, bf16[256,4,128]{2,0,1:T(8,128)(2,1)S(1)}, u32[]{:S(2)}, u32[]{:S(2)}) collective-permute-start(bf16[256,4,128]{2,0,1:T(8,128)(2,1)} %get-tuple-element.3054), channel_id=1, source_target_pairs={{252,0},{0,4},{4,8},{8,12},{12,16},{16,20},{20,24},{24,28},{28,32}... | collective-permute-start | bytes 786440 | tf_op jit(solution)/shard_map/while/body/eval_jaxpr/ppermute | solution.py:27
  118.3 18.7 %collective-permute-start.1 = (bf16[256,4,128]{2,0,1:T(8,128)(2,1)}, bf16[256,4,128]{2,0,1:T(8,128)(2,1)S(1)}, u32[]{:S(2)}, u32[]{:S(2)}) collective-permute-start(bf16[256,4,128]{2,0,1:T(8,128)(2,1)} %get-tuple-element.3055), channel_id=1, source_target_pairs={{252,0},{0,4},{4,8},{8,12},{12,16},{16,20},{20,24},{24,28},{28,32}... | collective-permute-start | bytes 786440 | tf_op jit(solution)/shard_map/while/body/eval_jaxpr/ppermute | solution.py:27
  457.6 19.5 %collective-permute-start.7 = (bf16[256,4,128]{2,0,1:T(8,128)(2,1)S(1)}, bf16[256,4,128]{2,0,1:T(8,128)(2,1)S(1)}, u32[]{:S(2)}, u32[]{:S(2)}) collective-permute-start(bf16[256,4,128]{2,0,1:T(8,128)(2,1)S(1)} %get-tuple-element.3157), channel_id=1, source_target_pairs={{252,0},{0,4},{4,8},{8,12},{12,16},{16,20},{20,24},{24,28},{28,32}... | collective-permute-start | bytes 786440 | tf_op jit(solution)/shard_map/while/body/eval_jaxpr/ppermute | solution.py:27
  457.7 22.3 %collective-permute-start.8 = (bf16[256,4,128]{2,0,1:T(8,128)(2,1)}, bf16[256,4,128]{2,0,1:T(8,128)(2,1)S(1)}, u32[]{:S(2)}, u32[]{:S(2)}) collective-permute-start(bf16[256,4,128]{2,0,1:T(8,128)(2,1)} %get-tuple-element.3158), channel_id=1, source_target_pairs={{252,0},{0,4},{4,8},{8,12},{12,16},{16,20},{20,24},{24,28},{28,32}... | collective-permute-start | bytes 786440 | tf_op jit(solution)/shard_map/while/body/eval_jaxpr/ppermute | solution.py:27
  457.8 25.0 %collective-permute-start.9 = (bf16[256,4,128]{2,0,1:T(8,128)(2,1)}, bf16[256,4,128]{2,0,1:T(8,128)(2,1)S(1)}, u32[]{:S(2)}, u32[]{:S(2)}) collective-permute-start(bf16[256,4,128]{2,0,1:T(8,128)(2,1)} %get-tuple-element.3159), channel_id=1, source_target_pairs={{252,0},{0,4},{4,8},{8,12},{12,16},{16,20},{20,24},{24,28},{28,32}... | collective-permute-start | bytes 786440 | tf_op jit(solution)/shard_map/while/body/eval_jaxpr/ppermute | solution.py:27
  483.8 18.6 %collective-permute-start.7 = (bf16[256,4,128]{2,0,1:T(8,128)(2,1)S(1)}, bf16[256,4,128]{2,0,1:T(8,128)(2,1)S(1)}, u32[]{:S(2)}, u32[]{:S(2)}) collective-permute-start(bf16[256,4,128]{2,0,1:T(8,128)(2,1)S(1)} %get-tuple-element.3157), channel_id=1, source_target_pairs={{252,0},{0,4},{4,8},{8,12},{12,16},{16,20},{20,24},{24,28},{28,32}... | collective-permute-start | bytes 786440 | tf_op jit(solution)/shard_map/while/body/eval_jaxpr/ppermute | solution.py:27
  483.8 21.4 %collective-permute-start.8 = (bf16[256,4,128]{2,0,1:T(8,128)(2,1)}, bf16[256,4,128]{2,0,1:T(8,128)(2,1)S(1)}, u32[]{:S(2)}, u32[]{:S(2)}) collective-permute-start(bf16[256,4,128]{2,0,1:T(8,128)(2,1)} %get-tuple-element.3158), channel_id=1, source_target_pairs={{252,0},{0,4},{4,8},{8,12},{12,16},{16,20},{20,24},{24,28},{28,32}... | collective-permute-start | bytes 786440 | tf_op jit(solution)/shard_map/while/body/eval_jaxpr/ppermute | solution.py:27
  483.9 24.2 %collective-permute-start.9 = (bf16[256,4,128]{2,0,1:T(8,128)(2,1)}, bf16[256,4,128]{2,0,1:T(8,128)(2,1)S(1)}, u32[]{:S(2)}, u32[]{:S(2)}) collective-permute-start(bf16[256,4,128]{2,0,1:T(8,128)(2,1)} %get-tuple-element.3159), channel_id=1, source_target_pairs={{252,0},{0,4},{4,8},{8,12},{12,16},{16,20},{20,24},{24,28},{28,32}... | collective-permute-start | bytes 786440 | tf_op jit(solution)/shard_map/while/body/eval_jaxpr/ppermute | solution.py:27
  509.1 17.9 %collective-permute-start.8 = (bf16[256,4,128]{2,0,1:T(8,128)(2,1)}, bf16[256,4,128]{2,0,1:T(8,128)(2,1)S(1)}, u32[]{:S(2)}, u32[]{:S(2)}) collective-permute-start(bf16[256,4,128]{2,0,1:T(8,128)(2,1)} %get-tuple-element.3158), channel_id=1, source_target_pairs={{252,0},{0,4},{4,8},{8,12},{12,16},{16,20},{20,24},{24,28},{28,32}... | collective-permute-start | bytes 786440 | tf_op jit(solution)/shard_map/while/body/eval_jaxpr/ppermute | solution.py:27
  509.1 22.2 %collective-permute-start.9 = (bf16[256,4,128]{2,0,1:T(8,128)(2,1)}, bf16[256,4,128]{2,0,1:T(8,128)(2,1)S(1)}, u32[]{:S(2)}, u32[]{:S(2)}) collective-permute-start(bf16[256,4,128]{2,0,1:T(8,128)(2,1)} %get-tuple-element.3159), channel_id=1, source_target_pairs={{252,0},{0,4},{4,8},{8,12},{12,16},{16,20},{20,24},{24,28},{28,32}... | collective-permute-start | bytes 786440 | tf_op jit(solution)/shard_map/while/body/eval_jaxpr/ppermute | solution.py:27
  533.5 350.4 %collective-permute-start.18 = (bf16[256,4,128]{0,2,1:T(8,128)(2,1)S(1)}, bf16[256,4,128]{0,2,1:T(8,128)(2,1)}, u32[]{:S(2)}, u32[]{:S(2)}) collective-permute-start(bf16[256,4,128]{0,2,1:T(8,128)(2,1)S(1)} %copy.528), channel_id=1, source_target_pairs={{12,0},{16,4},{20,8},{24,12},{28,16},{32,20},{36,24},{40,28},{44,3... | collective-permute-start | bytes 786440 | tf_op jit(solution)/shard_map/ppermute | solution.py:27
  537.6 15.3 %collective-permute-start.12 = (bf16[128,4,128]{2,0,1:T(8,128)(2,1)}, bf16[128,4,128]{2,0,1:T(8,128)(2,1)S(1)}, u32[]{:S(2)}, u32[]{:S(2)}) collective-permute-start(bf16[128,4,128]{2,0,1:T(8,128)(2,1)} %get-tuple-element.3212), channel_id=1, source_target_pairs={{252,0},{0,4},{4,8},{8,12},{12,16},{16,20},{20,24},{24,28},{28,32}... | collective-permute-start | bytes 393224 | tf_op jit(solution)/shard_map/while/body/eval_jaxpr/ppermute | solution.py:27
  540.0 15.7 %collective-permute-start.13 = (bf16[128,4,128]{2,0,1:T(8,128)(2,1)}, bf16[128,4,128]{2,0,1:T(8,128)(2,1)S(1)}, u32[]{:S(2)}, u32[]{:S(2)}) collective-permute-start(bf16[128,4,128]{2,0,1:T(8,128)(2,1)} %get-tuple-element.3213), channel_id=1, source_target_pairs={{252,0},{0,4},{4,8},{8,12},{12,16},{16,20},{20,24},{24,28},{28,32}... | collective-permute-start | bytes 393224 | tf_op jit(solution)/shard_map/while/body/eval_jaxpr/ppermute | solution.py:27
  556.6 17.9 %collective-permute-start.12 = (bf16[128,4,128]{2,0,1:T(8,128)(2,1)}, bf16[128,4,128]{2,0,1:T(8,128)(2,1)S(1)}, u32[]{:S(2)}, u32[]{:S(2)}) collective-permute-start(bf16[128,4,128]{2,0,1:T(8,128)(2,1)} %get-tuple-element.3212), channel_id=1, source_target_pairs={{252,0},{0,4},{4,8},{8,12},{12,16},{16,20},{20,24},{24,28},{28,32}... | collective-permute-start | bytes 393224 | tf_op jit(solution)/shard_map/while/body/eval_jaxpr/ppermute | solution.py:27
  556.6 19.9 %collective-permute-start.13 = (bf16[128,4,128]{2,0,1:T(8,128)(2,1)}, bf16[128,4,128]{2,0,1:T(8,128)(2,1)S(1)}, u32[]{:S(2)}, u32[]{:S(2)}) collective-permute-start(bf16[128,4,128]{2,0,1:T(8,128)(2,1)} %get-tuple-element.3213), channel_id=1, source_target_pairs={{252,0},{0,4},{4,8},{8,12},{12,16},{16,20},{20,24},{24,28},{28,32}... | collective-permute-start | bytes 393224 | tf_op jit(solution)/shard_map/while/body/eval_jaxpr/ppermute | solution.py:27
  577.4 15.2 %collective-permute-start.11 = (bf16[128,4,128]{2,0,1:T(8,128)(2,1)S(1)}, bf16[128,4,128]{2,0,1:T(8,128)(2,1)S(1)}, u32[]{:S(2)}, u32[]{:S(2)}) collective-permute-start(bf16[128,4,128]{2,0,1:T(8,128)(2,1)S(1)} %get-tuple-element.3211), channel_id=1, source_target_pairs={{252,0},{0,4},{4,8},{8,12},{12,16},{16,20},{20,24},{24,28},{28,32}... | collective-permute-start | bytes 393224 | tf_op jit(solution)/shard_map/while/body/eval_jaxpr/ppermute | solution.py:27
  577.4 17.6 %collective-permute-start.12 = (bf16[128,4,128]{2,0,1:T(8,128)(2,1)}, bf16[128,4,128]{2,0,1:T(8,128)(2,1)S(1)}, u32[]{:S(2)}, u32[]{:S(2)}) collective-permute-start(bf16[128,4,128]{2,0,1:T(8,128)(2,1)} %get-tuple-element.3212), channel_id=1, source_target_pairs={{252,0},{0,4},{4,8},{8,12},{12,16},{16,20},{20,24},{24,28},{28,32}... | collective-permute-start | bytes 393224 | tf_op jit(solution)/shard_map/while/body/eval_jaxpr/ppermute | solution.py:27
  577.4 19.0 %collective-permute-start.13 = (bf16[128,4,128]{2,0,1:T(8,128)(2,1)}, bf16[128,4,128]{2,0,1:T(8,128)(2,1)S(1)}, u32[]{:S(2)}, u32[]{:S(2)}) collective-permute-start(bf16[128,4,128]{2,0,1:T(8,128)(2,1)} %get-tuple-element.3213), channel_id=1, source_target_pairs={{252,0},{0,4},{4,8},{8,12},{12,16},{16,20},{20,24},{24,28},{28,32}... | collective-permute-start | bytes 393224 | tf_op jit(solution)/shard_map/while/body/eval_jaxpr/ppermute | solution.py:27
  597.3 16.7 %collective-permute-start.12 = (bf16[128,4,128]{2,0,1:T(8,128)(2,1)}, bf16[128,4,128]{2,0,1:T(8,128)(2,1)S(1)}, u32[]{:S(2)}, u32[]{:S(2)}) collective-permute-start(bf16[128,4,128]{2,0,1:T(8,128)(2,1)} %get-tuple-element.3212), channel_id=1, source_target_pairs={{252,0},{0,4},{4,8},{8,12},{12,16},{16,20},{20,24},{24,28},{28,32}... | collective-permute-start | bytes 393224 | tf_op jit(solution)/shard_map/while/body/eval_jaxpr/ppermute | solution.py:27
  597.3 18.1 %collective-permute-start.13 = (bf16[128,4,128]{2,0,1:T(8,128)(2,1)}, bf16[128,4,128]{2,0,1:T(8,128)(2,1)S(1)}, u32[]{:S(2)}, u32[]{:S(2)}) collective-permute-start(bf16[128,4,128]{2,0,1:T(8,128)(2,1)} %get-tuple-element.3213), channel_id=1, source_target_pairs={{252,0},{0,4},{4,8},{8,12},{12,16},{16,20},{20,24},{24,28},{28,32}... | collective-permute-start | bytes 393224 | tf_op jit(solution)/shard_map/while/body/eval_jaxpr/ppermute | solution.py:27
  616.3 15.9 %collective-permute-start.12 = (bf16[128,4,128]{2,0,1:T(8,128)(2,1)}, bf16[128,4,128]{2,0,1:T(8,128)(2,1)S(1)}, u32[]{:S(2)}, u32[]{:S(2)}) collective-permute-start(bf16[128,4,128]{2,0,1:T(8,128)(2,1)} %get-tuple-element.3212), channel_id=1, source_target_pairs={{252,0},{0,4},{4,8},{8,12},{12,16},{16,20},{20,24},{24,28},{28,32}... | collective-permute-start | bytes 393224 | tf_op jit(solution)/shard_map/while/body/eval_jaxpr/ppermute | solution.py:27
  616.3 17.2 %collective-permute-start.13 = (bf16[128,4,128]{2,0,1:T(8,128)(2,1)}, bf16[128,4,128]{2,0,1:T(8,128)(2,1)S(1)}, u32[]{:S(2)}, u32[]{:S(2)}) collective-permute-start(bf16[128,4,128]{2,0,1:T(8,128)(2,1)} %get-tuple-element.3213), channel_id=1, source_target_pairs={{252,0},{0,4},{4,8},{8,12},{12,16},{16,20},{20,24},{24,28},{28,32}... | collective-permute-start | bytes 393224 | tf_op jit(solution)/shard_map/while/body/eval_jaxpr/ppermute | solution.py:27
  650.4 15.8 %collective-permute-start.12 = (bf16[128,4,128]{2,0,1:T(8,128)(2,1)}, bf16[128,4,128]{2,0,1:T(8,128)(2,1)S(1)}, u32[]{:S(2)}, u32[]{:S(2)}) collective-permute-start(bf16[128,4,128]{2,0,1:T(8,128)(2,1)} %get-tuple-element.3212), channel_id=1, source_target_pairs={{252,0},{0,4},{4,8},{8,12},{12,16},{16,20},{20,24},{24,28},{28,32}... | collective-permute-start | bytes 393224 | tf_op jit(solution)/shard_map/while/body/eval_jaxpr/ppermute | solution.py:27
  650.4 17.9 %collective-permute-start.13 = (bf16[128,4,128]{2,0,1:T(8,128)(2,1)}, bf16[128,4,128]{2,0,1:T(8,128)(2,1)S(1)}, u32[]{:S(2)}, u32[]{:S(2)}) collective-permute-start(bf16[128,4,128]{2,0,1:T(8,128)(2,1)} %get-tuple-element.3213), channel_id=1, source_target_pairs={{252,0},{0,4},{4,8},{8,12},{12,16},{16,20},{20,24},{24,28},{28,32}... | collective-permute-start | bytes 393224 | tf_op jit(solution)/shard_map/while/body/eval_jaxpr/ppermute | solution.py:27
  864.1 19.9 %collective-permute-start.21 = (bf16[256,4,128]{0,2,1:T(8,128)(2,1)S(1)}, bf16[256,4,128]{0,2,1:T(8,128)(2,1)}, u32[]{:S(2)}, u32[]{:S(2)}) collective-permute-start(bf16[256,4,128]{0,2,1:T(8,128)(2,1)S(1)} %copy.534), channel_id=1, source_target_pairs={{12,0},{16,4},{20,8},{24,12},{28,16},{32,20},{36,24},{40,28},{44,3... | collective-permute-start | bytes 786440 | tf_op jit(solution)/shard_map/ppermute | solution.py:27
  867.0 16.7 %collective-permute-start.22 = (bf16[128,4,128]{2,0,1:T(8,128)(2,1)S(1)}, bf16[128,4,128]{2,0,1:T(8,128)(2,1)S(1)}, u32[]{:S(2)}, u32[]{:S(2)}) collective-permute-start(bf16[128,4,128]{2,0,1:T(8,128)(2,1)S(1)} %copy-done.37), channel_id=1, source_target_pairs={{28,0},{32,4},{36,8},{40,12},{44,16},{48,20},{52,24},{56,28},{60,3... | collective-permute-start | bytes 393224 | tf_op jit(solution)/shard_map/ppermute | solution.py:27
  867.0 16.8 %collective-permute-start.19 = (bf16[128,4,128]{2,0,1:T(8,128)(2,1)S(1)}, bf16[128,4,128]{2,0,1:T(8,128)(2,1)S(1)}, u32[]{:S(2)}, u32[]{:S(2)}) collective-permute-start(bf16[128,4,128]{2,0,1:T(8,128)(2,1)S(1)} %copy-done.36), channel_id=1, source_target_pairs={{28,0},{32,4},{36,8},{40,12},{44,16},{48,20},{52,24},{56,28},{60,3... | collective-permute-start | bytes 393224 | tf_op jit(solution)/shard_map/ppermute | solution.py:27
  (213 other events, 6776.7 us)
Sparse Core Ops, SparseCore 0:
  9.8 32.8 all-gather.1
where the time goes:
time: 902 us; the launch traced here: 898 us
  waiting for transfers between devices  624 us (69%)
  matrix products  112 us (12%)
  local copies, waits for them, and re-layouts  60.7 us (7%)
  other arithmetic  57.5 us (6%)
  starting transfers between devices  22.4 us (2%)
  between operations  15.9 us (2%)
    ppermute x156, waiting for transfers between devices, passed_along(): return lax.ppermute(block, axis, route)  601 us
    select_n x53, other arithmetic, linked_pairs(): return (query_pos // segment == key_pos // segment) & (key_pos <= query_pos)  25.9 us
    ppermute x156, starting transfers between devices, passed_along(): return lax.ppermute(block, axis, route)  22.3 us
    all_gather x1, waiting for transfers between devices, local(): lax.all_gather(out_grad, 'tp', axis=1, tiled=True)  21.8 us
  transfers between devices with their start and end apart: 157, of which 144 were waited for; matrix products, arithmetic and copies ran while one was open for 13% of the time, Pallas kernels for 0%

commit v1 on v0

v1 whole, which is shorter than its diff:
```python
import functools
import math

import jax
import jax.numpy as jnp
from jax import lax
from jax.experimental import pallas as pl
from jax.experimental.pallas import tpu as pltpu
from jax.sharding import PartitionSpec as P

TOK = 256
DIM = 128
BLOCK = 4 * TOK
SCALE = 1.0 / math.sqrt(DIM)
SCALE2 = SCALE * math.log2(math.e)
NEG = -1e30
F32 = jnp.float32
BF16 = jnp.bfloat16


def token_of_row(row):
    return 4 * (row & 63) + 2 * ((row >> 6) & 1) + (row >> 7)


def token_of_row_1(row):
    return 4 * (row & 63) + 2 * (row >> 6)


def iota(shape, dim):
    return lax.broadcasted_iota(jnp.int32, shape, dim)


def dot_nt(a, b):
    return lax.dot_general(a, b, (((1,), (1,)), ((), ())), preferred_element_type=F32)


def dot_nn(a, b):
    return lax.dot_general(a, b, (((1,), (0,)), ((), ())), preferred_element_type=F32)


def dot_tn(a, b):
    return lax.dot_general(a, b, (((0,), (0,)), ((), ())), preferred_element_type=F32)


def rows_at(start, size, unit=64):
    return pl.ds(pl.multiple_of(start, unit), size)


def cols_at(head):
    return pl.ds(pl.multiple_of(head * DIM, DIM), DIM)


def sort_matrix():
    return (iota((TOK, TOK), 1) == token_of_row(iota((TOK, TOK), 0))).astype(BF16)


def unsort_matrix():
    return (iota((TOK, TOK), 0) == token_of_row(iota((TOK, TOK), 1))).astype(BF16)


def wide_max(scores):
    return jnp.broadcast_to(jnp.max(scores, axis=1, keepdims=True), (scores.shape[0], DIM))


def call(kernel, outs, scratch=(), name=None, flops=0, bytes_accessed=0):
    def run(meta, *args):
        return pl.pallas_call(
            kernel,
            out_shape=[jax.ShapeDtypeStruct(shape, dtype) for shape, dtype in outs],
            in_specs=[pl.BlockSpec(memory_space=pltpu.SMEM)]
            + [pl.BlockSpec(memory_space=pltpu.VMEM)] * len(args),
            out_specs=[pl.BlockSpec(memory_space=pltpu.VMEM)] * len(outs),
            scratch_shapes=list(scratch),
            compiler_params=pltpu.CompilerParams(vmem_limit_bytes=40 << 20),
            cost_estimate=pl.CostEstimate(
                flops=flops, bytes_accessed=bytes_accessed, transcendentals=0
            ),
            name=name,
        )(meta, *args)

    return run


def pack_kernel(meta, q, k, v, *outs):
    kvs, qs = outs[:4], outs[4:]
    sort = sort_matrix()
    for s in range(4):
        head = (meta[0] + s) & 3
        kvs[s][:TOK] = dot_nn(sort, k[:, cols_at(head)]).astype(BF16)
        kvs[s][TOK:] = dot_nn(sort, v[:, cols_at(head)]).astype(BF16)
        qs[s][...] = dot_nn(sort, q[:, cols_at(head)]).astype(BF16)


def gather_kernel(meta, p0, p1, p2, p3, kv, kv1, kv2):
    for s, piece in enumerate((p0, p1, p2, p3)):
        place = (meta[0] - s) & 3
        for part in range(2):
            own = piece.at[part * TOK : (part + 1) * TOK]
            kv[rows_at(part * BLOCK + place * TOK, TOK)] = own[...]
            kv1[rows_at(part * 512 + place * 128, 128)] = own[rows_at(meta[2] * 128, 128)]
            kv2[rows_at(part * 256 + place * 64, 64)] = own[rows_at(meta[3] * 64, 64)]


def grad_kernel(meta, g0, g1, g2, g3, w, *outs):
    tp = meta[4]
    total = None
    for m, part in enumerate((g0, g1, g2, g3)):
        width = part.shape[1]
        cols = pl.ds(pl.multiple_of((tp ^ m) * width, width), width)
        term = dot_nt(part[...], w[:, cols])
        total = term if total is None else total + term
    sort = sort_matrix()
    sorted_grad = outs[4]
    sorted_grad[...] = dot_nn(sort, total.astype(BF16)).astype(BF16)
    for s in range(4):
        outs[s][...] = sorted_grad[:, cols_at((meta[0] + s) & 3)]


def ones_beside(target, values):
    target[:, :DIM] = values
    target[:, DIM:] = jnp.ones((target.shape[0], DIM), BF16)


def own_forward_kernel(
    meta, q0, q1, q2, q3, kv, kv1, kv2, qa, e0, e1, e2, top, out, vx0, vx1, vx2
):
    off1, group2 = meta[2], meta[3]
    for s, piece in enumerate((q0, q1, q2, q3)):
        qa[rows_at(((meta[0] - s) & 3) * TOK, TOK)] = piece[...]
    ones_beside(vx0, kv[BLOCK:])
    ones_beside(vx1, kv1[512:])
    ones_beside(vx2, kv2[256:])
    mask0 = token_of_row(iota((256, 256), 1)) <= token_of_row(iota((256, 256), 0))
    mask1 = token_of_row_1(iota((128, 128), 1)) <= token_of_row_1(iota((128, 128), 0))
    for b in range(4):
        strip = slice(b * 256, (b + 1) * 256)
        rows1 = rows_at(b * 256 + off1 * 128, 128)
        rows2 = rows_at(b * 256 + group2 * 64, 64)
        d1 = slice(b * 128, (b + 1) * 128)
        d2 = slice(b * 64, (b + 1) * 64)
        query, query1, query2 = qa[strip], qa[rows1], qa[rows2]
        near0 = jnp.where(mask0, dot_nt(query, kv[strip]) * SCALE2, NEG)
        near1 = jnp.where(mask1, dot_nt(query1, kv1[d1]) * SCALE2, NEG)
        mask2 = iota((64, 256), 1) <= iota((64, 256), 0) + b * 64
        all2 = jnp.where(mask2, dot_nt(query2, kv2[:256]) * SCALE2, NEG)
        high = wide_max(near0)
        high1 = wide_max(near1)
        if b:
            far0 = dot_nt(query, kv[: b * 256]) * SCALE2
            far1 = dot_nt(query1, kv1[: b * 128]) * SCALE2
            high = jnp.maximum(high, wide_max(far0))
            high1 = jnp.maximum(high1, wide_max(far1))
        top[strip] = high
        top[rows1] = jnp.maximum(top[rows1], high1)
        top[rows2] = jnp.maximum(top[rows2], wide_max(all2))
        top0, top1, top2 = top[strip][:, :1], top[rows1][:, :1], top[rows2][:, :1]
        w = jnp.exp2(near0 - top0).astype(BF16)
        e0[strip, strip] = w
        total = dot_nn(w, vx0[strip])
        if b:
            w = jnp.exp2(far0 - top0).astype(BF16)
            e0[strip, : b * 256] = w
            total = total + dot_nn(w, vx0[: b * 256])
        out[strip] = total
        w = jnp.exp2(near1 - top1).astype(BF16)
        e1[d1, d1] = w
        total = dot_nn(w, vx1[d1])
        if b:
            w = jnp.exp2(far1 - top1).astype(BF16)
            e1[d1, : b * 128] = w
            total = total + dot_nn(w, vx1[: b * 128])
        out[rows1] += total
        w = jnp.exp2(all2 - top2).astype(BF16)
        e2[d2] = w
        out[rows2] += dot_nn(w, vx2[...])


def cross_kernel(
    meta, qa, x1, x21, x22, x23, top, out, p0, p1, p2, p3,
    doa, dq, factor, delta, g1, g21, g22, g23,
    pq1, pq2, pd1, pd2, sc1, sc2, e1, e2, newtop, newout, inv, vx1, vx2,
):
    block, off1, group2 = meta[1], meta[2], meta[3]
    second = (block & 1) == 1
    earlier = ((x21, g21), (x22, g22), (x23, g23))
    for s, piece in enumerate((p0, p1, p2, p3)):
        doa[rows_at(((meta[0] - s) & 3) * TOK, TOK)] = piece[...]
    where1 = [rows_at(b * 256 + off1 * 128, 128) for b in range(4)]
    where2 = [rows_at(b * 256 + group2 * 64, 64) for b in range(4)]
    for b in range(4):
        pq1[b * 128 : (b + 1) * 128] = qa[where1[b]]
        pq2[b * 64 : (b + 1) * 64] = qa[where2[b]]
    newtop[...] = top[...]

    @pl.when(second)
    def _():
        ones_beside(vx1, x1[512:])
        sc1[...] = dot_nt(pq1[...], x1[:512]) * SCALE2
        for b in range(4):
            high = wide_max(sc1[b * 128 : (b + 1) * 128])
            newtop[where1[b]] = jnp.maximum(newtop[where1[b]], high)

    for d, (x2, _) in enumerate(earlier):

        @pl.when(block > d)
        def _(d=d, x2=x2):
            ones_beside(vx2.at[d], x2[256:])
            sc2[d] = dot_nt(pq2[...], x2[:256]) * SCALE2
            for b in range(4):
                high = wide_max(sc2[d, b * 64 : (b + 1) * 64])
                newtop[where2[b]] = jnp.maximum(newtop[where2[b]], high)

    shrink = jnp.exp2(top[...] - newtop[...])
    newout[:, :DIM] = out[:, :DIM] * shrink
    newout[:, DIM:] = out[:, DIM:] * shrink

    @pl.when(second)
    def _():
        for b in range(4):
            part = slice(b * 128, (b + 1) * 128)
            w = jnp.exp2(sc1[part] - newtop[where1[b]][:, :1]).astype(BF16)
            e1[part] = w
            newout[where1[b]] += dot_nn(w, vx1[...])

    for d in range(3):

        @pl.when(block > d)
        def _(d=d):
            for b in range(4):
                part = slice(b * 64, (b + 1) * 64)
                w = jnp.exp2(sc2[d, part] - newtop[where2[b]][:, :1]).astype(BF16)
                e2[d, part] = w
                newout[where2[b]] += dot_nn(w, vx2[d])

    inv[...] = 1.0 / newout[:, DIM:]
    grads = doa[...].astype(F32)
    row_delta = jnp.sum(grads * newout[:, :DIM] * inv[...], axis=1, keepdims=True)
    delta[...] = jnp.broadcast_to(row_delta, delta.shape)
    factor[...] = shrink * inv[...]
    dq[...] = jnp.zeros(dq.shape, F32)
    for b in range(4):
        pd1[b * 128 : (b + 1) * 128] = (doa[where1[b]].astype(F32) * inv[where1[b]]).astype(BF16)
        pd2[b * 64 : (b + 1) * 64] = (doa[where2[b]].astype(F32) * inv[where2[b]]).astype(BF16)

    @pl.when(second)
    def _():
        prob = dot_nt(pd1[...], x1[512:])
        level = jnp.concatenate([(delta[r] * inv[r])[:, :1] for r in where1], axis=0)
        score_grad = (e1[...].astype(F32) * (prob - level)).astype(BF16)
        part = dot_nn(score_grad, x1[:512])
        for b in range(4):
            dq[where1[b]] += part[b * 128 : (b + 1) * 128]
        g1[:512] = (dot_tn(score_grad, pq1[...]) * SCALE).astype(BF16)
        g1[512:] = dot_tn(e1[...], pd1[...]).astype(BF16)

    for d, (x2, g2) in enumerate(earlier):

        @pl.when(block > d)
        def _(d=d, x2=x2, g2=g2):
            prob = dot_nt(pd2[...], x2[256:])
            level = jnp.concatenate([(delta[r] * inv[r])[:, :1] for r in where2], axis=0)
            score_grad = (e2[d].astype(F32) * (prob - level)).astype(BF16)
            part = dot_nn(score_grad, x2[:256])
            for b in range(4):
                dq[where2[b]] += part[b * 64 : (b + 1) * 64]
            g2[:256] = (dot_tn(score_grad, pq2[...]) * SCALE).astype(BF16)
            g2[256:] = dot_tn(e2[d], pd2[...]).astype(BF16)


def own_backward_kernel(
    meta, e0, e1, e2, factor, delta, doa, qa, kv, kv1, kv2, dq_in,
    o0, o1, o2, o3, dkv, dq, low, shift, dkv1, dkv2, low_q,
):
    off1, group2 = meta[2], meta[3]
    low[...] = (doa[...].astype(F32) * factor[...]).astype(BF16)
    shift[...] = factor[...] * delta[...]
    dq[...] = dq_in[...]
    for b in range(3, -1, -1):
        strip = slice(b * 256, (b + 1) * 256)
        n0, n1 = (b + 1) * 256, (b + 1) * 128
        rows1 = rows_at(b * 256 + off1 * 128, 128)
        rows2 = rows_at(b * 256 + group2 * 64, 64)
        d1 = slice(b * 128, (b + 1) * 128)
        d2 = slice(b * 64, (b + 1) * 64)
        parts = (
            (strip, strip, e0, kv, BLOCK, n0, dkv),
            (rows1, d1, e1, kv1, 512, n1, dkv1),
            (rows2, d2, e2, kv2, 256, 256, dkv2),
        )
        for rows, part, weights, pair, half, count, grads in parts:
            grad_low = low[rows]
            prob = dot_nt(grad_low, pair[half : half + count])
            w = weights[part, :count]
            score_grad = (w.astype(F32) * (prob - shift[rows][:, :1])).astype(BF16)
            dq[rows] += dot_nn(score_grad, pair[:count])
            key_term = dot_tn(score_grad, qa[rows])
            value_term = dot_tn(w, grad_low)
            if b == 3:
                grads[:count] = key_term
                grads[half : half + count] = value_term
            else:
                grads[:count] += key_term
                grads[half : half + count] += value_term
    for p in range(4):
        for part in range(2):
            dkv[rows_at(part * BLOCK + p * 256 + off1 * 128, 128)] += dkv1[
                part * 512 + p * 128 : part * 512 + (p + 1) * 128
            ]
            dkv[rows_at(part * BLOCK + p * 256 + group2 * 64, 64)] += dkv2[
                part * 256 + p * 64 : part * 256 + (p + 1) * 64
            ]
    dkv[:BLOCK] = dkv[:BLOCK] * SCALE
    low_q[...] = (dq[...] * SCALE).astype(BF16)
    for s, target in enumerate((o0, o1, o2, o3)):
        target[...] = low_q[rows_at(((meta[0] + s) & 3) * TOK, TOK)]


def combine_kernel(meta, dkv, y1, y21, y22, y23, o0, o1, o2, o3, total):
    off1, group2 = meta[2], meta[3]
    total[...] = dkv[...]
    for p in range(4):
        for part in range(2):
            one = slice(part * 512 + p * 128, part * 512 + (p + 1) * 128)
            two = slice(part * 256 + p * 64, part * 256 + (p + 1) * 64)
            total[rows_at(part * BLOCK + p * 256 + off1 * 128, 128)] += y1[one].astype(F32)
            total[rows_at(part * BLOCK + p * 256 + group2 * 64, 64)] += (
                y21[two].astype(F32) + y22[two].astype(F32) + y23[two].astype(F32)
            )
    for s, target in enumerate((o0, o1, o2, o3)):
        place = (meta[0] + s) & 3
        for part in range(2):
            target[part * TOK : (part + 1) * TOK] = total[
                rows_at(part * BLOCK + place * TOK, TOK)
            ].astype(BF16)


def finish_kernel(meta, q0, q1, q2, q3, r0, r1, r2, r3, dq, dk, dv):
    unsort = unsort_matrix()
    for s, (query, pair) in enumerate(((q0, r0), (q1, r1), (q2, r2), (q3, r3))):
        cols = cols_at((meta[0] - s) & 3)
        dq[:, cols] = dot_nn(unsort, query[...]).astype(BF16)
        dk[:, cols] = dot_nn(unsort, pair[:TOK]).astype(BF16)
        dv[:, cols] = dot_nn(unsort, pair[TOK:]).astype(BF16)


def local(queries, keys, values, out_grad, w_out, offsets):
    devices = lax.axis_size("ctx")
    seat = (lax.axis_index("ctx") - 2) % devices
    place, block, tp = seat % 4, seat // 4 % 4, lax.axis_index("tp")
    own = lax.dynamic_slice_in_dim(offsets, place, 1, 0)[0]
    meta = jnp.stack([place, block, own[1], ((own[2] & 1) << 1) | (own[2] >> 1), tp])

    def at(index):
        return (index + 2) % devices

    def exchange(part, s):
        route = [
            (at(u), at(u // 4 * 4 + (u % 4 + s) % 4)) for u in range(devices)
        ]
        return lax.ppermute(part, "ctx", route)

    def to_block(part, distance, blocks):
        route = [
            (at(u), at(u + 4 * distance)) for u in range(devices) if u // 4 % 4 in blocks
        ]
        return lax.ppermute(part, "ctx", route)

    def across(part, m):
        return lax.ppermute(part, "tp", [(i, i ^ m) for i in range(4)])

    packed = call(
        pack_kernel, [((2 * TOK, DIM), BF16)] * 4 + [((TOK, DIM), BF16)] * 4, name="pack"
    )(meta, queries, keys, values)
    pairs = [packed[0]] + [exchange(packed[s], s) for s in (1, 2, 3)]
    grad_y = across(out_grad, 2)
    query_parts = [packed[4]] + [exchange(packed[4 + s], s) for s in (1, 2, 3)]
    grad_core = across(out_grad, 1)
    grad_far = across(grad_y, 1)

    kv, kv1, kv2 = call(
        gather_kernel,
        [((2 * BLOCK, DIM), BF16), ((1024, DIM), BF16), ((512, DIM), BF16)],
        name="gather",
    )(meta, *pairs)
    x1 = to_block(kv1, 1, (0, 2))
    x2 = [to_block(kv2, d, range(4 - d)) for d in (1, 2, 3)]

    grads = call(
        grad_kernel,
        [((TOK, DIM), BF16)] * 4,
        [pltpu.VMEM((TOK, 4 * DIM), BF16)],
        name="grad",
        flops=2 * TOK * 512 * 4096,
        bytes_accessed=6 << 20,
    )(meta, out_grad, grad_core, grad_y, grad_far, w_out)
    grad_parts = [grads[0]] + [exchange(grads[s], s) for s in (1, 2, 3)]

    qa, e0, e1, e2, top, out = call(
        own_forward_kernel,
        [
            ((BLOCK, DIM), BF16),
            ((BLOCK, BLOCK), BF16),
            ((512, 512), BF16),
            ((256, 256), BF16),
            ((BLOCK, DIM), F32),
            ((BLOCK, 2 * DIM), F32),
        ],
        [
            pltpu.VMEM((BLOCK, 2 * DIM), BF16),
            pltpu.VMEM((512, 2 * DIM), BF16),
            pltpu.VMEM((256, 2 * DIM), BF16),
        ],
        name="own_forward",
        flops=10**9,
        bytes_accessed=6 << 20,
    )(meta, *query_parts, kv, kv1, kv2)

    doa, dq, factor, delta, g1, g21, g22, g23 = call(
        cross_kernel,
        [
            ((BLOCK, DIM), BF16),
            ((BLOCK, DIM), F32),
            ((BLOCK, DIM), F32),
            ((BLOCK, DIM), F32),
            ((1024, DIM), BF16),
            ((512, DIM), BF16),
            ((512, DIM), BF16),
            ((512, DIM), BF16),
        ],
        [
            pltpu.VMEM((512, DIM), BF16),
            pltpu.VMEM((256, DIM), BF16),
            pltpu.VMEM((512, DIM), BF16),
            pltpu.VMEM((256, DIM), BF16),
            pltpu.VMEM((512, 512), F32),
            pltpu.VMEM((3, 256, 256), F32),
            pltpu.VMEM((512, 512), BF16),
            pltpu.VMEM((3, 256, 256), BF16),
            pltpu.VMEM((BLOCK, DIM), F32),
            pltpu.VMEM((BLOCK, 2 * DIM), F32),
            pltpu.VMEM((BLOCK, DIM), F32),
            pltpu.VMEM((512, 2 * DIM), BF16),
            pltpu.VMEM((3, 256, 2 * DIM), BF16),
        ],
        name="cross",
        flops=10**9,
        bytes_accessed=6 << 20,
    )(meta, qa, x1, *x2, top, out, *grad_parts)
    y1 = to_block(g1, -1, (1, 3))
    y2 = [to_block(g, -d, range(d, 4)) for d, g in ((1, g21), (2, g22), (3, g23))]

    *dq_parts, dkv = call(
        own_backward_kernel,
        [((TOK, DIM), BF16)] * 4 + [((2 * BLOCK, DIM), F32)],
        [
            pltpu.VMEM((BLOCK, DIM), F32),
            pltpu.VMEM((BLOCK, DIM), BF16),
            pltpu.VMEM((BLOCK, DIM), F32),
            pltpu.VMEM((1024, DIM), F32),
            pltpu.VMEM((512, DIM), F32),
            pltpu.VMEM((BLOCK, DIM), BF16),
        ],
        name="own_backward",
        flops=2 * 10**9,
        bytes_accessed=8 << 20,
    )(meta, e0, e1, e2, factor, delta, doa, qa, kv, kv1, kv2, dq)
    dq_parts = [dq_parts[0]] + [exchange(dq_parts[s], s) for s in (1, 2, 3)]

    pairs = call(
        combine_kernel,
        [((2 * TOK, DIM), BF16)] * 4,
        [pltpu.VMEM((2 * BLOCK, DIM), F32)],
        name="combine",
    )(meta, dkv, y1, *y2)
    pairs = [pairs[0]] + [exchange(pairs[s], s) for s in (1, 2, 3)]
    return tuple(
        call(finish_kernel, [((TOK, 4 * DIM), BF16)] * 3, name="finish")(meta, *dq_parts, *pairs)
    )


def solution(mesh):
    return jax.shard_map(
        local,
        mesh=mesh,
        in_specs=(
            P("ctx", "tp"),
            P("ctx", "tp"),
            P("ctx", "tp"),
            P("ctx", "tp"),
            P("tp", None),
            P("tp", None),
        ),
        out_specs=(P("ctx", "tp"), P("ctx", "tp"), P("ctx", "tp")),
        check_vma=False,
    )
```

time: 902 us -> 141 us (0.16)
  the two profiles are of different devices: /device:TPU:8 before, /device:TPU:33 now
where the time goes in v1:
time: 141 us
  starting transfers between devices  70.4 us (50%)
  waiting for transfers between devices  40.7 us (29%)
  Pallas kernels  19.9 us (14%)
  local copies, waits for them, and re-layouts  7.41 us (5%)
  between operations  2.17 us (2%)
    ppermute x15, starting transfers between devices, exchange(): return lax.ppermute(part, 'ctx', route)  56.2 us
    ppermute x15, waiting for transfers between devices, exchange(): return lax.ppermute(part, 'ctx', route)  29.9 us
    pallas_call x8, Pallas kernels, run(): pl.pallas_call(kernel, out_shape=[jax.ShapeDtypeStruct(shape, dtype) for...  19.9 us
    ppermute x3, waiting for transfers between devices, across(): return lax.ppermute(part, 'tp', [(i, i ^ m) for i in range(4)])  10.8 us
    ppermute x8, starting transfers between devices, to_block(): return lax.ppermute(part, 'ctx', route)  10.4 us
    unnamed x12, local copies, waits for them, and re-layouts  6.08 us
    ppermute x3, starting transfers between devices, across(): return lax.ppermute(part, 'tp', [(i, i ^ m) for i in range(4)])  3.89 us
  transfers between devices with their start and end apart: 26, of which 8 were waited for; matrix products, arithmetic and copies ran while one was open for 1% of the time, Pallas kernels for 9%

profile of v1, /device:TPU:33, one launch (start us, length us, event | category | flops | bytes accessed | tf_op | source)
XLA Modules:
  0.0 140.6 jit_solution(7072419614683060244)
XLA Ops:
  0.6 1.4 collective-permute-start.11
  3.0 10.8 %collective-permute-done.11.g2 = bf16[256,1024]{1,0:T(8,128)(2,1)S(1)} collective-permute-done((bf16[256,1024]{1,0:T(8,128)(2,1)}, bf16[256,1024]{1,0:T(8,128)(2,1)S(1)}, u32[]{:S(2)}, u32[]{:S(2)}) %collective-permute-start.11) | collective-permute-done | bytes 524320 | tf_op jit(solution)/shard_map/ppermute | solution.py:369
  13.7 1.5 %collective-permute-start.12 = (bf16[256,1024]{1,0:T(8,128)(2,1)S(1)}, bf16[256,1024]{1,0:T(8,128)(2,1)S(1)}, u32[]{:S(2)}, u32[]{:S(2)}) collective-permute-start(bf16[256,1024]{1,0:T(8,128)(2,1)S(1)} %collective-permute-done.11.g2), channel_id=1, source_target_pairs={{0,1},{1,0},{2,3},{3,2},{4,5},{5,4},{6,7},{7,6},{8,9},{9,8},{10,11... | collective-permute-start | bytes 1572872 | tf_op jit(solution)/shard_map/ppermute | solution.py:369
  21.9 10.5 %collective-permute-start.3 = (bf16[512,128]{1,0:T(8,128)(2,1)S(1)}, bf16[512,128]{1,0:T(8,128)(2,1)S(1)}, u32[]{:S(2)}, u32[]{:S(2)}) collective-permute-start(bf16[512,128]{1,0:T(8,128)(2,1)S(1)} %get-tuple-element.46), channel_id=1, source_target_pairs={{8,12},{12,16},{16,20},{20,8},{24,28},{28,32},{32,36},{36,24},{40,... | collective-permute-start | bytes 393224 | tf_op jit(solution)/shard_map/ppermute | solution.py:360
  33.4 2.0 %collective-permute-done.3.p1 = bf16[512,128]{1,0:T(8,128)(2,1)S(1)} collective-permute-done((bf16[512,128]{1,0:T(8,128)(2,1)S(1)}, bf16[512,128]{1,0:T(8,128)(2,1)S(1)}, u32[]{:S(2)}, u32[]{:S(2)}) %collective-permute-start.3) | collective-permute-done | bytes 131104 | tf_op jit(solution)/shard_map/ppermute | solution.py:360
  35.3 9.7 %collective-permute-start = (bf16[256,128]{1,0:T(8,128)(2,1)S(1)}, bf16[256,128]{1,0:T(8,128)(2,1)S(1)}, u32[]{:S(2)}, u32[]{:S(2)}) collective-permute-start(bf16[256,128]{1,0:T(8,128)(2,1)S(1)} %get-tuple-element.42), channel_id=1, source_target_pairs={{8,12},{12,16},{16,20},{20,8},{24,28},{28,32},{32,36},{36,24},{40,... | collective-permute-start | bytes 196616 | tf_op jit(solution)/shard_map/ppermute | solution.py:360
  45.0 1.5 %collective-permute-done.4.p2 = bf16[512,128]{1,0:T(8,128)(2,1)S(1)} collective-permute-done((bf16[512,128]{1,0:T(8,128)(2,1)S(1)}, bf16[512,128]{1,0:T(8,128)(2,1)S(1)}, u32[]{:S(2)}, u32[]{:S(2)}) %collective-permute-start.4) | collective-permute-done | bytes 131104 | tf_op jit(solution)/shard_map/ppermute | solution.py:360
  48.3 1.3 collective-permute-start.6
  49.6 1.3 collective-permute-start.9
  50.9 5.5 %collective-permute-done.1.q2 = bf16[256,128]{1,0:T(8,128)(2,1)S(1)} collective-permute-done((bf16[256,128]{1,0:T(8,128)(2,1)S(1)}, bf16[256,128]{1,0:T(8,128)(2,1)S(1)}, u32[]{:S(2)}, u32[]{:S(2)}) %collective-permute-start.1) | collective-permute-done | bytes 65568 | tf_op jit(solution)/shard_map/ppermute | solution.py:360
  57.7 1.3 collective-permute-start.7
  59.0 2.2 %copy-done.1 = bf16[512,4096]{1,0:T(8,128)(2,1)S(1)} copy-done((bf16[512,4096]{1,0:T(8,128)(2,1)S(1)}, bf16[512,4096]{1,0:T(8,128)(2,1)}, u32[]{:S(2)}) %copy-start.1) | copy-done | bytes 4194328
  62.3 2.1 %grad.1 = (bf16[256,128]{1,0:T(8,128)(2,1)S(1)}, bf16[256,128]{1,0:T(8,128)(2,1)S(1)}, bf16[256,128]{1,0:T(8,128)(2,1)S(1)}, bf16[256,128]{1,0:T(8,128)(2,1)S(1)}) custom-call(s32[5]{0:T(128)S(1)} %stack.19.meta, bf16[256,1024]{1,0:T(8,128)(2,1)S(1)} %copy-done.2, bf16[256,1024]{1,0:T(8,128)(2,1)S(1)} %collective-permute-done.10.g1, ...), custom_call_target="tpu_custom_call" | custom-call | flops 1073741824 | bytes 6291456 | tf_op jit(solution)/shard_map/grad/pallas_call | solution.py:67
  64.4 5.5 %collective-permute-done.2.q3 = bf16[256,128]{1,0:T(8,128)(2,1)S(1)} collective-permute-done((bf16[256,128]{1,0:T(8,128)(2,1)S(1)}, bf16[256,128]{1,0:T(8,128)(2,1)S(1)}, u32[]{:S(2)}, u32[]{:S(2)}) %collective-permute-start.2) | collective-permute-done | bytes 65568 | tf_op jit(solution)/shard_map/ppermute | solution.py:360
  69.9 3.5 %collective-permute-start.13 = (bf16[256,128]{1,0:T(8,128)(2,1)S(1)}, bf16[256,128]{1,0:T(8,128)(2,1)S(1)}, u32[]{:S(2)}, u32[]{:S(2)}) collective-permute-start(bf16[256,128]{1,0:T(8,128)(2,1)S(1)} %get-tuple-element.59), channel_id=1, source_target_pairs={{8,12},{12,16},{16,20},{20,8},{24,28},{28,32},{32,36},{36,24},{40,... | collective-permute-start | bytes 196616 | tf_op jit(solution)/shard_map/ppermute | solution.py:360
  73.4 3.3 %collective-permute-start.14 = (bf16[256,128]{1,0:T(8,128)(2,1)S(1)}, bf16[256,128]{1,0:T(8,128)(2,1)S(1)}, u32[]{:S(2)}, u32[]{:S(2)}) collective-permute-start(bf16[256,128]{1,0:T(8,128)(2,1)S(1)} %get-tuple-element.60), channel_id=1, source_target_pairs={{8,16},{12,20},{16,8},{20,12},{24,32},{28,36},{32,24},{36,28},{40,... | collective-permute-start | bytes 196616 | tf_op jit(solution)/shard_map/ppermute | solution.py:360
  76.7 3.4 %own_forward.1 = (bf16[1024,128]{1,0:T(8,128)(2,1)S(1)}, bf16[1024,1024]{1,0:T(8,128)(2,1)S(1)}, bf16[512,512]{1,0:T(8,128)(2,1)S(1)}, bf16[256,256]{1,0:T(8,128...) custom-call(s32[5]{0:T(128)S(1)} %stack.19.meta, bf16[256,128]{1,0:T(8,128)(2,1)S(1)} %get-tuple-element.41.q0, ...), custom_call_target="tpu_custom_call" | custom-call | flops 1000000000 | bytes 6291456 | tf_op jit(solution)/shard_map/own_forward/pallas_call | solution.py:67
  80.1 3.2 %collective-permute-done.14.p2 = bf16[256,128]{1,0:T(8,128)(2,1)S(1)} collective-permute-done((bf16[256,128]{1,0:T(8,128)(2,1)S(1)}, bf16[256,128]{1,0:T(8,128)(2,1)S(1)}, u32[]{:S(2)}, u32[]{:S(2)}) %collective-permute-start.14) | collective-permute-done | bytes 65568 | tf_op jit(solution)/shard_map/ppermute | solution.py:360
  83.3 4.3 %collective-permute-done.15.p3 = bf16[256,128]{1,0:T(8,128)(2,1)S(1)} collective-permute-done((bf16[256,128]{1,0:T(8,128)(2,1)S(1)}, bf16[256,128]{1,0:T(8,128)(2,1)S(1)}, u32[]{:S(2)}, u32[]{:S(2)}) %collective-permute-start.15) | collective-permute-done | bytes 65568 | tf_op jit(solution)/shard_map/ppermute | solution.py:360
  87.6 5.6 %cross.1 = (bf16[1024,128]{1,0:T(8,128)(2,1)S(1)}, f32[1024,128]{1,0:T(8,128)S(1)}, f32[1024,128]{1,0:T(8,128)S(1)}, f32[1024,128]{1,0:T(8,128)S(1)}, bf16[1024,...) custom-call(s32[5]{0:T(128)S(1)} %stack.19.meta, ...), custom_call_target="tpu_custom_call" | custom-call | flops 1000000000 | bytes 6291456 | tf_op jit(solution)/shard_map/cross/pallas_call | solution.py:67
  93.2 1.3 collective-permute-start.19
  94.5 1.3 collective-permute-start.20
  95.8 1.3 collective-permute-start.21
  97.1 1.3 collective-permute-start.22
  98.4 4.5 %own_backward.1 = (bf16[256,128]{1,0:T(8,128)(2,1)S(1)}, bf16[256,128]{1,0:T(8,128)(2,1)S(1)}, bf16[256,128]{1,0:T(8,128)(2,1)S(1)}, bf16[256,128]{1,0:T(8,128)(2,1)S(1)}, f32[2048,128]{1,0:T(8,128)S(1)}) custom-call(s32[5]{0:T(128)S(1)} %stack.19.meta, bf16[1024,1024]{1,0:T(8,128)(2,1)S(1)} %get-tuple-element.52.e0, ...), custom_call_target="tpu_custom_call" | custom-call | flops 2000000000 | bytes 8388608 | tf_op jit(solution)/shard_map/own_backward/pallas_call | solution.py:67
  102.9 1.6 %collective-permute-start.16 = (bf16[256,128]{1,0:T(8,128)(2,1)S(1)}, bf16[256,128]{1,0:T(8,128)(2,1)S(1)}, u32[]{:S(2)}, u32[]{:S(2)}) collective-permute-start(bf16[256,128]{1,0:T(8,128)(2,1)S(1)} %get-tuple-element.67), channel_id=1, source_target_pairs={{8,12},{12,16},{16,20},{20,8},{24,28},{28,32},{32,36},{36,24},{40,... | collective-permute-start | bytes 196616 | tf_op jit(solution)/shard_map/ppermute | solution.py:360
  105.3 3.8 %collective-permute-start.23 = (bf16[512,128]{1,0:T(8,128)(2,1)S(1)}, bf16[512,128]{1,0:T(8,128)(2,1)S(1)}, u32[]{:S(2)}, u32[]{:S(2)}) collective-permute-start(bf16[512,128]{1,0:T(8,128)(2,1)S(1)} %get-tuple-element.76), channel_id=1, source_target_pairs={{8,12},{12,16},{16,20},{20,8},{24,28},{28,32},{32,36},{36,24},{40,... | collective-permute-start | bytes 393224 | tf_op jit(solution)/shard_map/ppermute | solution.py:360
  109.2 12.4 %collective-permute-start.24 = (bf16[512,128]{1,0:T(8,128)(2,1)S(1)}, bf16[512,128]{1,0:T(8,128)(2,1)S(1)}, u32[]{:S(2)}, u32[]{:S(2)}) collective-permute-start(bf16[512,128]{1,0:T(8,128)(2,1)S(1)} %get-tuple-element.77), channel_id=1, source_target_pairs={{8,16},{12,20},{16,8},{20,12},{24,32},{28,36},{32,24},{36,28},{40,... | collective-permute-start | bytes 393224 | tf_op jit(solution)/shard_map/ppermute | solution.py:360
  121.6 1.4 collective-permute-start.25
  122.9 7.9 %collective-permute-start.18 = (bf16[256,128]{1,0:T(8,128)(2,1)S(1)}, bf16[256,128]{1,0:T(8,128)(2,1)S(1)}, u32[]{:S(2)}, u32[]{:S(2)}) collective-permute-start(bf16[256,128]{1,0:T(8,128)(2,1)S(1)} %get-tuple-element.69), channel_id=1, source_target_pairs={{8,20},{12,8},{16,12},{20,16},{24,36},{28,24},{32,28},{36,32},{40,... | collective-permute-start | bytes 196616 | tf_op jit(solution)/shard_map/ppermute | solution.py:360
  130.8 7.9 %collective-permute-done.17.q2 = bf16[256,128]{1,0:T(8,128)(2,1)S(1)} collective-permute-done((bf16[256,128]{1,0:T(8,128)(2,1)S(1)}, bf16[256,128]{1,0:T(8,128)(2,1)S(1)}, u32[]{:S(2)}, u32[]{:S(2)}) %collective-permute-start.17) | collective-permute-done | bytes 65568 | tf_op jit(solution)/shard_map/ppermute | solution.py:360
  138.7 1.9 %finish.1 = (bf16[256,512]{1,0:T(8,128)(2,1)}, bf16[256,512]{1,0:T(8,128)(2,1)}, bf16[256,512]{1,0:T(8,128)(2,1)}) custom-call(s32[5]{0:T(128)S(1)} %stack.19.meta, bf16[256,128]{1,0:T(8,128)(2,1)S(1)} %get-tuple-element.66.q0, bf16[256,128]{1,0:T(8,128)(2,1)S(1)} %collective-permute-done.16.q1, bf16[256,128]{1,0:T(8,128)(2,1)S(1)} %collective-permute-done.17.q2, ...), custom_call_target="tpu_custom_call" | custom-call | tf_op jit(solution)/shard_map/finish/pallas_call | solution.py:67
  (43 shorter events, 12.1 us)
Async XLA Ops:
  0.6 14.7 %copy-start = (s32[4,3]{1,0:T(4,128)S(1)}, s32[4,3]{1,0:T(4,128)}, u32[]{:S(2)}) copy-start(s32[4,3]{1,0:T(4,128)} %param.11) | copy-start | bytes 148
  0.6 13.1 %collective-permute-start.11 = (bf16[256,1024]{1,0:T(8,128)(2,1)}, bf16[256,1024]{1,0:T(8,128)(2,1)S(1)}, u32[]{:S(2)}, u32[]{:S(2)}) collective-permute-start(bf16[256,1024]{1,0:T(8,128)(2,1)} %g0.1), channel_id=1, source_target_pairs={{0,2},{1,3},{2,0},{3,1},{4,6},{5,7},{6,4},{7,5},{8,10},{9,11},{10,... | collective-permute-start | bytes 1572872 | tf_op jit(solution)/shard_map/ppermute | solution.py:369
  2.0 55.6 %collective-permute-start.10 = (bf16[256,1024]{1,0:T(8,128)(2,1)}, bf16[256,1024]{1,0:T(8,128)(2,1)S(1)}, u32[]{:S(2)}, u32[]{:S(2)}) collective-permute-start(bf16[256,1024]{1,0:T(8,128)(2,1)} %g0.1), channel_id=1, source_target_pairs={{0,1},{1,0},{2,3},{3,2},{4,5},{5,4},{6,7},{7,6},{8,9},{9,8},{10,11... | collective-permute-start | bytes 1572872 | tf_op jit(solution)/shard_map/ppermute | solution.py:369
  13.7 44.0 %collective-permute-start.12 = (bf16[256,1024]{1,0:T(8,128)(2,1)S(1)}, bf16[256,1024]{1,0:T(8,128)(2,1)S(1)}, u32[]{:S(2)}, u32[]{:S(2)}) collective-permute-start(bf16[256,1024]{1,0:T(8,128)(2,1)S(1)} %collective-permute-done.11.g2), channel_id=1, source_target_pairs={{0,1},{1,0},{2,3},{3,2},{4,5},{5,4},{6,7},{7,6},{8,9},{9,8},{10,11... | collective-permute-start | bytes 1572872 | tf_op jit(solution)/shard_map/ppermute | solution.py:369
  17.9 1.0 copy-start.3
  18.9 0.9 copy-start.4
  19.8 0.9 copy-start.5
  21.9 13.4 %collective-permute-start.3 = (bf16[512,128]{1,0:T(8,128)(2,1)S(1)}, bf16[512,128]{1,0:T(8,128)(2,1)S(1)}, u32[]{:S(2)}, u32[]{:S(2)}) collective-permute-start(bf16[512,128]{1,0:T(8,128)(2,1)S(1)} %get-tuple-element.46), channel_id=1, source_target_pairs={{8,12},{12,16},{16,20},{20,8},{24,28},{28,32},{32,36},{36,24},{40,... | collective-permute-start | bytes 393224 | tf_op jit(solution)/shard_map/ppermute | solution.py:360
  32.4 14.2 %collective-permute-start.4 = (bf16[512,128]{1,0:T(8,128)(2,1)S(1)}, bf16[512,128]{1,0:T(8,128)(2,1)S(1)}, u32[]{:S(2)}, u32[]{:S(2)}) collective-permute-start(bf16[512,128]{1,0:T(8,128)(2,1)S(1)} %get-tuple-element.47), channel_id=1, source_target_pairs={{8,16},{12,20},{16,8},{20,12},{24,32},{28,36},{32,24},{36,28},{40,... | collective-permute-start | bytes 393224 | tf_op jit(solution)/shard_map/ppermute | solution.py:360
  32.4 15.3 %collective-permute-start.5 = (bf16[512,128]{1,0:T(8,128)(2,1)S(1)}, bf16[512,128]{1,0:T(8,128)(2,1)S(1)}, u32[]{:S(2)}, u32[]{:S(2)}) collective-permute-start(bf16[512,128]{1,0:T(8,128)(2,1)S(1)} %get-tuple-element.48), channel_id=1, source_target_pairs={{8,20},{12,8},{16,12},{20,16},{24,36},{28,24},{32,28},{36,32},{40,... | collective-permute-start | bytes 393224 | tf_op jit(solution)/shard_map/ppermute | solution.py:360
  35.3 14.2 %collective-permute-start = (bf16[256,128]{1,0:T(8,128)(2,1)S(1)}, bf16[256,128]{1,0:T(8,128)(2,1)S(1)}, u32[]{:S(2)}, u32[]{:S(2)}) collective-permute-start(bf16[256,128]{1,0:T(8,128)(2,1)S(1)} %get-tuple-element.42), channel_id=1, source_target_pairs={{8,12},{12,16},{16,20},{20,8},{24,28},{28,32},{32,36},{36,24},{40,... | collective-permute-start | bytes 196616 | tf_op jit(solution)/shard_map/ppermute | solution.py:360
  46.6 9.7 %collective-permute-start.1 = (bf16[256,128]{1,0:T(8,128)(2,1)S(1)}, bf16[256,128]{1,0:T(8,128)(2,1)S(1)}, u32[]{:S(2)}, u32[]{:S(2)}) collective-permute-start(bf16[256,128]{1,0:T(8,128)(2,1)S(1)} %get-tuple-element.43), channel_id=1, source_target_pairs={{8,16},{12,20},{16,8},{20,12},{24,32},{28,36},{32,24},{36,28},{40,... | collective-permute-start | bytes 196616 | tf_op jit(solution)/shard_map/ppermute | solution.py:360
  48.3 31.8 %collective-permute-start.6 = (bf16[1024,128]{1,0:T(8,128)(2,1)S(1)}, bf16[1024,128]{1,0:T(8,128)(2,1)S(1)}, u32[]{:S(2)}, u32[]{:S(2)}) collective-permute-start(bf16[1024,128]{1,0:T(8,128)(2,1)S(1)} %get-tuple-element.50.kv1), channel_id=1, source_target_pairs={{8,24},{12,28},{16,32},{20,36},{40,56},{44,60},{48,64},{52,68},{72... | collective-permute-start | bytes 786440 | tf_op jit(solution)/shard_map/ppermute | solution.py:366
  49.6 23.8 %collective-permute-start.9 = (bf16[512,128]{1,0:T(8,128)(2,1)S(1)}, bf16[512,128]{1,0:T(8,128)(2,1)S(1)}, u32[]{:S(2)}, u32[]{:S(2)}) collective-permute-start(bf16[512,128]{1,0:T(8,128)(2,1)S(1)} %get-tuple-element.51.kv2), channel_id=1, source_target_pairs={{8,56},{12,60},{16,64},{20,68},{72,120},{76,124},{80,128},{84,132}... | collective-permute-start | bytes 393224 | tf_op jit(solution)/shard_map/ppermute | solution.py:366
  56.3 20.4 %collective-permute-start.8 = (bf16[512,128]{1,0:T(8,128)(2,1)S(1)}, bf16[512,128]{1,0:T(8,128)(2,1)S(1)}, u32[]{:S(2)}, u32[]{:S(2)}) collective-permute-start(bf16[512,128]{1,0:T(8,128)(2,1)S(1)} %get-tuple-element.51.kv2), channel_id=1, source_target_pairs={{8,40},{12,44},{16,48},{20,52},{24,56},{28,60},{32,64},{36,68},{72... | collective-permute-start | bytes 393224 | tf_op jit(solution)/shard_map/ppermute | solution.py:366
  57.6 12.3 %collective-permute-start.2 = (bf16[256,128]{1,0:T(8,128)(2,1)S(1)}, bf16[256,128]{1,0:T(8,128)(2,1)S(1)}, u32[]{:S(2)}, u32[]{:S(2)}) collective-permute-start(bf16[256,128]{1,0:T(8,128)(2,1)S(1)} %get-tuple-element.44), channel_id=1, source_target_pairs={{8,20},{12,8},{16,12},{20,16},{24,36},{28,24},{32,28},{36,32},{40,... | collective-permute-start | bytes 196616 | tf_op jit(solution)/shard_map/ppermute | solution.py:360
  57.7 22.4 %collective-permute-start.7 = (bf16[512,128]{1,0:T(8,128)(2,1)S(1)}, bf16[512,128]{1,0:T(8,128)(2,1)S(1)}, u32[]{:S(2)}, u32[]{:S(2)}) collective-permute-start(bf16[512,128]{1,0:T(8,128)(2,1)S(1)} %get-tuple-element.51.kv2), channel_id=1, source_target_pairs={{8,24},{12,28},{16,32},{20,36},{24,40},{28,44},{32,48},{36,52},{40... | collective-permute-start | bytes 393224 | tf_op jit(solution)/shard_map/ppermute | solution.py:366
  59.0 2.2 %copy-start.1 = (bf16[512,4096]{1,0:T(8,128)(2,1)S(1)}, bf16[512,4096]{1,0:T(8,128)(2,1)}, u32[]{:S(2)}) copy-start(bf16[512,4096]{1,0:T(8,128)(2,1)} %w.1) | copy-start | bytes 12582916
  61.2 1.0 copy-start.2
  69.9 10.2 %collective-permute-start.13 = (bf16[256,128]{1,0:T(8,128)(2,1)S(1)}, bf16[256,128]{1,0:T(8,128)(2,1)S(1)}, u32[]{:S(2)}, u32[]{:S(2)}) collective-permute-start(bf16[256,128]{1,0:T(8,128)(2,1)S(1)} %get-tuple-element.59), channel_id=1, source_target_pairs={{8,12},{12,16},{16,20},{20,8},{24,28},{28,32},{32,36},{36,24},{40,... | collective-permute-start | bytes 196616 | tf_op jit(solution)/shard_map/ppermute | solution.py:360
  73.4 9.9 %collective-permute-start.14 = (bf16[256,128]{1,0:T(8,128)(2,1)S(1)}, bf16[256,128]{1,0:T(8,128)(2,1)S(1)}, u32[]{:S(2)}, u32[]{:S(2)}) collective-permute-start(bf16[256,128]{1,0:T(8,128)(2,1)S(1)} %get-tuple-element.60), channel_id=1, source_target_pairs={{8,16},{12,20},{16,8},{20,12},{24,32},{28,36},{32,24},{36,28},{40,... | collective-permute-start | bytes 196616 | tf_op jit(solution)/shard_map/ppermute | solution.py:360
  76.7 10.9 %collective-permute-start.15 = (bf16[256,128]{1,0:T(8,128)(2,1)S(1)}, bf16[256,128]{1,0:T(8,128)(2,1)S(1)}, u32[]{:S(2)}, u32[]{:S(2)}) collective-permute-start(bf16[256,128]{1,0:T(8,128)(2,1)S(1)} %get-tuple-element.61), channel_id=1, source_target_pairs={{8,20},{12,8},{16,12},{20,16},{24,36},{28,24},{32,28},{36,32},{40,... | collective-permute-start | bytes 196616 | tf_op jit(solution)/shard_map/ppermute | solution.py:360
  93.2 11.3 %collective-permute-start.19 = (bf16[1024,128]{1,0:T(8,128)(2,1)S(1)}, bf16[1024,128]{1,0:T(8,128)(2,1)S(1)}, u32[]{:S(2)}, u32[]{:S(2)}) collective-permute-start(bf16[1024,128]{1,0:T(8,128)(2,1)S(1)} %get-tuple-element.71), channel_id=1, source_target_pairs={{24,8},{28,12},{32,16},{36,20},{56,40},{60,44},{64,48},{68,52},{88... | collective-permute-start | bytes 786440 | tf_op jit(solution)/shard_map/ppermute | solution.py:366
  94.5 10.0 %collective-permute-start.20 = (bf16[512,128]{1,0:T(8,128)(2,1)S(1)}, bf16[512,128]{1,0:T(8,128)(2,1)S(1)}, u32[]{:S(2)}, u32[]{:S(2)}) collective-permute-start(bf16[512,128]{1,0:T(8,128)(2,1)S(1)} %get-tuple-element.72), channel_id=1, source_target_pairs={{24,8},{28,12},{32,16},{36,20},{40,24},{44,28},{48,32},{52,36},{56... | collective-permute-start | bytes 393224 | tf_op jit(solution)/shard_map/ppermute | solution.py:366
  95.8 8.7 %collective-permute-start.21 = (bf16[512,128]{1,0:T(8,128)(2,1)S(1)}, bf16[512,128]{1,0:T(8,128)(2,1)S(1)}, u32[]{:S(2)}, u32[]{:S(2)}) collective-permute-start(bf16[512,128]{1,0:T(8,128)(2,1)S(1)} %get-tuple-element.73), channel_id=1, source_target_pairs={{40,8},{44,12},{48,16},{52,20},{56,24},{60,28},{64,32},{68,36},{10... | collective-permute-start | bytes 393224 | tf_op jit(solution)/shard_map/ppermute | solution.py:366
  97.1 7.4 %collective-permute-start.22 = (bf16[512,128]{1,0:T(8,128)(2,1)S(1)}, bf16[512,128]{1,0:T(8,128)(2,1)S(1)}, u32[]{:S(2)}, u32[]{:S(2)}) collective-permute-start(bf16[512,128]{1,0:T(8,128)(2,1)S(1)} %get-tuple-element.74), channel_id=1, source_target_pairs={{56,8},{60,12},{64,16},{68,20},{120,72},{124,76},{128,80},{132,84}... | collective-permute-start | bytes 393224 | tf_op jit(solution)/shard_map/ppermute | solution.py:366
  102.9 20.0 %collective-permute-start.16 = (bf16[256,128]{1,0:T(8,128)(2,1)S(1)}, bf16[256,128]{1,0:T(8,128)(2,1)S(1)}, u32[]{:S(2)}, u32[]{:S(2)}) collective-permute-start(bf16[256,128]{1,0:T(8,128)(2,1)S(1)} %get-tuple-element.67), channel_id=1, source_target_pairs={{8,12},{12,16},{16,20},{20,8},{24,28},{28,32},{32,36},{36,24},{40,... | collective-permute-start | bytes 196616 | tf_op jit(solution)/shard_map/ppermute | solution.py:360
  105.3 33.4 %collective-permute-start.23 = (bf16[512,128]{1,0:T(8,128)(2,1)S(1)}, bf16[512,128]{1,0:T(8,128)(2,1)S(1)}, u32[]{:S(2)}, u32[]{:S(2)}) collective-permute-start(bf16[512,128]{1,0:T(8,128)(2,1)S(1)} %get-tuple-element.76), channel_id=1, source_target_pairs={{8,12},{12,16},{16,20},{20,8},{24,28},{28,32},{32,36},{36,24},{40,... | collective-permute-start | bytes 393224 | tf_op jit(solution)/shard_map/ppermute | solution.py:360
  109.2 29.5 %collective-permute-start.24 = (bf16[512,128]{1,0:T(8,128)(2,1)S(1)}, bf16[512,128]{1,0:T(8,128)(2,1)S(1)}, u32[]{:S(2)}, u32[]{:S(2)}) collective-permute-start(bf16[512,128]{1,0:T(8,128)(2,1)S(1)} %get-tuple-element.77), channel_id=1, source_target_pairs={{8,16},{12,20},{16,8},{20,12},{24,32},{28,36},{32,24},{36,28},{40,... | collective-permute-start | bytes 393224 | tf_op jit(solution)/shard_map/ppermute | solution.py:360
  121.6 17.2 %collective-permute-start.25 = (bf16[512,128]{1,0:T(8,128)(2,1)S(1)}, bf16[512,128]{1,0:T(8,128)(2,1)S(1)}, u32[]{:S(2)}, u32[]{:S(2)}) collective-permute-start(bf16[512,128]{1,0:T(8,128)(2,1)S(1)} %get-tuple-element.78), channel_id=1, source_target_pairs={{8,20},{12,8},{16,12},{20,16},{24,36},{28,24},{32,28},{36,32},{40,... | collective-permute-start | bytes 393224 | tf_op jit(solution)/shard_map/ppermute | solution.py:360
  122.9 15.8 %collective-permute-start.17 = (bf16[256,128]{1,0:T(8,128)(2,1)S(1)}, bf16[256,128]{1,0:T(8,128)(2,1)S(1)}, u32[]{:S(2)}, u32[]{:S(2)}) collective-permute-start(bf16[256,128]{1,0:T(8,128)(2,1)S(1)} %get-tuple-element.68), channel_id=1, source_target_pairs={{8,16},{12,20},{16,8},{20,12},{24,32},{28,36},{32,24},{36,28},{40,... | collective-permute-start | bytes 196616 | tf_op jit(solution)/shard_map/ppermute | solution.py:360
  122.9 15.8 %collective-permute-start.18 = (bf16[256,128]{1,0:T(8,128)(2,1)S(1)}, bf16[256,128]{1,0:T(8,128)(2,1)S(1)}, u32[]{:S(2)}, u32[]{:S(2)}) collective-permute-start(bf16[256,128]{1,0:T(8,128)(2,1)S(1)} %get-tuple-element.69), channel_id=1, source_target_pairs={{8,20},{12,8},{16,12},{20,16},{24,36},{28,24},{32,28},{36,32},{40,... | collective-permute-start | bytes 196616 | tf_op jit(solution)/shard_map/ppermute | solution.py:360

commit v2 on v1

--- a/solution.py
+++ b/solution.py
@@ -1,4 +1,3 @@
-import functools
 import math
 
 import jax
@@ -62,13 +61,25 @@
     return jnp.broadcast_to(jnp.max(scores, axis=1, keepdims=True), (scores.shape[0], DIM))
 
 
-def call(kernel, outs, scratch=(), name=None, flops=0, bytes_accessed=0):
-    def run(meta, *args):
+def call(kernel, outs, scratch=(), name=None, flops=0, bytes_accessed=0, far=()):
+    def run(*args):
+        args = [
+            pltpu.with_memory_space_constraint(arg, pltpu.HBM) if i in far else arg
+            for i, arg in enumerate(args)
+        ]
         return pl.pallas_call(
             kernel,
             out_shape=[jax.ShapeDtypeStruct(shape, dtype) for shape, dtype in outs],
-            in_specs=[pl.BlockSpec(memory_space=pltpu.SMEM)]
-            + [pl.BlockSpec(memory_space=pltpu.VMEM)] * len(args),
+            in_specs=[
+                pl.BlockSpec(
+                    memory_space=pltpu.SMEM
+                    if arg.dtype == jnp.int32
+                    else pltpu.HBM
+                    if i in far
+                    else pltpu.VMEM
+                )
+                for i, arg in enumerate(args)
+            ],
             out_specs=[pl.BlockSpec(memory_space=pltpu.VMEM)] * len(outs),
             scratch_shapes=list(scratch),
             compiler_params=pltpu.CompilerParams(vmem_limit_bytes=40 << 20),
@@ -76,44 +87,82 @@
                 flops=flops, bytes_accessed=bytes_accessed, transcendentals=0
             ),
             name=name,
-        )(meta, *args)
+        )(*args)
 
     return run
 
 
-def pack_kernel(meta, q, k, v, *outs):
-    kvs, qs = outs[:4], outs[4:]
+def seat():
+    devices = lax.axis_size("ctx")
+    return lax.rem(lax.axis_index("ctx") + (devices - 2), devices)
+
+
+def place_and_block():
+    return seat() & 3, (seat() >> 2) & 3
+
+
+def head_at(place, block):
+    return jnp.where((block & 1) == 1, 3 - place, place)
+
+
+def places(offsets):
+    place, block = place_and_block()
+    head = head_at(place, block)
+    off2 = offsets[head, 2]
+    return place, block, offsets[head, 1], ((off2 & 1) << 1) | (off2 >> 1)
+
+
+def pack_kernel(q, k, v, o0, o1, o2, o3, held, sem):
+    place, block = place_and_block()
+    copies = [pltpu.make_async_copy(src, held.at[i], sem.at[i]) for i, src in enumerate((k, v, q))]
+    for copy in copies:
+        copy.start()
     sort = sort_matrix()
-    for s in range(4):
-        head = (meta[0] + s) & 3
-        kvs[s][:TOK] = dot_nn(sort, k[:, cols_at(head)]).astype(BF16)
-        kvs[s][TOK:] = dot_nn(sort, v[:, cols_at(head)]).astype(BF16)
-        qs[s][...] = dot_nn(sort, q[:, cols_at(head)]).astype(BF16)
-
-
-def gather_kernel(meta, p0, p1, p2, p3, kv, kv1, kv2):
+    for i, copy in enumerate(copies):
+        copy.wait()
+        for s, target in enumerate((o0, o1, o2, o3)):
+            head = head_at((place + s) & 3, block)
+            rows = held.at[i]
+            target[i * TOK : (i + 1) * TOK] = dot_nn(sort, rows[:, cols_at(head)]).astype(BF16)
+
+
+def gather_kernel(offsets, p0, p1, p2, p3, qa, kv, both, kv2):
+    place, _, off1, group2 = places(offsets)
     for s, piece in enumerate((p0, p1, p2, p3)):
-        place = (meta[0] - s) & 3
+        source = (place - s) & 3
+        qa[rows_at(source * TOK, TOK)] = piece[2 * TOK :]
         for part in range(2):
             own = piece.at[part * TOK : (part + 1) * TOK]
-            kv[rows_at(part * BLOCK + place * TOK, TOK)] = own[...]
-            kv1[rows_at(part * 512 + place * 128, 128)] = own[rows_at(meta[2] * 128, 128)]
-            kv2[rows_at(part * 256 + place * 64, 64)] = own[rows_at(meta[3] * 64, 64)]
-
-
-def grad_kernel(meta, g0, g1, g2, g3, w, *outs):
-    tp = meta[4]
-    total = None
-    for m, part in enumerate((g0, g1, g2, g3)):
-        width = part.shape[1]
+            kv[rows_at(part * BLOCK + source * TOK, TOK)] = own[...]
+            both[rows_at(part * 512 + source * 128, 128)] = own[rows_at(off1 * 128, 128)]
+            rows2 = own[rows_at(group2 * 64, 64)]
+            both[rows_at(1024 + part * 256 + source * 64, 64)] = rows2
+            kv2[rows_at(part * 256 + source * 64, 64)] = rows2
+
+
+def grad_near_kernel(g0, g1, w, out, w_far, held, sem):
+    tp = lax.axis_index("tp")
+    width = g0.shape[1]
+    slots = (held.at[0], held.at[1], w_far.at[0], w_far.at[1])
+    copies = []
+    for m, slot in enumerate(slots):
         cols = pl.ds(pl.multiple_of((tp ^ m) * width, width), width)
-        term = dot_nt(part[...], w[:, cols])
-        total = term if total is None else total + term
-    sort = sort_matrix()
-    sorted_grad = outs[4]
-    sorted_grad[...] = dot_nn(sort, total.astype(BF16)).astype(BF16)
-    for s in range(4):
-        outs[s][...] = sorted_grad[:, cols_at((meta[0] + s) & 3)]
+        copies.append(pltpu.make_async_copy(w.at[:, cols], slot, sem.at[m]))
+        copies[m].start()
+    copies[0].wait()
+    out[...] = dot_nt(g0[...], held[0])
+    copies[1].wait()
+    out[...] += dot_nt(g1[...], held[1])
+    copies[2].wait()
+    copies[3].wait()
+
+
+def grad_far_kernel(near, g2, g3, w, o0, o1, o2, o3, sorted_grad):
+    place, block = place_and_block()
+    total = near[...] + dot_nt(g2[...], w[0]) + dot_nt(g3[...], w[1])
+    sorted_grad[...] = dot_nn(sort_matrix(), total.astype(BF16)).astype(BF16)
+    for s, target in enumerate((o0, o1, o2, o3)):
+        target[...] = sorted_grad[:, cols_at(head_at((place + s) & 3, block))]
 
 
 def ones_beside(target, values):
@@ -122,11 +171,10 @@
 
 
 def own_forward_kernel(
-    meta, q0, q1, q2, q3, kv, kv1, kv2, qa, e0, e1, e2, top, out, vx0, vx1, vx2
+    offsets, qa, kv, both, e0, e1, e2, top, out, vx0, vx1, vx2
 ):
-    off1, group2 = meta[2], meta[3]
-    for s, piece in enumerate((q0, q1, q2, q3)):
-        qa[rows_at(((meta[0] - s) & 3) * TOK, TOK)] = piece[...]
+    _, _, off1, group2 = places(offsets)
+    kv1, kv2 = both.at[:1024], both.at[1024:]
     ones_beside(vx0, kv[BLOCK:])
     ones_beside(vx1, kv1[512:])
     ones_beside(vx2, kv2[256:])
@@ -176,15 +224,20 @@
 
 
 def cross_kernel(
-    meta, qa, x1, x21, x22, x23, top, out, p0, p1, p2, p3,
-    doa, dq, factor, delta, g1, g21, g22, g23,
+    offsets, qa, xa, xb, xc, top, out, p0, p1, p2, p3,
+    doa, dq, factor, delta, ga, gb, gc,
     pq1, pq2, pd1, pd2, sc1, sc2, e1, e2, newtop, newout, inv, vx1, vx2,
 ):
-    block, off1, group2 = meta[1], meta[2], meta[3]
-    second = (block & 1) == 1
-    earlier = ((x21, g21), (x22, g22), (x23, g23))
+    place, block, off1, group2 = places(offsets)
+    second, later = (block & 1) == 1, block >= 2
+    x1, g1 = xa.at[:1024], ga.at[:1024]
+    earlier = (
+        (second, xa.at[1024:], ga.at[1024:]),
+        (later, xb, gb),
+        (later, xc, gc),
+    )
     for s, piece in enumerate((p0, p1, p2, p3)):
-        doa[rows_at(((meta[0] - s) & 3) * TOK, TOK)] = piece[...]
+        doa[rows_at(((place - s) & 3) * TOK, TOK)] = piece[...]
     where1 = [rows_at(b * 256 + off1 * 128, 128) for b in range(4)]
     where2 = [rows_at(b * 256 + group2 * 64, 64) for b in range(4)]
     for b in range(4):
@@ -200,9 +253,9 @@
             high = wide_max(sc1[b * 128 : (b + 1) * 128])
             newtop[where1[b]] = jnp.maximum(newtop[where1[b]], high)
 
-    for d, (x2, _) in enumerate(earlier):
-
-        @pl.when(block > d)
+    for d, (valid, x2, _) in enumerate(earlier):
+
+        @pl.when(valid)
         def _(d=d, x2=x2):
             ones_beside(vx2.at[d], x2[256:])
             sc2[d] = dot_nt(pq2[...], x2[:256]) * SCALE2
@@ -222,9 +275,9 @@
             e1[part] = w
             newout[where1[b]] += dot_nn(w, vx1[...])
 
-    for d in range(3):
-
-        @pl.when(block > d)
+    for d, (valid, _, _) in enumerate(earlier):
+
+        @pl.when(valid)
         def _(d=d):
             for b in range(4):
                 part = slice(b * 64, (b + 1) * 64)
@@ -253,9 +306,9 @@
         g1[:512] = (dot_tn(score_grad, pq1[...]) * SCALE).astype(BF16)
         g1[512:] = dot_tn(e1[...], pd1[...]).astype(BF16)
 
-    for d, (x2, g2) in enumerate(earlier):
-
-        @pl.when(block > d)
+    for d, (valid, x2, g2) in enumerate(earlier):
+
+        @pl.when(valid)
         def _(d=d, x2=x2, g2=g2):
             prob = dot_nt(pd2[...], x2[256:])
             level = jnp.concatenate([(delta[r] * inv[r])[:, :1] for r in where2], axis=0)
@@ -268,10 +321,11 @@
 
 
 def own_backward_kernel(
-    meta, e0, e1, e2, factor, delta, doa, qa, kv, kv1, kv2, dq_in,
+    offsets, e0, e1, e2, factor, delta, doa, qa, kv, both, dq_in,
     o0, o1, o2, o3, dkv, dq, low, shift, dkv1, dkv2, low_q,
 ):
-    off1, group2 = meta[2], meta[3]
+    place, _, off1, group2 = places(offsets)
+    kv1, kv2 = both.at[:1024], both.at[1024:]
     low[...] = (doa[...].astype(F32) * factor[...]).astype(BF16)
     shift[...] = factor[...] * delta[...]
     dq[...] = dq_in[...]
@@ -312,11 +366,12 @@
     dkv[:BLOCK] = dkv[:BLOCK] * SCALE
     low_q[...] = (dq[...] * SCALE).astype(BF16)
     for s, target in enumerate((o0, o1, o2, o3)):
-        target[...] = low_q[rows_at(((meta[0] + s) & 3) * TOK, TOK)]
-
-
-def combine_kernel(meta, dkv, y1, y21, y22, y23, o0, o1, o2, o3, total):
-    off1, group2 = meta[2], meta[3]
+        target[...] = low_q[rows_at(((place + s) & 3) * TOK, TOK)]
+
+
+def combine_kernel(offsets, dkv, last_q, ya, yb, yc, o0, o1, o2, o3, total):
+    home, _, off1, group2 = places(offsets)
+    y1, y2 = ya.at[:1024], ya.at[1024:]
     total[...] = dkv[...]
     for p in range(4):
         for part in range(2):
@@ -324,81 +379,115 @@
             two = slice(part * 256 + p * 64, part * 256 + (p + 1) * 64)
             total[rows_at(part * BLOCK + p * 256 + off1 * 128, 128)] += y1[one].astype(F32)
             total[rows_at(part * BLOCK + p * 256 + group2 * 64, 64)] += (
-                y21[two].astype(F32) + y22[two].astype(F32) + y23[two].astype(F32)
+                y2[two].astype(F32) + yb[two].astype(F32) + yc[two].astype(F32)
             )
     for s, target in enumerate((o0, o1, o2, o3)):
-        place = (meta[0] + s) & 3
+        place = (home + s) & 3
         for part in range(2):
             target[part * TOK : (part + 1) * TOK] = total[
                 rows_at(part * BLOCK + place * TOK, TOK)
             ].astype(BF16)
-
-
-def finish_kernel(meta, q0, q1, q2, q3, r0, r1, r2, r3, dq, dk, dv):
+    o3[2 * TOK :] = last_q[...]
+
+
+def unsort_pieces(pieces, outs):
+    place, block = place_and_block()
     unsort = unsort_matrix()
-    for s, (query, pair) in enumerate(((q0, r0), (q1, r1), (q2, r2), (q3, r3))):
-        cols = cols_at((meta[0] - s) & 3)
-        dq[:, cols] = dot_nn(unsort, query[...]).astype(BF16)
-        dk[:, cols] = dot_nn(unsort, pair[:TOK]).astype(BF16)
-        dv[:, cols] = dot_nn(unsort, pair[TOK:]).astype(BF16)
+    for s, piece in enumerate(pieces):
+        cols = cols_at(head_at((place - s) & 3, block))
+        for i, out in enumerate(outs):
+            out[:, cols] = dot_nn(unsort, piece[i * TOK : (i + 1) * TOK]).astype(BF16)
+
+
+def finish_query_kernel(p0, p1, p2, dq):
+    unsort_pieces((p0, p1, p2), (dq,))
+
+
+def finish_kernel(dq_in, p0, p1, p2, p3, dq, dk, dv):
+    dq[...] = dq_in[...]
+    unsort_pieces((p0, p1, p2, p3), (dk, dv))
+    place, block = place_and_block()
+    last = dot_nn(unsort_matrix(), p3[2 * TOK :]).astype(BF16)
+    dq[:, cols_at(head_at((place - 3) & 3, block))] = last
 
 
 def local(queries, keys, values, out_grad, w_out, offsets):
     devices = lax.axis_size("ctx")
-    seat = (lax.axis_index("ctx") - 2) % devices
-    place, block, tp = seat % 4, seat // 4 % 4, lax.axis_index("tp")
-    own = lax.dynamic_slice_in_dim(offsets, place, 1, 0)[0]
-    meta = jnp.stack([place, block, own[1], ((own[2] & 1) << 1) | (own[2] >> 1), tp])
 
     def at(index):
         return (index + 2) % devices
 
     def exchange(part, s):
-        route = [
-            (at(u), at(u // 4 * 4 + (u % 4 + s) % 4)) for u in range(devices)
-        ]
+        route = [(at(u), at(u // 4 * 4 + (u % 4 + s) % 4)) for u in range(devices)]
         return lax.ppermute(part, "ctx", route)
 
-    def to_block(part, distance, blocks):
-        route = [
-            (at(u), at(u + 4 * distance)) for u in range(devices) if u // 4 % 4 in blocks
-        ]
+    def to_blocks(part, pairs, back=False):
+        route = []
+        for first in range(0, devices, 16):
+            for source, target in pairs:
+                for place in range(4):
+                    there = 3 - place if (source + target) % 2 else place
+                    pair = (at(first + 4 * source + place), at(first + 4 * target + there))
+                    route.append(pair[::-1] if back else pair)
         return lax.ppermute(part, "ctx", route)
 
     def across(part, m):
         return lax.ppermute(part, "tp", [(i, i ^ m) for i in range(4)])
 
+    def after(part, *others):
+        return lax.optimization_barrier((part, *others))[0]
+
+    links = (((0, 1), (2, 3)), ((1, 2), (0, 3)), ((0, 2), (1, 3)))
+    width = out_grad.shape[1]
+    half = (2, 4 * DIM, width)
+
+    grad_y = across(out_grad, 2)
     packed = call(
-        pack_kernel, [((2 * TOK, DIM), BF16)] * 4 + [((TOK, DIM), BF16)] * 4, name="pack"
-    )(meta, queries, keys, values)
-    pairs = [packed[0]] + [exchange(packed[s], s) for s in (1, 2, 3)]
-    grad_y = across(out_grad, 2)
-    query_parts = [packed[4]] + [exchange(packed[4 + s], s) for s in (1, 2, 3)]
-    grad_core = across(out_grad, 1)
-    grad_far = across(grad_y, 1)
-
-    kv, kv1, kv2 = call(
-        gather_kernel,
-        [((2 * BLOCK, DIM), BF16), ((1024, DIM), BF16), ((512, DIM), BF16)],
-        name="gather",
-    )(meta, *pairs)
-    x1 = to_block(kv1, 1, (0, 2))
-    x2 = [to_block(kv2, d, range(4 - d)) for d in (1, 2, 3)]
-
+        pack_kernel,
+        [((3 * TOK, DIM), BF16)] * 4,
+        [pltpu.VMEM((3, TOK, 4 * DIM), BF16), pltpu.SemaphoreType.DMA((3,))],
+        name="pack",
+        flops=2 * 10**8,
+        bytes_accessed=2 << 20,
+        far=(0, 1, 2),
+    )(queries, keys, values)
+    pieces = [exchange(packed[s], s) for s in (1, 2, 3)]
+    grad_core = across(after(out_grad, packed[1]), 1)
+    near, w_far = call(
+        grad_near_kernel,
+        [((TOK, 4 * DIM), F32), (half, BF16)],
+        [pltpu.VMEM(half, BF16), pltpu.SemaphoreType.DMA((4,))],
+        name="grad_near",
+        far=(2,),
+    )(out_grad, grad_core, w_out)
+    grad_far = across(after(grad_y, near, *pieces), 1)
     grads = call(
-        grad_kernel,
+        grad_far_kernel,
         [((TOK, DIM), BF16)] * 4,
         [pltpu.VMEM((TOK, 4 * DIM), BF16)],
-        name="grad",
-        flops=2 * TOK * 512 * 4096,
-        bytes_accessed=6 << 20,
-    )(meta, out_grad, grad_core, grad_y, grad_far, w_out)
-    grad_parts = [grads[0]] + [exchange(grads[s], s) for s in (1, 2, 3)]
-
-    qa, e0, e1, e2, top, out = call(
+        name="grad_far",
+        flops=TOK * 512 * 4096,
+        bytes_accessed=4 << 20,
+    )(near, grad_y, grad_far, w_far)
+
+    qa, kv, both, kv2 = call(
+        gather_kernel,
+        [
+            ((BLOCK, DIM), BF16),
+            ((2 * BLOCK, DIM), BF16),
+            ((1536, DIM), BF16),
+            ((512, DIM), BF16),
+        ],
+        name="gather",
+        flops=10**7,
+        bytes_accessed=2 << 20,
+    )(offsets, packed[0], after(pieces[0], near), *pieces[1:])
+    xs = [to_blocks(part, pairs) for part, pairs in zip((both, kv2, kv2), links)]
+    grad_parts = [grads[0]] + [exchange(after(grads[s], kv2), s) for s in (1, 2, 3)]
+
+    e0, e1, e2, top, out = call(
         own_forward_kernel,
         [
-            ((BLOCK, DIM), BF16),
             ((BLOCK, BLOCK), BF16),
             ((512, 512), BF16),
             ((256, 256), BF16),
@@ -413,17 +502,16 @@
         name="own_forward",
         flops=10**9,
         bytes_accessed=6 << 20,
-    )(meta, *query_parts, kv, kv1, kv2)
-
-    doa, dq, factor, delta, g1, g21, g22, g23 = call(
+    )(offsets, qa, kv, both)
+
+    doa, dq, factor, delta, *partials = call(
         cross_kernel,
         [
             ((BLOCK, DIM), BF16),
             ((BLOCK, DIM), F32),
             ((BLOCK, DIM), F32),
             ((BLOCK, DIM), F32),
-            ((1024, DIM), BF16),
-            ((512, DIM), BF16),
+            ((1536, DIM), BF16),
             ((512, DIM), BF16),
             ((512, DIM), BF16),
         ],
@@ -445,9 +533,8 @@
         name="cross",
         flops=10**9,
         bytes_accessed=6 << 20,
-    )(meta, qa, x1, *x2, top, out, *grad_parts)
-    y1 = to_block(g1, -1, (1, 3))
-    y2 = [to_block(g, -d, range(d, 4)) for d, g in ((1, g21), (2, g22), (3, g23))]
+    )(offsets, qa, *xs, top, out, *grad_parts)
+    ys = [to_blocks(part, pairs, back=True) for part, pairs in zip(partials, links)]
 
     *dq_parts, dkv = call(
         own_backward_kernel,
@@ -463,18 +550,24 @@
         name="own_backward",
         flops=2 * 10**9,
         bytes_accessed=8 << 20,
-    )(meta, e0, e1, e2, factor, delta, doa, qa, kv, kv1, kv2, dq)
-    dq_parts = [dq_parts[0]] + [exchange(dq_parts[s], s) for s in (1, 2, 3)]
+    )(offsets, e0, e1, e2, factor, delta, doa, qa, kv, both, dq)
+    near_parts = [dq_parts[0]] + [exchange(dq_parts[s], s) for s in (1, 2)]
 
     pairs = call(
         combine_kernel,
-        [((2 * TOK, DIM), BF16)] * 4,
+        [((2 * TOK, DIM), BF16)] * 3 + [((3 * TOK, DIM), BF16)],
         [pltpu.VMEM((2 * BLOCK, DIM), F32)],
         name="combine",
-    )(meta, dkv, y1, *y2)
+        flops=10**7,
+        bytes_accessed=4 << 20,
+    )(offsets, after(dkv, *near_parts), dq_parts[3], *ys)
+    query_grad = call(finish_query_kernel, [((TOK, 4 * DIM), BF16)], name="finish_query")(
+        near_parts[0], after(near_parts[1], pairs[0]), near_parts[2]
+    )[0]
     pairs = [pairs[0]] + [exchange(pairs[s], s) for s in (1, 2, 3)]
+    pairs[1] = after(pairs[1], query_grad)
     return tuple(
-        call(finish_kernel, [((TOK, 4 * DIM), BF16)] * 3, name="finish")(meta, *dq_parts, *pairs)
+        call(finish_kernel, [((TOK, 4 * DIM), BF16)] * 3, name="finish")(query_grad, *pairs)
     )
 
 

time: 141 us -> 117 us (0.83)
  the two profiles are of different devices: /device:TPU:33 before, /device:TPU:32 now
where the time goes in v2:
time: 117 us; the launch traced here: 116 us
  starting transfers between devices  67.4 us (58%)
  waiting for transfers between devices  26.5 us (23%)
  Pallas kernels  20.6 us (18%)
    ppermute x11, starting transfers between devices, exchange(): return lax.ppermute(part, 'ctx', route)  56.2 us
    ppermute x11, waiting for transfers between devices, exchange(): return lax.ppermute(part, 'ctx', route)  21.6 us
    pallas_call x10, Pallas kernels, run(): pl.pallas_call(kernel, out_shape=[jax.ShapeDtypeStruct(shape, dtype) for...  20.6 us
    ppermute x6, starting transfers between devices, to_blocks(): return lax.ppermute(part, 'ctx', route)  9.46 us
    ppermute x6, waiting for transfers between devices, to_blocks(): return lax.ppermute(part, 'ctx', route)  4.9 us
  transfers between devices with their start and end apart: 20, of which 6 were waited for; matrix products, arithmetic and copies ran while one was open for 0% of the time, Pallas kernels for 10%

profile of v2, /device:TPU:32, one launch (start us, length us, event | category | flops | bytes accessed | tf_op | source)
XLA Modules:
  0.0 116.4 jit_solution(666890138351198327)
XLA Ops:
  0.6 1.9 %pack.1 = (bf16[768,128]{1,0:T(8,128)(2,1)S(1)}, bf16[768,128]{1,0:T(8,128)(2,1)S(1)}, bf16[768,128]{1,0:T(8,128)(2,1)S(1)}, bf16[768,128]{1,0:T(8,128)(2,1)S(1)}) custom-call(bf16[256,512]{1,0:T(8,128)(2,1)} %q.1, bf16[256,512]{1,0:T(8,128)(2,1)} %k.1, bf16[256,512]{1,0:T(8,128)(2,1)} %v.1), custom_call_target="tpu_custom_call" | custom-call | flops 200000000 | bytes 2097152 | tf_op jit(solution)/shard_map/pack/pallas_call | solution.py:70
  2.6 1.7 %collective-permute-start.7 = (bf16[256,1024]{1,0:T(8,128)(2,1)}, bf16[256,1024]{1,0:T(8,128)(2,1)S(1)}, u32[]{:S(2)}, u32[]{:S(2)}) collective-permute-start(bf16[256,1024]{1,0:T(8,128)(2,1)} %g0.1), channel_id=1, source_target_pairs={{0,2},{1,3},{2,0},{3,1},{4,6},{5,7},{6,4},{7,5},{8,10},{9,11},{10,... | collective-permute-start | bytes 1572872 | tf_op jit(solution)/shard_map/ppermute | solution.py:435
  4.2 9.9 %collective-permute-start.2 = (bf16[768,128]{1,0:T(8,128)(2,1)S(1)}, bf16[768,128]{1,0:T(8,128)(2,1)S(1)}, u32[]{:S(2)}, u32[]{:S(2)}) collective-permute-start(bf16[768,128]{1,0:T(8,128)(2,1)S(1)} %get-tuple-element.52), channel_id=1, source_target_pairs={{8,16},{12,20},{16,8},{20,12},{24,32},{28,36},{32,24},{36,28},{40,... | collective-permute-start | bytes 589832 | tf_op jit(solution)/shard_map/ppermute | solution.py:422
  14.2 1.0 collective-permute-start.3
  15.2 8.5 %collective-permute-start = (bf16[768,128]{1,0:T(8,128)(2,1)S(1)}, bf16[768,128]{1,0:T(8,128)(2,1)S(1)}, u32[]{:S(2)}, u32[]{:S(2)}) collective-permute-start(bf16[768,128]{1,0:T(8,128)(2,1)S(1)} %get-tuple-element.48), channel_id=1, source_target_pairs={{8,12},{12,16},{16,20},{20,8},{24,28},{28,32},{32,36},{36,24},{40,... | collective-permute-start | bytes 589832 | tf_op jit(solution)/shard_map/ppermute | solution.py:422
  23.7 1.0 copy-done
  24.8 2.2 %grad_near.1 = (f32[256,512]{1,0:T(8,128)S(1)}, bf16[2,512,1024]{2,1,0:T(8,128)(2,1)S(1)}) custom-call(bf16[256,1024]{1,0:T(8,128)(2,1)S(1)} %copy-done, bf16[256,1024]{1,0:T(8,128)(2,1)S(1)} %collective-permute-done.1.g1, bf16[512,4096]{1,0:T(8,128)(2,1)} %w.1), custom_call_target="tpu_custom_call" | custom-call | tf_op jit(solution)/shard_map/grad_near/pallas_call | solution.py:70
  27.0 2.5 %collective-permute-done.3.p3 = bf16[768,128]{1,0:T(8,128)(2,1)S(1)} collective-permute-done((bf16[768,128]{1,0:T(8,128)(2,1)S(1)}, bf16[768,128]{1,0:T(8,128)(2,1)S(1)}, u32[]{:S(2)}, u32[]{:S(2)}) %collective-permute-start.3) | collective-permute-done | bytes 196640 | tf_op jit(solution)/shard_map/ppermute | solution.py:422
  29.5 0.7 gather.1
  30.2 1.3 %collective-permute-start.4 = (bf16[1536,128]{1,0:T(8,128)(2,1)S(1)}, bf16[1536,128]{1,0:T(8,128)(2,1)S(1)}, u32[]{:S(2)}, u32[]{:S(2)}) collective-permute-start(bf16[1536,128]{1,0:T(8,128)(2,1)S(1)} %get-tuple-element.56.both), channel_id=1, source_target_pairs={{8,36},{12,32},{16,28},{20,24},{40,68},{44,64},{48,60},{52,56},{72... | collective-permute-start | bytes 1179656 | tf_op jit(solution)/shard_map/ppermute | solution.py:432
  31.5 1.3 %collective-permute-start.6 = (bf16[512,128]{1,0:T(8,128)(2,1)S(1)}, bf16[512,128]{1,0:T(8,128)(2,1)S(1)}, u32[]{:S(2)}, u32[]{:S(2)}) collective-permute-start(bf16[512,128]{1,0:T(8,128)(2,1)S(1)} %get-tuple-element.60), channel_id=1, source_target_pairs={{8,40},{12,44},{16,48},{20,52},{24,56},{28,60},{32,64},{36,68},{72... | collective-permute-start | bytes 393224 | tf_op jit(solution)/shard_map/ppermute | solution.py:432
  32.8 1.3 %collective-permute-start.5 = (bf16[512,128]{1,0:T(8,128)(2,1)S(1)}, bf16[512,128]{1,0:T(8,128)(2,1)S(1)}, u32[]{:S(2)}, u32[]{:S(2)}) collective-permute-start(bf16[512,128]{1,0:T(8,128)(2,1)S(1)} %get-tuple-element.60), channel_id=1, source_target_pairs={{24,52},{28,48},{32,44},{36,40},{8,68},{12,64},{16,60},{20,56},{88... | collective-permute-start | bytes 393224 | tf_op jit(solution)/shard_map/ppermute | solution.py:432
  34.1 1.0 grad_far.1
  35.1 3.2 %collective-permute-start.11 = (bf16[256,128]{1,0:T(8,128)(2,1)S(1)}, bf16[256,128]{1,0:T(8,128)(2,1)S(1)}, u32[]{:S(2)}, u32[]{:S(2)}) collective-permute-start(bf16[256,128]{1,0:T(8,128)(2,1)S(1)} %get-tuple-element.71), channel_id=1, source_target_pairs={{8,20},{12,8},{16,12},{20,16},{24,36},{28,24},{32,28},{36,32},{40,... | collective-permute-start | bytes 196616 | tf_op jit(solution)/shard_map/ppermute | solution.py:422
  38.3 7.4 %collective-permute-start.10 = (bf16[256,128]{1,0:T(8,128)(2,1)S(1)}, bf16[256,128]{1,0:T(8,128)(2,1)S(1)}, u32[]{:S(2)}, u32[]{:S(2)}) collective-permute-start(bf16[256,128]{1,0:T(8,128)(2,1)S(1)} %get-tuple-element.69), channel_id=1, source_target_pairs={{8,16},{12,20},{16,8},{20,12},{24,32},{28,36},{32,24},{36,28},{40,... | collective-permute-start | bytes 196616 | tf_op jit(solution)/shard_map/ppermute | solution.py:422
  45.8 1.4 %collective-permute-done.6.xc = bf16[512,128]{1,0:T(8,128)(2,1)S(1)} collective-permute-done((bf16[512,128]{1,0:T(8,128)(2,1)S(1)}, bf16[512,128]{1,0:T(8,128)(2,1)S(1)}, u32[]{:S(2)}, u32[]{:S(2)}) %collective-permute-start.6) | collective-permute-done | bytes 131104 | tf_op jit(solution)/shard_map/ppermute | solution.py:432
  47.2 7.1 %collective-permute-start.9 = (bf16[256,128]{1,0:T(8,128)(2,1)S(1)}, bf16[256,128]{1,0:T(8,128)(2,1)S(1)}, u32[]{:S(2)}, u32[]{:S(2)}) collective-permute-start(bf16[256,128]{1,0:T(8,128)(2,1)S(1)} %get-tuple-element.67), channel_id=1, source_target_pairs={{8,12},{12,16},{16,20},{20,8},{24,28},{28,32},{32,36},{36,24},{40,... | collective-permute-start | bytes 196616 | tf_op jit(solution)/shard_map/ppermute | solution.py:422
  54.3 3.4 %own_forward.1 = (bf16[1024,1024]{1,0:T(8,128)(2,1)S(1)}, bf16[512,512]{1,0:T(8,128)(2,1)S(1)}, bf16[256,256]{1,0:T(8,128)(2,1)S(1)}, f32[1024,128]{1,0:T(8,128)S(1)}, f32[1024,256]{1,0:T(8,128)S(1)}) custom-call(s32[4,3]{1,0:T(4,128)S(1)} %copy-done.1, bf16[1024,128]{1,0:T(8,128)(2,1)S(1)} %get-tuple-element.54.qa, ...), custom_call_target="tpu_custom_call" | custom-call | flops 1000000000 | bytes 6291456 | tf_op jit(solution)/shard_map/own_forward/pallas_call | solution.py:70
  57.8 3.4 %collective-permute-done.5.xb = bf16[512,128]{1,0:T(8,128)(2,1)S(1)} collective-permute-done((bf16[512,128]{1,0:T(8,128)(2,1)S(1)}, bf16[512,128]{1,0:T(8,128)(2,1)S(1)}, u32[]{:S(2)}, u32[]{:S(2)}) %collective-permute-start.5) | collective-permute-done | bytes 131104 | tf_op jit(solution)/shard_map/ppermute | solution.py:432
  61.2 4.6 %cross.1 = (bf16[1024,128]{1,0:T(8,128)(2,1)S(1)}, f32[1024,128]{1,0:T(8,128)S(1)}, f32[1024,128]{1,0:T(8,128)S(1)}, f32[1024,128]{1,0:T(8,128)S(1)}, bf16[1536,...) custom-call(s32[4,3]{1,0:T(4,128)S(1)} %copy-done.1, ...), custom_call_target="tpu_custom_call" | custom-call | flops 1000000000 | bytes 6291456 | tf_op jit(solution)/shard_map/cross/pallas_call | solution.py:70
  65.9 1.3 %collective-permute-start.14 = (bf16[1536,128]{1,0:T(8,128)(2,1)S(1)}, bf16[1536,128]{1,0:T(8,128)(2,1)S(1)}, u32[]{:S(2)}, u32[]{:S(2)}) collective-permute-start(bf16[1536,128]{1,0:T(8,128)(2,1)S(1)} %get-tuple-element.82), channel_id=1, source_target_pairs={{36,8},{32,12},{28,16},{24,20},{68,40},{64,44},{60,48},{56,52},{10... | collective-permute-start | bytes 1179656 | tf_op jit(solution)/shard_map/ppermute | solution.py:432
  67.2 1.3 %collective-permute-start.15 = (bf16[512,128]{1,0:T(8,128)(2,1)S(1)}, bf16[512,128]{1,0:T(8,128)(2,1)S(1)}, u32[]{:S(2)}, u32[]{:S(2)}) collective-permute-start(bf16[512,128]{1,0:T(8,128)(2,1)S(1)} %get-tuple-element.83), channel_id=1, source_target_pairs={{52,24},{48,28},{44,32},{40,36},{68,8},{64,12},{60,16},{56,20},{11... | collective-permute-start | bytes 393224 | tf_op jit(solution)/shard_map/ppermute | solution.py:432
  68.5 3.0 %collective-permute-start.16 = (bf16[512,128]{1,0:T(8,128)(2,1)S(1)}, bf16[512,128]{1,0:T(8,128)(2,1)S(1)}, u32[]{:S(2)}, u32[]{:S(2)}) collective-permute-start(bf16[512,128]{1,0:T(8,128)(2,1)S(1)} %get-tuple-element.84), channel_id=1, source_target_pairs={{40,8},{44,12},{48,16},{52,20},{56,24},{60,28},{64,32},{68,36},{10... | collective-permute-start | bytes 393224 | tf_op jit(solution)/shard_map/ppermute | solution.py:432
  71.5 4.5 %own_backward.1 = (bf16[256,128]{1,0:T(8,128)(2,1)S(1)}, bf16[256,128]{1,0:T(8,128)(2,1)S(1)}, bf16[256,128]{1,0:T(8,128)(2,1)S(1)}, bf16[256,128]{1,0:T(8,128)(2,1)S(1)}, f32[2048,128]{1,0:T(8,128)S(1)}) custom-call(s32[4,3]{1,0:T(4,128)S(1)} %copy-done.1, bf16[1024,1024]{1,0:T(8,128)(2,1)S(1)} %get-tuple-element.57.e0, ...), custom_call_target="tpu_custom_call" | custom-call | flops 2000000000 | bytes 8388608 | tf_op jit(solution)/shard_map/own_backward/pallas_call | solution.py:70
  76.0 6.3 %collective-permute-start.12 = (bf16[256,128]{1,0:T(8,128)(2,1)S(1)}, bf16[256,128]{1,0:T(8,128)(2,1)S(1)}, u32[]{:S(2)}, u32[]{:S(2)}) collective-permute-start(bf16[256,128]{1,0:T(8,128)(2,1)S(1)} %get-tuple-element.77), channel_id=1, source_target_pairs={{8,12},{12,16},{16,20},{20,8},{24,28},{28,32},{32,36},{36,24},{40,... | collective-permute-start | bytes 196616 | tf_op jit(solution)/shard_map/ppermute | solution.py:422
  82.2 2.4 %collective-permute-start.13 = (bf16[256,128]{1,0:T(8,128)(2,1)S(1)}, bf16[256,128]{1,0:T(8,128)(2,1)S(1)}, u32[]{:S(2)}, u32[]{:S(2)}) collective-permute-start(bf16[256,128]{1,0:T(8,128)(2,1)S(1)} %get-tuple-element.79), channel_id=1, source_target_pairs={{8,16},{12,20},{16,8},{20,12},{24,32},{28,36},{32,24},{36,28},{40,... | collective-permute-start | bytes 196616 | tf_op jit(solution)/shard_map/ppermute | solution.py:422
  84.7 8.4 %collective-permute-done.13.p2 = bf16[256,128]{1,0:T(8,128)(2,1)S(1)} collective-permute-done((bf16[256,128]{1,0:T(8,128)(2,1)S(1)}, bf16[256,128]{1,0:T(8,128)(2,1)S(1)}, u32[]{:S(2)}, u32[]{:S(2)}) %collective-permute-start.13) | collective-permute-done | bytes 65568 | tf_op jit(solution)/shard_map/ppermute | solution.py:422
  93.1 0.8 combine.1
  94.0 9.5 %collective-permute-start.17 = (bf16[512,128]{1,0:T(8,128)(2,1)S(1)}, bf16[512,128]{1,0:T(8,128)(2,1)S(1)}, u32[]{:S(2)}, u32[]{:S(2)}) collective-permute-start(bf16[512,128]{1,0:T(8,128)(2,1)S(1)} %get-tuple-element.87), channel_id=1, source_target_pairs={{8,12},{12,16},{16,20},{20,8},{24,28},{28,32},{32,36},{36,24},{40,... | collective-permute-start | bytes 393224 | tf_op jit(solution)/shard_map/ppermute | solution.py:422
  104.5 1.6 %collective-permute-done.17.p1 = bf16[512,128]{1,0:T(8,128)(2,1)S(1)} collective-permute-done((bf16[512,128]{1,0:T(8,128)(2,1)S(1)}, bf16[512,128]{1,0:T(8,128)(2,1)S(1)}, u32[]{:S(2)}, u32[]{:S(2)}) %collective-permute-start.17) | collective-permute-done | bytes 131104 | tf_op jit(solution)/shard_map/ppermute | solution.py:422
  106.1 9.1 %collective-permute-done.18.p2 = bf16[512,128]{1,0:T(8,128)(2,1)S(1)} collective-permute-done((bf16[512,128]{1,0:T(8,128)(2,1)S(1)}, bf16[512,128]{1,0:T(8,128)(2,1)S(1)}, u32[]{:S(2)}, u32[]{:S(2)}) %collective-permute-start.18) | collective-permute-done | bytes 131104 | tf_op jit(solution)/shard_map/ppermute | solution.py:422
  115.2 1.3 %finish.1 = (bf16[256,512]{1,0:T(8,128)(2,1)}, bf16[256,512]{1,0:T(8,128)(2,1)}, bf16[256,512]{1,0:T(8,128)(2,1)}) custom-call(bf16[256,512]{1,0:T(8,128)(2,1)S(1)} %finish_query.1.dq_in, bf16[512,128]{1,0:T(8,128)(2,1)S(1)} %get-tuple-element.85.p0, bf16[512,128]{1,0:T(8,128)(2,1)S(1)} %collective-permute-done.17.p1, ...), custom_call_target="tpu_custom_call" | custom-call | tf_op jit(solution)/shard_map/finish/pallas_call | solution.py:70
  (22 shorter events, 1.1 us)
Async XLA Ops:
  2.5 21.2 %collective-permute-start.1 = (bf16[256,1024]{1,0:T(8,128)(2,1)}, bf16[256,1024]{1,0:T(8,128)(2,1)S(1)}, u32[]{:S(2)}, u32[]{:S(2)}) collective-permute-start(bf16[256,1024]{1,0:T(8,128)(2,1)} %g0.1), channel_id=1, source_target_pairs={{0,1},{1,0},{2,3},{3,2},{4,5},{5,4},{6,7},{7,6},{8,9},{9,8},{10,11... | collective-permute-start | bytes 1572872 | tf_op jit(solution)/shard_map/ppermute | solution.py:435
  2.6 26.9 %collective-permute-start.7 = (bf16[256,1024]{1,0:T(8,128)(2,1)}, bf16[256,1024]{1,0:T(8,128)(2,1)S(1)}, u32[]{:S(2)}, u32[]{:S(2)}) collective-permute-start(bf16[256,1024]{1,0:T(8,128)(2,1)} %g0.1), channel_id=1, source_target_pairs={{0,2},{1,3},{2,0},{3,1},{4,6},{5,7},{6,4},{7,5},{8,10},{9,11},{10,... | collective-permute-start | bytes 1572872 | tf_op jit(solution)/shard_map/ppermute | solution.py:435
  4.2 22.8 %collective-permute-start.2 = (bf16[768,128]{1,0:T(8,128)(2,1)S(1)}, bf16[768,128]{1,0:T(8,128)(2,1)S(1)}, u32[]{:S(2)}, u32[]{:S(2)}) collective-permute-start(bf16[768,128]{1,0:T(8,128)(2,1)S(1)} %get-tuple-element.52), channel_id=1, source_target_pairs={{8,16},{12,20},{16,8},{20,12},{24,32},{28,36},{32,24},{36,28},{40,... | collective-permute-start | bytes 589832 | tf_op jit(solution)/shard_map/ppermute | solution.py:422
  14.2 15.3 %collective-permute-start.3 = (bf16[768,128]{1,0:T(8,128)(2,1)S(1)}, bf16[768,128]{1,0:T(8,128)(2,1)S(1)}, u32[]{:S(2)}, u32[]{:S(2)}) collective-permute-start(bf16[768,128]{1,0:T(8,128)(2,1)S(1)} %get-tuple-element.53), channel_id=1, source_target_pairs={{8,20},{12,8},{16,12},{20,16},{24,36},{28,24},{32,28},{36,32},{40,... | collective-permute-start | bytes 589832 | tf_op jit(solution)/shard_map/ppermute | solution.py:422
  15.2 14.3 %collective-permute-start = (bf16[768,128]{1,0:T(8,128)(2,1)S(1)}, bf16[768,128]{1,0:T(8,128)(2,1)S(1)}, u32[]{:S(2)}, u32[]{:S(2)}) collective-permute-start(bf16[768,128]{1,0:T(8,128)(2,1)S(1)} %get-tuple-element.48), channel_id=1, source_target_pairs={{8,12},{12,16},{16,20},{20,8},{24,28},{28,32},{32,36},{36,24},{40,... | collective-permute-start | bytes 589832 | tf_op jit(solution)/shard_map/ppermute | solution.py:422
  23.7 1.0 copy-start
  24.8 4.7 %copy-start.1 = (s32[4,3]{1,0:T(4,128)S(1)}, s32[4,3]{1,0:T(4,128)}, u32[]{:S(2)}) copy-start(s32[4,3]{1,0:T(4,128)} %offsets.9) | copy-start | bytes 148
  29.5 4.6 %collective-permute-start.8 = (bf16[256,1024]{1,0:T(8,128)(2,1)S(1)}, bf16[256,1024]{1,0:T(8,128)(2,1)S(1)}, u32[]{:S(2)}, u32[]{:S(2)}) collective-permute-start(bf16[256,1024]{1,0:T(8,128)(2,1)S(1)} %collective-permute-done.7.g2), channel_id=1, source_target_pairs={{0,1},{1,0},{2,3},{3,2},{4,5},{5,4},{6,7},{7,6},{8,9},{9,8},{10,11... | collective-permute-start | bytes 1572872 | tf_op jit(solution)/shard_map/ppermute | solution.py:435
  30.2 31.0 %collective-permute-start.4 = (bf16[1536,128]{1,0:T(8,128)(2,1)S(1)}, bf16[1536,128]{1,0:T(8,128)(2,1)S(1)}, u32[]{:S(2)}, u32[]{:S(2)}) collective-permute-start(bf16[1536,128]{1,0:T(8,128)(2,1)S(1)} %get-tuple-element.56.both), channel_id=1, source_target_pairs={{8,36},{12,32},{16,28},{20,24},{40,68},{44,64},{48,60},{52,56},{72... | collective-permute-start | bytes 1179656 | tf_op jit(solution)/shard_map/ppermute | solution.py:432
  31.5 15.7 %collective-permute-start.6 = (bf16[512,128]{1,0:T(8,128)(2,1)S(1)}, bf16[512,128]{1,0:T(8,128)(2,1)S(1)}, u32[]{:S(2)}, u32[]{:S(2)}) collective-permute-start(bf16[512,128]{1,0:T(8,128)(2,1)S(1)} %get-tuple-element.60), channel_id=1, source_target_pairs={{8,40},{12,44},{16,48},{20,52},{24,56},{28,60},{32,64},{36,68},{72... | collective-permute-start | bytes 393224 | tf_op jit(solution)/shard_map/ppermute | solution.py:432
  32.8 28.4 %collective-permute-start.5 = (bf16[512,128]{1,0:T(8,128)(2,1)S(1)}, bf16[512,128]{1,0:T(8,128)(2,1)S(1)}, u32[]{:S(2)}, u32[]{:S(2)}) collective-permute-start(bf16[512,128]{1,0:T(8,128)(2,1)S(1)} %get-tuple-element.60), channel_id=1, source_target_pairs={{24,52},{28,48},{32,44},{36,40},{8,68},{12,64},{16,60},{20,56},{88... | collective-permute-start | bytes 393224 | tf_op jit(solution)/shard_map/ppermute | solution.py:432
  35.1 26.1 %collective-permute-start.11 = (bf16[256,128]{1,0:T(8,128)(2,1)S(1)}, bf16[256,128]{1,0:T(8,128)(2,1)S(1)}, u32[]{:S(2)}, u32[]{:S(2)}) collective-permute-start(bf16[256,128]{1,0:T(8,128)(2,1)S(1)} %get-tuple-element.71), channel_id=1, source_target_pairs={{8,20},{12,8},{16,12},{20,16},{24,36},{28,24},{32,28},{36,32},{40,... | collective-permute-start | bytes 196616 | tf_op jit(solution)/shard_map/ppermute | solution.py:422
  38.3 22.9 %collective-permute-start.10 = (bf16[256,128]{1,0:T(8,128)(2,1)S(1)}, bf16[256,128]{1,0:T(8,128)(2,1)S(1)}, u32[]{:S(2)}, u32[]{:S(2)}) collective-permute-start(bf16[256,128]{1,0:T(8,128)(2,1)S(1)} %get-tuple-element.69), channel_id=1, source_target_pairs={{8,16},{12,20},{16,8},{20,12},{24,32},{28,36},{32,24},{36,28},{40,... | collective-permute-start | bytes 196616 | tf_op jit(solution)/shard_map/ppermute | solution.py:422
  47.2 14.0 %collective-permute-start.9 = (bf16[256,128]{1,0:T(8,128)(2,1)S(1)}, bf16[256,128]{1,0:T(8,128)(2,1)S(1)}, u32[]{:S(2)}, u32[]{:S(2)}) collective-permute-start(bf16[256,128]{1,0:T(8,128)(2,1)S(1)} %get-tuple-element.67), channel_id=1, source_target_pairs={{8,12},{12,16},{16,20},{20,8},{24,28},{28,32},{32,36},{36,24},{40,... | collective-permute-start | bytes 196616 | tf_op jit(solution)/shard_map/ppermute | solution.py:422
  65.9 27.3 %collective-permute-start.14 = (bf16[1536,128]{1,0:T(8,128)(2,1)S(1)}, bf16[1536,128]{1,0:T(8,128)(2,1)S(1)}, u32[]{:S(2)}, u32[]{:S(2)}) collective-permute-start(bf16[1536,128]{1,0:T(8,128)(2,1)S(1)} %get-tuple-element.82), channel_id=1, source_target_pairs={{36,8},{32,12},{28,16},{24,20},{68,40},{64,44},{60,48},{56,52},{10... | collective-permute-start | bytes 1179656 | tf_op jit(solution)/shard_map/ppermute | solution.py:432
  67.2 26.0 %collective-permute-start.15 = (bf16[512,128]{1,0:T(8,128)(2,1)S(1)}, bf16[512,128]{1,0:T(8,128)(2,1)S(1)}, u32[]{:S(2)}, u32[]{:S(2)}) collective-permute-start(bf16[512,128]{1,0:T(8,128)(2,1)S(1)} %get-tuple-element.83), channel_id=1, source_target_pairs={{52,24},{48,28},{44,32},{40,36},{68,8},{64,12},{60,16},{56,20},{11... | collective-permute-start | bytes 393224 | tf_op jit(solution)/shard_map/ppermute | solution.py:432
  68.5 24.7 %collective-permute-start.16 = (bf16[512,128]{1,0:T(8,128)(2,1)S(1)}, bf16[512,128]{1,0:T(8,128)(2,1)S(1)}, u32[]{:S(2)}, u32[]{:S(2)}) collective-permute-start(bf16[512,128]{1,0:T(8,128)(2,1)S(1)} %get-tuple-element.84), channel_id=1, source_target_pairs={{40,8},{44,12},{48,16},{52,20},{56,24},{60,28},{64,32},{68,36},{10... | collective-permute-start | bytes 393224 | tf_op jit(solution)/shard_map/ppermute | solution.py:432
  76.0 8.7 %collective-permute-start.12 = (bf16[256,128]{1,0:T(8,128)(2,1)S(1)}, bf16[256,128]{1,0:T(8,128)(2,1)S(1)}, u32[]{:S(2)}, u32[]{:S(2)}) collective-permute-start(bf16[256,128]{1,0:T(8,128)(2,1)S(1)} %get-tuple-element.77), channel_id=1, source_target_pairs={{8,12},{12,16},{16,20},{20,8},{24,28},{28,32},{32,36},{36,24},{40,... | collective-permute-start | bytes 196616 | tf_op jit(solution)/shard_map/ppermute | solution.py:422
  82.2 10.9 %collective-permute-start.13 = (bf16[256,128]{1,0:T(8,128)(2,1)S(1)}, bf16[256,128]{1,0:T(8,128)(2,1)S(1)}, u32[]{:S(2)}, u32[]{:S(2)}) collective-permute-start(bf16[256,128]{1,0:T(8,128)(2,1)S(1)} %get-tuple-element.79), channel_id=1, source_target_pairs={{8,16},{12,20},{16,8},{20,12},{24,32},{28,36},{32,24},{36,28},{40,... | collective-permute-start | bytes 196616 | tf_op jit(solution)/shard_map/ppermute | solution.py:422
  93.9 21.2 %collective-permute-start.19 = (bf16[768,128]{1,0:T(8,128)(2,1)S(1)}, bf16[768,128]{1,0:T(8,128)(2,1)S(1)}, u32[]{:S(2)}, u32[]{:S(2)}) collective-permute-start(bf16[768,128]{1,0:T(8,128)(2,1)S(1)} %get-tuple-element.90), channel_id=1, source_target_pairs={{8,20},{12,8},{16,12},{20,16},{24,36},{28,24},{32,28},{36,32},{40,... | collective-permute-start | bytes 589832 | tf_op jit(solution)/shard_map/ppermute | solution.py:422
  94.0 12.1 %collective-permute-start.17 = (bf16[512,128]{1,0:T(8,128)(2,1)S(1)}, bf16[512,128]{1,0:T(8,128)(2,1)S(1)}, u32[]{:S(2)}, u32[]{:S(2)}) collective-permute-start(bf16[512,128]{1,0:T(8,128)(2,1)S(1)} %get-tuple-element.87), channel_id=1, source_target_pairs={{8,12},{12,16},{16,20},{20,8},{24,28},{28,32},{32,36},{36,24},{40,... | collective-permute-start | bytes 393224 | tf_op jit(solution)/shard_map/ppermute | solution.py:422
  103.6 11.6 %collective-permute-start.18 = (bf16[512,128]{1,0:T(8,128)(2,1)S(1)}, bf16[512,128]{1,0:T(8,128)(2,1)S(1)}, u32[]{:S(2)}, u32[]{:S(2)}) collective-permute-start(bf16[512,128]{1,0:T(8,128)(2,1)S(1)} %get-tuple-element.89), channel_id=1, source_target_pairs={{8,16},{12,20},{16,8},{20,12},{24,32},{28,36},{32,24},{36,28},{40,... | collective-permute-start | bytes 393224 | tf_op jit(solution)/shard_map/ppermute | solution.py:422

commit v3 on v2

--- a/solution.py
+++ b/solution.py
@@ -82,7 +82,7 @@
             ],
             out_specs=[pl.BlockSpec(memory_space=pltpu.VMEM)] * len(outs),
             scratch_shapes=list(scratch),
-            compiler_params=pltpu.CompilerParams(vmem_limit_bytes=40 << 20),
+            compiler_params=pltpu.CompilerParams(vmem_limit_bytes=16 << 20),
             cost_estimate=pl.CostEstimate(
                 flops=flops, bytes_accessed=bytes_accessed, transcendentals=0
             ),
@@ -229,61 +229,56 @@
     pq1, pq2, pd1, pd2, sc1, sc2, e1, e2, newtop, newout, inv, vx1, vx2,
 ):
     place, block, off1, group2 = places(offsets)
-    second, later = (block & 1) == 1, block >= 2
-    x1, g1 = xa.at[:1024], ga.at[:1024]
-    earlier = (
-        (second, xa.at[1024:], ga.at[1024:]),
-        (later, xb, gb),
-        (later, xc, gc),
-    )
+    where1 = [rows_at(b * 256 + off1 * 128, 128) for b in range(4)]
+    where2 = [rows_at(b * 256 + group2 * 64, 64) for b in range(4)]
+    one = (xa.at[:1024], ga.at[:1024], sc1, e1, vx1, where1, pq1, pd1)
+    two = [
+        (x, g, sc2.at[d], e2.at[d], vx2.at[d], where2, pq2, pd2)
+        for d, (x, g) in enumerate(((xa.at[1024:], ga.at[1024:]), (xb, gb), (xc, gc)))
+    ]
+    groups = (((block & 1) == 1, (one, two[0])), (block >= 2, two[1:]))
     for s, piece in enumerate((p0, p1, p2, p3)):
         doa[rows_at(((place - s) & 3) * TOK, TOK)] = piece[...]
-    where1 = [rows_at(b * 256 + off1 * 128, 128) for b in range(4)]
-    where2 = [rows_at(b * 256 + group2 * 64, 64) for b in range(4)]
     for b in range(4):
         pq1[b * 128 : (b + 1) * 128] = qa[where1[b]]
         pq2[b * 64 : (b + 1) * 64] = qa[where2[b]]
     newtop[...] = top[...]
 
-    @pl.when(second)
-    def _():
-        ones_beside(vx1, x1[512:])
-        sc1[...] = dot_nt(pq1[...], x1[:512]) * SCALE2
-        for b in range(4):
-            high = wide_max(sc1[b * 128 : (b + 1) * 128])
-            newtop[where1[b]] = jnp.maximum(newtop[where1[b]], high)
-
-    for d, (valid, x2, _) in enumerate(earlier):
+    for valid, tiles in groups:
 
         @pl.when(valid)
-        def _(d=d, x2=x2):
-            ones_beside(vx2.at[d], x2[256:])
-            sc2[d] = dot_nt(pq2[...], x2[:256]) * SCALE2
-            for b in range(4):
-                high = wide_max(sc2[d, b * 64 : (b + 1) * 64])
-                newtop[where2[b]] = jnp.maximum(newtop[where2[b]], high)
+        def _(tiles=tiles):
+            highs = []
+            for x, _, scores, _, values, _, queries, _ in tiles:
+                half = x.shape[0] // 2
+                ones_beside(values, x[half:])
+                product = dot_nt(queries[...], x[:half]) * SCALE2
+                scores[...] = product
+                highs.append(wide_max(product))
+            for high, (_, _, _, _, _, where, _, _) in zip(highs, tiles):
+                size = high.shape[0] // 4
+                for b in range(4):
+                    part = high[b * size : (b + 1) * size]
+                    newtop[where[b]] = jnp.maximum(newtop[where[b]], part)
 
     shrink = jnp.exp2(top[...] - newtop[...])
     newout[:, :DIM] = out[:, :DIM] * shrink
     newout[:, DIM:] = out[:, DIM:] * shrink
 
-    @pl.when(second)
-    def _():
-        for b in range(4):
-            part = slice(b * 128, (b + 1) * 128)
-            w = jnp.exp2(sc1[part] - newtop[where1[b]][:, :1]).astype(BF16)
-            e1[part] = w
-            newout[where1[b]] += dot_nn(w, vx1[...])
-
-    for d, (valid, _, _) in enumerate(earlier):
+    for valid, tiles in groups:
 
         @pl.when(valid)
-        def _(d=d):
-            for b in range(4):
-                part = slice(b * 64, (b + 1) * 64)
-                w = jnp.exp2(sc2[d, part] - newtop[where2[b]][:, :1]).astype(BF16)
-                e2[d, part] = w
-                newout[where2[b]] += dot_nn(w, vx2[d])
+        def _(tiles=tiles):
+            sums = []
+            for _, _, scores, weights, values, where, _, _ in tiles:
+                level = jnp.concatenate([newtop[r][:, :1] for r in where], axis=0)
+                w = jnp.exp2(scores[...] - level).astype(BF16)
+                weights[...] = w
+                sums.append(dot_nn(w, values[...]))
+            for total, (_, _, _, _, _, where, _, _) in zip(sums, tiles):
+                size = total.shape[0] // 4
+                for b in range(4):
+                    newout[where[b]] += total[b * size : (b + 1) * size]
 
     inv[...] = 1.0 / newout[:, DIM:]
     grads = doa[...].astype(F32)
@@ -295,34 +290,29 @@
         pd1[b * 128 : (b + 1) * 128] = (doa[where1[b]].astype(F32) * inv[where1[b]]).astype(BF16)
         pd2[b * 64 : (b + 1) * 64] = (doa[where2[b]].astype(F32) * inv[where2[b]]).astype(BF16)
 
-    @pl.when(second)
-    def _():
-        prob = dot_nt(pd1[...], x1[512:])
-        level = jnp.concatenate([(delta[r] * inv[r])[:, :1] for r in where1], axis=0)
-        score_grad = (e1[...].astype(F32) * (prob - level)).astype(BF16)
-        part = dot_nn(score_grad, x1[:512])
-        for b in range(4):
-            dq[where1[b]] += part[b * 128 : (b + 1) * 128]
-        g1[:512] = (dot_tn(score_grad, pq1[...]) * SCALE).astype(BF16)
-        g1[512:] = dot_tn(e1[...], pd1[...]).astype(BF16)
-
-    for d, (valid, x2, g2) in enumerate(earlier):
+    for valid, tiles in groups:
 
         @pl.when(valid)
-        def _(d=d, x2=x2, g2=g2):
-            prob = dot_nt(pd2[...], x2[256:])
-            level = jnp.concatenate([(delta[r] * inv[r])[:, :1] for r in where2], axis=0)
-            score_grad = (e2[d].astype(F32) * (prob - level)).astype(BF16)
-            part = dot_nn(score_grad, x2[:256])
-            for b in range(4):
-                dq[where2[b]] += part[b * 64 : (b + 1) * 64]
-            g2[:256] = (dot_tn(score_grad, pq2[...]) * SCALE).astype(BF16)
-            g2[256:] = dot_tn(e2[d], pd2[...]).astype(BF16)
+        def _(tiles=tiles):
+            parts = []
+            for x, g, _, weights, _, where, queries, grad_low in tiles:
+                half = x.shape[0] // 2
+                prob = dot_nt(grad_low[...], x[half:])
+                level = jnp.concatenate([(delta[r] * inv[r])[:, :1] for r in where], axis=0)
+                w = weights[...]
+                score_grad = (w.astype(F32) * (prob - level)).astype(BF16)
+                g[half:] = dot_tn(w, grad_low[...]).astype(BF16)
+                g[:half] = (dot_tn(score_grad, queries[...]) * SCALE).astype(BF16)
+                parts.append(dot_nn(score_grad, x[:half]))
+            for part, (_, _, _, _, _, where, _, _) in zip(parts, tiles):
+                size = part.shape[0] // 4
+                for b in range(4):
+                    dq[where[b]] += part[b * size : (b + 1) * size]
 
 
 def own_backward_kernel(
     offsets, e0, e1, e2, factor, delta, doa, qa, kv, both, dq_in,
-    o0, o1, o2, o3, dkv, dq, low, shift, dkv1, dkv2, low_q,
+    o0, o1, o2, o3, dkv, dq, low, shift, dkv1, dkv2,
 ):
     place, _, off1, group2 = places(offsets)
     kv1, kv2 = both.at[:1024], both.at[1024:]
@@ -363,52 +353,51 @@
             dkv[rows_at(part * BLOCK + p * 256 + group2 * 64, 64)] += dkv2[
                 part * 256 + p * 64 : part * 256 + (p + 1) * 64
             ]
-    dkv[:BLOCK] = dkv[:BLOCK] * SCALE
-    low_q[...] = (dq[...] * SCALE).astype(BF16)
     for s, target in enumerate((o0, o1, o2, o3)):
-        target[...] = low_q[rows_at(((place + s) & 3) * TOK, TOK)]
-
-
-def combine_kernel(offsets, dkv, last_q, ya, yb, yc, o0, o1, o2, o3, total):
-    home, _, off1, group2 = places(offsets)
-    y1, y2 = ya.at[:1024], ya.at[1024:]
-    total[...] = dkv[...]
-    for p in range(4):
+        at = ((place + s) & 3) * TOK
+        target[:TOK] = (dkv[rows_at(at, TOK)] * SCALE).astype(BF16)
+        target[TOK : 2 * TOK] = dkv[rows_at(BLOCK + at, TOK)].astype(BF16)
+        target[2 * TOK :] = (dq[rows_at(at, TOK)] * SCALE).astype(BF16)
+
+
+def combine_kernel(ya, yb, yc, o0, o1, o2, o3):
+    place, _ = place_and_block()
+    for s, target in enumerate((o0, o1, o2, o3)):
+        token = (place + s) & 3
         for part in range(2):
-            one = slice(part * 512 + p * 128, part * 512 + (p + 1) * 128)
-            two = slice(part * 256 + p * 64, part * 256 + (p + 1) * 64)
-            total[rows_at(part * BLOCK + p * 256 + off1 * 128, 128)] += y1[one].astype(F32)
-            total[rows_at(part * BLOCK + p * 256 + group2 * 64, 64)] += (
-                y2[two].astype(F32) + yb[two].astype(F32) + yc[two].astype(F32)
-            )
-    for s, target in enumerate((o0, o1, o2, o3)):
-        place = (home + s) & 3
-        for part in range(2):
-            target[part * TOK : (part + 1) * TOK] = total[
-                rows_at(part * BLOCK + place * TOK, TOK)
-            ].astype(BF16)
-    o3[2 * TOK :] = last_q[...]
-
-
-def unsort_pieces(pieces, outs):
+            one = rows_at(part * 512 + token * 128, 128)
+            two = part * 256 + token * 64
+            target[part * 128 : (part + 1) * 128] = ya[one]
+            target[256 + part * 64 : 256 + (part + 1) * 64] = (
+                ya[rows_at(1024 + two, 64)].astype(F32)
+                + yb[rows_at(two, 64)].astype(F32)
+                + yc[rows_at(two, 64)].astype(F32)
+            ).astype(BF16)
+
+
+def finish_query_kernel(p0, p1, p2, p3, dq):
     place, block = place_and_block()
     unsort = unsort_matrix()
-    for s, piece in enumerate(pieces):
+    for s, piece in enumerate((p0, p1, p2, p3)):
         cols = cols_at(head_at((place - s) & 3, block))
-        for i, out in enumerate(outs):
-            out[:, cols] = dot_nn(unsort, piece[i * TOK : (i + 1) * TOK]).astype(BF16)
-
-
-def finish_query_kernel(p0, p1, p2, dq):
-    unsort_pieces((p0, p1, p2), (dq,))
-
-
-def finish_kernel(dq_in, p0, p1, p2, p3, dq, dk, dv):
-    dq[...] = dq_in[...]
-    unsort_pieces((p0, p1, p2, p3), (dk, dv))
+        dq[:, cols] = dot_nn(unsort, piece[2 * TOK :]).astype(BF16)
+
+
+def finish_kernel(offsets, p0, p1, p2, p3, c0, c1, c2, c3, dk, dv, total):
     place, block = place_and_block()
-    last = dot_nn(unsort_matrix(), p3[2 * TOK :]).astype(BF16)
-    dq[:, cols_at(head_at((place - 3) & 3, block))] = last
+    unsort = unsort_matrix()
+    for s, (piece, cross) in enumerate(((p0, c0), (p1, c1), (p2, c2), (p3, c3))):
+        head = head_at((place - s) & 3, block)
+        off1, off2 = offsets[head, 1], offsets[head, 2]
+        group2 = ((off2 & 1) << 1) | (off2 >> 1)
+        cols = cols_at(head)
+        for part, out in enumerate((dk, dv)):
+            both = total.at[2 * s + part]
+            both[...] = piece[part * TOK : (part + 1) * TOK].astype(F32)
+            rows1, rows2 = rows_at(off1 * 128, 128), rows_at(group2 * 64, 64)
+            both[rows1] += cross[part * 128 : (part + 1) * 128].astype(F32)
+            both[rows2] += cross[256 + part * 64 : 256 + (part + 1) * 64].astype(F32)
+            out[:, cols] = dot_nn(unsort, both[...].astype(BF16)).astype(BF16)
 
 
 def local(queries, keys, values, out_grad, w_out, offsets):
@@ -417,8 +406,12 @@
     def at(index):
         return (index + 2) % devices
 
-    def exchange(part, s):
-        route = [(at(u), at(u // 4 * 4 + (u % 4 + s) % 4)) for u in range(devices)]
+    def exchange(part, s, blocks=(0, 1, 2, 3)):
+        route = [
+            (at(u), at(u // 4 * 4 + (u % 4 + s) % 4))
+            for u in range(devices)
+            if u // 4 % 4 in blocks
+        ]
         return lax.ppermute(part, "ctx", route)
 
     def to_blocks(part, pairs, back=False):
@@ -482,8 +475,9 @@
         flops=10**7,
         bytes_accessed=2 << 20,
     )(offsets, packed[0], after(pieces[0], near), *pieces[1:])
-    xs = [to_blocks(part, pairs) for part, pairs in zip((both, kv2, kv2), links)]
-    grad_parts = [grads[0]] + [exchange(after(grads[s], kv2), s) for s in (1, 2, 3)]
+    first, rest = after(both, grads[1]), after(kv2, grads[1])
+    xs = [to_blocks(part, pairs) for part, pairs in zip((first, rest, rest), links)]
+    grad_parts = [grads[0]] + [exchange(grads[s], s) for s in (1, 2, 3)]
 
     e0, e1, e2, top, out = call(
         own_forward_kernel,
@@ -536,39 +530,46 @@
     )(offsets, qa, *xs, top, out, *grad_parts)
     ys = [to_blocks(part, pairs, back=True) for part, pairs in zip(partials, links)]
 
-    *dq_parts, dkv = call(
+    own_parts = call(
         own_backward_kernel,
-        [((TOK, DIM), BF16)] * 4 + [((2 * BLOCK, DIM), F32)],
+        [((3 * TOK, DIM), BF16)] * 4,
         [
+            pltpu.VMEM((2 * BLOCK, DIM), F32),
             pltpu.VMEM((BLOCK, DIM), F32),
             pltpu.VMEM((BLOCK, DIM), BF16),
             pltpu.VMEM((BLOCK, DIM), F32),
             pltpu.VMEM((1024, DIM), F32),
             pltpu.VMEM((512, DIM), F32),
-            pltpu.VMEM((BLOCK, DIM), BF16),
         ],
         name="own_backward",
         flops=2 * 10**9,
         bytes_accessed=8 << 20,
     )(offsets, e0, e1, e2, factor, delta, doa, qa, kv, both, dq)
-    near_parts = [dq_parts[0]] + [exchange(dq_parts[s], s) for s in (1, 2)]
-
-    pairs = call(
+    own_parts = list(own_parts)
+    own_parts[3] = after(own_parts[3], *ys[1:])
+    own_parts = [own_parts[0]] + [exchange(own_parts[s], s) for s in (1, 2, 3)]
+
+    cross_parts = call(
         combine_kernel,
-        [((2 * TOK, DIM), BF16)] * 3 + [((3 * TOK, DIM), BF16)],
-        [pltpu.VMEM((2 * BLOCK, DIM), F32)],
+        [((384, DIM), BF16)] * 4,
         name="combine",
         flops=10**7,
-        bytes_accessed=4 << 20,
-    )(offsets, after(dkv, *near_parts), dq_parts[3], *ys)
+        bytes_accessed=1 << 20,
+    )(after(ys[0], *own_parts[:3]), *ys[1:])
+    cross_parts = [cross_parts[0]] + [
+        exchange(cross_parts[s], s, (0, 1, 2)) for s in (1, 2, 3)
+    ]
     query_grad = call(finish_query_kernel, [((TOK, 4 * DIM), BF16)], name="finish_query")(
-        near_parts[0], after(near_parts[1], pairs[0]), near_parts[2]
+        *own_parts
     )[0]
-    pairs = [pairs[0]] + [exchange(pairs[s], s) for s in (1, 2, 3)]
-    pairs[1] = after(pairs[1], query_grad)
-    return tuple(
-        call(finish_kernel, [((TOK, 4 * DIM), BF16)] * 3, name="finish")(query_grad, *pairs)
-    )
+    cross_parts[1] = after(cross_parts[1], query_grad)
+    key_value_grads = call(
+        finish_kernel,
+        [((TOK, 4 * DIM), BF16)] * 2,
+        [pltpu.VMEM((8, TOK, DIM), F32)],
+        name="finish",
+    )(offsets, *own_parts, *cross_parts)
+    return (query_grad, *key_value_grads)
 
 
 def solution(mesh):

time: 117 us -> 112 us (0.957)
  the two profiles are of different devices: /device:TPU:32 before, /device:TPU:166 now
where the time goes in v3:
time: 112 us; the launch traced here: 111 us
  starting transfers between devices  55.2 us (49%)
  waiting for transfers between devices  36.2 us (32%)
  Pallas kernels  17.9 us (16%)
    ppermute x12, starting transfers between devices, exchange(): return lax.ppermute(part, 'ctx', route)  36.3 us
    ppermute x12, waiting for transfers between devices, exchange(): return lax.ppermute(part, 'ctx', route)  19.6 us
    pallas_call x10, Pallas kernels, run(): pl.pallas_call(kernel, out_shape=[jax.ShapeDtypeStruct(shape, dtype) for...  17.9 us
    ppermute x6, starting transfers between devices, to_blocks(): return lax.ppermute(part, 'ctx', route)  17 us
    ppermute x6, waiting for transfers between devices, to_blocks(): return lax.ppermute(part, 'ctx', route)  15.4 us
  transfers between devices with their start and end apart: 21, of which 6 were waited for; matrix products, arithmetic and copies ran while one was open for 0% of the time, Pallas kernels for 11%

profile of v3, /device:TPU:166, one launch (start us, length us, event | category | flops | bytes accessed | tf_op | source)
XLA Modules:
  0.0 111.2 jit_solution(12753201631200626521)
XLA Ops:
  0.6 1.8 %pack.1 = (bf16[768,128]{1,0:T(8,128)(2,1)S(1)}, bf16[768,128]{1,0:T(8,128)(2,1)S(1)}, bf16[768,128]{1,0:T(8,128)(2,1)S(1)}, bf16[768,128]{1,0:T(8,128)(2,1)S(1)}) custom-call(bf16[256,512]{1,0:T(8,128)(2,1)} %q.1, bf16[256,512]{1,0:T(8,128)(2,1)} %k.1, bf16[256,512]{1,0:T(8,128)(2,1)} %v.1), custom_call_target="tpu_custom_call" | custom-call | flops 200000000 | bytes 2097152 | tf_op jit(solution)/shard_map/pack/pallas_call | solution.py:70
  2.6 1.7 %collective-permute-start.4 = (bf16[256,1024]{1,0:T(8,128)(2,1)}, bf16[256,1024]{1,0:T(8,128)(2,1)S(1)}, u32[]{:S(2)}, u32[]{:S(2)}) collective-permute-start(bf16[256,1024]{1,0:T(8,128)(2,1)} %g0.1), channel_id=1, source_target_pairs={{0,2},{1,3},{2,0},{3,1},{4,6},{5,7},{6,4},{7,5},{8,10},{9,11},{10,... | collective-permute-start | bytes 1572872 | tf_op jit(solution)/shard_map/ppermute | solution.py:428
  4.3 0.6 collective-permute-start.2
  5.3 4.6 %collective-permute-start = (bf16[768,128]{1,0:T(8,128)(2,1)S(1)}, bf16[768,128]{1,0:T(8,128)(2,1)S(1)}, u32[]{:S(2)}, u32[]{:S(2)}) collective-permute-start(bf16[768,128]{1,0:T(8,128)(2,1)S(1)} %get-tuple-element.48), channel_id=1, source_target_pairs={{8,12},{12,16},{16,20},{20,8},{24,28},{28,32},{32,36},{36,24},{40,... | collective-permute-start | bytes 589832 | tf_op jit(solution)/shard_map/ppermute | solution.py:415
  9.8 1.0 copy-done
  10.9 2.2 %grad_near.1 = (f32[256,512]{1,0:T(8,128)S(1)}, bf16[2,512,1024]{2,1,0:T(8,128)(2,1)S(1)}) custom-call(bf16[256,1024]{1,0:T(8,128)(2,1)S(1)} %copy-done, bf16[256,1024]{1,0:T(8,128)(2,1)S(1)} %collective-permute-done.1.g1, bf16[512,4096]{1,0:T(8,128)(2,1)} %w.1), custom_call_target="tpu_custom_call" | custom-call | tf_op jit(solution)/shard_map/grad_near/pallas_call | solution.py:70
  13.1 9.1 %collective-permute-done.2.p2 = bf16[768,128]{1,0:T(8,128)(2,1)S(1)} collective-permute-done((bf16[768,128]{1,0:T(8,128)(2,1)S(1)}, bf16[768,128]{1,0:T(8,128)(2,1)S(1)}, u32[]{:S(2)}, u32[]{:S(2)}) %collective-permute-start.2) | collective-permute-done | bytes 196640 | tf_op jit(solution)/shard_map/ppermute | solution.py:415
  22.4 0.7 gather.1
  23.1 1.2 %collective-permute-done.5.g3 = bf16[256,1024]{1,0:T(8,128)(2,1)S(1)} collective-permute-done((bf16[256,1024]{1,0:T(8,128)(2,1)S(1)}, bf16[256,1024]{1,0:T(8,128)(2,1)S(1)}, u32[]{:S(2)}, u32[]{:S(2)}) %collective-permute-start.5) | collective-permute-done | bytes 524320 | tf_op jit(solution)/shard_map/ppermute | solution.py:428
  24.3 1.0 grad_far.1
  25.3 5.4 %collective-permute-start.6 = (bf16[1536,128]{1,0:T(8,128)(2,1)S(1)}, bf16[1536,128]{1,0:T(8,128)(2,1)S(1)}, u32[]{:S(2)}, u32[]{:S(2)}) collective-permute-start(bf16[1536,128]{1,0:T(8,128)(2,1)S(1)} %get-tuple-element.63.both), channel_id=1, source_target_pairs={{8,36},{12,32},{16,28},{20,24},{40,68},{44,64},{48,60},{52,56},{72... | collective-permute-start | bytes 1179656 | tf_op jit(solution)/shard_map/ppermute | solution.py:425
  30.7 4.9 %collective-permute-start.10 = (bf16[256,128]{1,0:T(8,128)(2,1)S(1)}, bf16[256,128]{1,0:T(8,128)(2,1)S(1)}, u32[]{:S(2)}, u32[]{:S(2)}) collective-permute-start(bf16[256,128]{1,0:T(8,128)(2,1)S(1)} %get-tuple-element.69), channel_id=1, source_target_pairs={{8,16},{12,20},{16,8},{20,12},{24,32},{28,36},{32,24},{36,28},{40,... | collective-permute-start | bytes 196616 | tf_op jit(solution)/shard_map/ppermute | solution.py:415
  35.6 6.5 %collective-permute-start.8 = (bf16[512,128]{1,0:T(8,128)(2,1)S(1)}, bf16[512,128]{1,0:T(8,128)(2,1)S(1)}, u32[]{:S(2)}, u32[]{:S(2)}) collective-permute-start(bf16[512,128]{1,0:T(8,128)(2,1)S(1)} %get-tuple-element.65), channel_id=1, source_target_pairs={{8,40},{12,44},{16,48},{20,52},{24,56},{28,60},{32,64},{36,68},{72... | collective-permute-start | bytes 393224 | tf_op jit(solution)/shard_map/ppermute | solution.py:425
  42.0 1.3 %collective-permute-start.7 = (bf16[512,128]{1,0:T(8,128)(2,1)S(1)}, bf16[512,128]{1,0:T(8,128)(2,1)S(1)}, u32[]{:S(2)}, u32[]{:S(2)}) collective-permute-start(bf16[512,128]{1,0:T(8,128)(2,1)S(1)} %get-tuple-element.65), channel_id=1, source_target_pairs={{24,52},{28,48},{32,44},{36,40},{8,68},{12,64},{16,60},{20,56},{88... | collective-permute-start | bytes 393224 | tf_op jit(solution)/shard_map/ppermute | solution.py:425
  43.3 4.3 %collective-permute-start.9 = (bf16[256,128]{1,0:T(8,128)(2,1)S(1)}, bf16[256,128]{1,0:T(8,128)(2,1)S(1)}, u32[]{:S(2)}, u32[]{:S(2)}) collective-permute-start(bf16[256,128]{1,0:T(8,128)(2,1)S(1)} %get-tuple-element.62), channel_id=1, source_target_pairs={{8,12},{12,16},{16,20},{20,8},{24,28},{28,32},{32,36},{36,24},{40,... | collective-permute-start | bytes 196616 | tf_op jit(solution)/shard_map/ppermute | solution.py:415
  47.7 3.4 %own_forward.1 = (bf16[1024,1024]{1,0:T(8,128)(2,1)S(1)}, bf16[512,512]{1,0:T(8,128)(2,1)S(1)}, bf16[256,256]{1,0:T(8,128)(2,1)S(1)}, f32[1024,128]{1,0:T(8,128)S(1)}, f32[1024,256]{1,0:T(8,128)S(1)}) custom-call(s32[4,3]{1,0:T(4,128)S(1)} %copy-done.1, bf16[1024,128]{1,0:T(8,128)(2,1)S(1)} %get-tuple-element.54.qa, ...), custom_call_target="tpu_custom_call" | custom-call | flops 1000000000 | bytes 6291456 | tf_op jit(solution)/shard_map/own_forward/pallas_call | solution.py:70
  51.1 3.8 %collective-permute-done.11.p3 = bf16[256,128]{1,0:T(8,128)(2,1)S(1)} collective-permute-done((bf16[256,128]{1,0:T(8,128)(2,1)S(1)}, bf16[256,128]{1,0:T(8,128)(2,1)S(1)}, u32[]{:S(2)}, u32[]{:S(2)}) %collective-permute-start.11) | collective-permute-done | bytes 65568 | tf_op jit(solution)/shard_map/ppermute | solution.py:415
  55.0 1.3 %cross.1 = (bf16[1024,128]{1,0:T(8,128)(2,1)S(1)}, f32[1024,128]{1,0:T(8,128)S(1)}, f32[1024,128]{1,0:T(8,128)S(1)}, f32[1024,128]{1,0:T(8,128)S(1)}, bf16[1536,...) custom-call(s32[4,3]{1,0:T(4,128)S(1)} %copy-done.1, ...), custom_call_target="tpu_custom_call" | custom-call | flops 1000000000 | bytes 6291456 | tf_op jit(solution)/shard_map/cross/pallas_call | solution.py:70
  56.2 1.3 %collective-permute-start.17 = (bf16[1536,128]{1,0:T(8,128)(2,1)S(1)}, bf16[1536,128]{1,0:T(8,128)(2,1)S(1)}, u32[]{:S(2)}, u32[]{:S(2)}) collective-permute-start(bf16[1536,128]{1,0:T(8,128)(2,1)S(1)} %get-tuple-element.82), channel_id=1, source_target_pairs={{36,8},{32,12},{28,16},{24,20},{68,40},{64,44},{60,48},{56,52},{10... | collective-permute-start | bytes 1179656 | tf_op jit(solution)/shard_map/ppermute | solution.py:425
  57.5 1.3 %collective-permute-start.14 = (bf16[512,128]{1,0:T(8,128)(2,1)S(1)}, bf16[512,128]{1,0:T(8,128)(2,1)S(1)}, u32[]{:S(2)}, u32[]{:S(2)}) collective-permute-start(bf16[512,128]{1,0:T(8,128)(2,1)S(1)} %get-tuple-element.79), channel_id=1, source_target_pairs={{52,24},{48,28},{44,32},{40,36},{68,8},{64,12},{60,16},{56,20},{11... | collective-permute-start | bytes 393224 | tf_op jit(solution)/shard_map/ppermute | solution.py:425
  58.9 1.3 %collective-permute-start.15 = (bf16[512,128]{1,0:T(8,128)(2,1)S(1)}, bf16[512,128]{1,0:T(8,128)(2,1)S(1)}, u32[]{:S(2)}, u32[]{:S(2)}) collective-permute-start(bf16[512,128]{1,0:T(8,128)(2,1)S(1)} %get-tuple-element.80), channel_id=1, source_target_pairs={{40,8},{44,12},{48,16},{52,20},{56,24},{60,28},{64,32},{68,36},{10... | collective-permute-start | bytes 393224 | tf_op jit(solution)/shard_map/ppermute | solution.py:425
  60.1 4.5 %own_backward.1 = (bf16[768,128]{1,0:T(8,128)(2,1)S(1)}, bf16[768,128]{1,0:T(8,128)(2,1)S(1)}, bf16[768,128]{1,0:T(8,128)(2,1)S(1)}, bf16[768,128]{1,0:T(8,128)(2,1)S(1)}) custom-call(s32[4,3]{1,0:T(4,128)S(1)} %copy-done.1, bf16[1024,1024]{1,0:T(8,128)(2,1)S(1)} %get-tuple-element.57.e0, bf16[512,512]{1,0:T(8,128)(2,1)S(1)} %get-tuple-element.58.e1, ...), custom_call_target="tpu_custom_call" | custom-call | flops 2000000000 | bytes 8388608 | tf_op jit(solution)/shard_map/own_backward/pallas_call | solution.py:70
  64.7 1.3 %collective-permute-start.12 = (bf16[768,128]{1,0:T(8,128)(2,1)S(1)}, bf16[768,128]{1,0:T(8,128)(2,1)S(1)}, u32[]{:S(2)}, u32[]{:S(2)}) collective-permute-start(bf16[768,128]{1,0:T(8,128)(2,1)S(1)} %get-tuple-element.76), channel_id=1, source_target_pairs={{8,12},{12,16},{16,20},{20,8},{24,28},{28,32},{32,36},{36,24},{40,... | collective-permute-start | bytes 589832 | tf_op jit(solution)/shard_map/ppermute | solution.py:415
  66.0 15.4 %collective-permute-done.14.yb = bf16[512,128]{1,0:T(8,128)(2,1)S(1)} collective-permute-done((bf16[512,128]{1,0:T(8,128)(2,1)S(1)}, bf16[512,128]{1,0:T(8,128)(2,1)S(1)}, u32[]{:S(2)}, u32[]{:S(2)}) %collective-permute-start.14) | collective-permute-done | bytes 131104 | tf_op jit(solution)/shard_map/ppermute | solution.py:425
  81.4 11.8 %collective-permute-start.16 = (bf16[768,128]{1,0:T(8,128)(2,1)S(1)}, bf16[768,128]{1,0:T(8,128)(2,1)S(1)}, u32[]{:S(2)}, u32[]{:S(2)}) collective-permute-start(bf16[768,128]{1,0:T(8,128)(2,1)S(1)} %get-tuple-element.81), channel_id=1, source_target_pairs={{8,20},{12,8},{16,12},{20,16},{24,36},{28,24},{32,28},{36,32},{40,... | collective-permute-start | bytes 589832 | tf_op jit(solution)/shard_map/ppermute | solution.py:415
  93.3 1.9 %collective-permute-start.18 = (bf16[384,128]{1,0:T(8,128)(2,1)S(1)}, bf16[384,128]{1,0:T(8,128)(2,1)S(1)}, u32[]{:S(2)}, u32[]{:S(2)}) collective-permute-start(bf16[384,128]{1,0:T(8,128)(2,1)S(1)} %get-tuple-element.85), channel_id=1, source_target_pairs={{8,12},{12,16},{16,20},{20,8},{24,28},{28,32},{32,36},{36,24},{40,... | collective-permute-start | bytes 294920 | tf_op jit(solution)/shard_map/ppermute | solution.py:415
  95.2 4.6 %collective-permute-start.19 = (bf16[384,128]{1,0:T(8,128)(2,1)S(1)}, bf16[384,128]{1,0:T(8,128)(2,1)S(1)}, u32[]{:S(2)}, u32[]{:S(2)}) collective-permute-start(bf16[384,128]{1,0:T(8,128)(2,1)S(1)} %get-tuple-element.87), channel_id=1, source_target_pairs={{8,16},{12,20},{16,8},{20,12},{24,32},{28,36},{32,24},{36,28},{40,... | collective-permute-start | bytes 294920 | tf_op jit(solution)/shard_map/ppermute | solution.py:415
  99.8 1.9 %collective-permute-start.20 = (bf16[384,128]{1,0:T(8,128)(2,1)S(1)}, bf16[384,128]{1,0:T(8,128)(2,1)S(1)}, u32[]{:S(2)}, u32[]{:S(2)}) collective-permute-start(bf16[384,128]{1,0:T(8,128)(2,1)S(1)} %get-tuple-element.88), channel_id=1, source_target_pairs={{8,20},{12,8},{16,12},{20,16},{24,36},{28,24},{32,28},{36,32},{40,... | collective-permute-start | bytes 294920 | tf_op jit(solution)/shard_map/ppermute | solution.py:415
  101.8 1.0 finish_query.1
  102.8 3.2 %collective-permute-done.19.c2 = bf16[384,128]{1,0:T(8,128)(2,1)S(1)} collective-permute-done((bf16[384,128]{1,0:T(8,128)(2,1)S(1)}, bf16[384,128]{1,0:T(8,128)(2,1)S(1)}, u32[]{:S(2)}, u32[]{:S(2)}) %collective-permute-start.19) | collective-permute-done | bytes 98336 | tf_op jit(solution)/shard_map/ppermute | solution.py:415
  106.0 3.4 %collective-permute-done.20.c3 = bf16[384,128]{1,0:T(8,128)(2,1)S(1)} collective-permute-done((bf16[384,128]{1,0:T(8,128)(2,1)S(1)}, bf16[384,128]{1,0:T(8,128)(2,1)S(1)}, u32[]{:S(2)}, u32[]{:S(2)}) %collective-permute-start.20) | collective-permute-done | bytes 98336 | tf_op jit(solution)/shard_map/ppermute | solution.py:415
  109.3 1.9 %finish.1 = (bf16[256,512]{1,0:T(8,128)(2,1)}, bf16[256,512]{1,0:T(8,128)(2,1)}) custom-call(s32[4,3]{1,0:T(4,128)S(1)} %copy-done.1, bf16[768,128]{1,0:T(8,128)(2,1)S(1)} %get-tuple-element.75.p0, bf16[768,128]{1,0:T(8,128)(2,1)S(1)} %collective-permute-done.12.p1, bf16[768,128]{1,0:T(8,128)(2,1)S(1)} %collective-permute-done.13.p2, ...), custom_call_target="tpu_custom_call" | custom-call | tf_op jit(solution)/shard_map/finish/pallas_call | solution.py:70
  (24 shorter events, 0.8 us)
Async XLA Ops:
  2.5 7.4 %collective-permute-start.1 = (bf16[256,1024]{1,0:T(8,128)(2,1)}, bf16[256,1024]{1,0:T(8,128)(2,1)S(1)}, u32[]{:S(2)}, u32[]{:S(2)}) collective-permute-start(bf16[256,1024]{1,0:T(8,128)(2,1)} %g0.1), channel_id=1, source_target_pairs={{0,1},{1,0},{2,3},{3,2},{4,5},{5,4},{6,7},{7,6},{8,9},{9,8},{10,11... | collective-permute-start | bytes 1572872 | tf_op jit(solution)/shard_map/ppermute | solution.py:428
  2.6 19.7 %collective-permute-start.4 = (bf16[256,1024]{1,0:T(8,128)(2,1)}, bf16[256,1024]{1,0:T(8,128)(2,1)S(1)}, u32[]{:S(2)}, u32[]{:S(2)}) collective-permute-start(bf16[256,1024]{1,0:T(8,128)(2,1)} %g0.1), channel_id=1, source_target_pairs={{0,2},{1,3},{2,0},{3,1},{4,6},{5,7},{6,4},{7,5},{8,10},{9,11},{10,... | collective-permute-start | bytes 1572872 | tf_op jit(solution)/shard_map/ppermute | solution.py:428
  4.3 18.0 %collective-permute-start.2 = (bf16[768,128]{1,0:T(8,128)(2,1)S(1)}, bf16[768,128]{1,0:T(8,128)(2,1)S(1)}, u32[]{:S(2)}, u32[]{:S(2)}) collective-permute-start(bf16[768,128]{1,0:T(8,128)(2,1)S(1)} %get-tuple-element.52), channel_id=1, source_target_pairs={{8,16},{12,20},{16,8},{20,12},{24,32},{28,36},{32,24},{36,28},{40,... | collective-permute-start | bytes 589832 | tf_op jit(solution)/shard_map/ppermute | solution.py:415
  4.8 17.5 %collective-permute-start.3 = (bf16[768,128]{1,0:T(8,128)(2,1)S(1)}, bf16[768,128]{1,0:T(8,128)(2,1)S(1)}, u32[]{:S(2)}, u32[]{:S(2)}) collective-permute-start(bf16[768,128]{1,0:T(8,128)(2,1)S(1)} %get-tuple-element.53), channel_id=1, source_target_pairs={{8,20},{12,8},{16,12},{20,16},{24,36},{28,24},{32,28},{36,32},{40,... | collective-permute-start | bytes 589832 | tf_op jit(solution)/shard_map/ppermute | solution.py:415
  5.3 17.0 %collective-permute-start = (bf16[768,128]{1,0:T(8,128)(2,1)S(1)}, bf16[768,128]{1,0:T(8,128)(2,1)S(1)}, u32[]{:S(2)}, u32[]{:S(2)}) collective-permute-start(bf16[768,128]{1,0:T(8,128)(2,1)S(1)} %get-tuple-element.48), channel_id=1, source_target_pairs={{8,12},{12,16},{16,20},{20,8},{24,28},{28,32},{32,36},{36,24},{40,... | collective-permute-start | bytes 589832 | tf_op jit(solution)/shard_map/ppermute | solution.py:415
  9.8 1.0 copy-start
  10.9 11.5 %copy-start.1 = (s32[4,3]{1,0:T(4,128)S(1)}, s32[4,3]{1,0:T(4,128)}, u32[]{:S(2)}) copy-start(s32[4,3]{1,0:T(4,128)} %offsets.9) | copy-start | bytes 148
  22.3 2.0 %collective-permute-start.5 = (bf16[256,1024]{1,0:T(8,128)(2,1)S(1)}, bf16[256,1024]{1,0:T(8,128)(2,1)S(1)}, u32[]{:S(2)}, u32[]{:S(2)}) collective-permute-start(bf16[256,1024]{1,0:T(8,128)(2,1)S(1)} %collective-permute-done.4.g2), channel_id=1, source_target_pairs={{0,1},{1,0},{2,3},{3,2},{4,5},{5,4},{6,7},{7,6},{8,9},{9,8},{10,11... | collective-permute-start | bytes 1572872 | tf_op jit(solution)/shard_map/ppermute | solution.py:428
  25.3 29.7 %collective-permute-start.6 = (bf16[1536,128]{1,0:T(8,128)(2,1)S(1)}, bf16[1536,128]{1,0:T(8,128)(2,1)S(1)}, u32[]{:S(2)}, u32[]{:S(2)}) collective-permute-start(bf16[1536,128]{1,0:T(8,128)(2,1)S(1)} %get-tuple-element.63.both), channel_id=1, source_target_pairs={{8,36},{12,32},{16,28},{20,24},{40,68},{44,64},{48,60},{52,56},{72... | collective-permute-start | bytes 1179656 | tf_op jit(solution)/shard_map/ppermute | solution.py:425
  30.7 17.0 %collective-permute-start.10 = (bf16[256,128]{1,0:T(8,128)(2,1)S(1)}, bf16[256,128]{1,0:T(8,128)(2,1)S(1)}, u32[]{:S(2)}, u32[]{:S(2)}) collective-permute-start(bf16[256,128]{1,0:T(8,128)(2,1)S(1)} %get-tuple-element.69), channel_id=1, source_target_pairs={{8,16},{12,20},{16,8},{20,12},{24,32},{28,36},{32,24},{36,28},{40,... | collective-permute-start | bytes 196616 | tf_op jit(solution)/shard_map/ppermute | solution.py:415
  35.6 19.4 %collective-permute-start.8 = (bf16[512,128]{1,0:T(8,128)(2,1)S(1)}, bf16[512,128]{1,0:T(8,128)(2,1)S(1)}, u32[]{:S(2)}, u32[]{:S(2)}) collective-permute-start(bf16[512,128]{1,0:T(8,128)(2,1)S(1)} %get-tuple-element.65), channel_id=1, source_target_pairs={{8,40},{12,44},{16,48},{20,52},{24,56},{28,60},{32,64},{36,68},{72... | collective-permute-start | bytes 393224 | tf_op jit(solution)/shard_map/ppermute | solution.py:425
  42.0 12.9 %collective-permute-start.7 = (bf16[512,128]{1,0:T(8,128)(2,1)S(1)}, bf16[512,128]{1,0:T(8,128)(2,1)S(1)}, u32[]{:S(2)}, u32[]{:S(2)}) collective-permute-start(bf16[512,128]{1,0:T(8,128)(2,1)S(1)} %get-tuple-element.65), channel_id=1, source_target_pairs={{24,52},{28,48},{32,44},{36,40},{8,68},{12,64},{16,60},{20,56},{88... | collective-permute-start | bytes 393224 | tf_op jit(solution)/shard_map/ppermute | solution.py:425
  43.3 11.6 %collective-permute-start.9 = (bf16[256,128]{1,0:T(8,128)(2,1)S(1)}, bf16[256,128]{1,0:T(8,128)(2,1)S(1)}, u32[]{:S(2)}, u32[]{:S(2)}) collective-permute-start(bf16[256,128]{1,0:T(8,128)(2,1)S(1)} %get-tuple-element.62), channel_id=1, source_target_pairs={{8,12},{12,16},{16,20},{20,8},{24,28},{28,32},{32,36},{36,24},{40,... | collective-permute-start | bytes 196616 | tf_op jit(solution)/shard_map/ppermute | solution.py:415
  47.7 7.3 %collective-permute-start.11 = (bf16[256,128]{1,0:T(8,128)(2,1)S(1)}, bf16[256,128]{1,0:T(8,128)(2,1)S(1)}, u32[]{:S(2)}, u32[]{:S(2)}) collective-permute-start(bf16[256,128]{1,0:T(8,128)(2,1)S(1)} %get-tuple-element.70), channel_id=1, source_target_pairs={{8,20},{12,8},{16,12},{20,16},{24,36},{28,24},{32,28},{36,32},{40,... | collective-permute-start | bytes 196616 | tf_op jit(solution)/shard_map/ppermute | solution.py:415
  56.2 37.0 %collective-permute-start.17 = (bf16[1536,128]{1,0:T(8,128)(2,1)S(1)}, bf16[1536,128]{1,0:T(8,128)(2,1)S(1)}, u32[]{:S(2)}, u32[]{:S(2)}) collective-permute-start(bf16[1536,128]{1,0:T(8,128)(2,1)S(1)} %get-tuple-element.82), channel_id=1, source_target_pairs={{36,8},{32,12},{28,16},{24,20},{68,40},{64,44},{60,48},{56,52},{10... | collective-permute-start | bytes 1179656 | tf_op jit(solution)/shard_map/ppermute | solution.py:425
  57.5 23.9 %collective-permute-start.14 = (bf16[512,128]{1,0:T(8,128)(2,1)S(1)}, bf16[512,128]{1,0:T(8,128)(2,1)S(1)}, u32[]{:S(2)}, u32[]{:S(2)}) collective-permute-start(bf16[512,128]{1,0:T(8,128)(2,1)S(1)} %get-tuple-element.79), channel_id=1, source_target_pairs={{52,24},{48,28},{44,32},{40,36},{68,8},{64,12},{60,16},{56,20},{11... | collective-permute-start | bytes 393224 | tf_op jit(solution)/shard_map/ppermute | solution.py:425
  58.9 22.6 %collective-permute-start.15 = (bf16[512,128]{1,0:T(8,128)(2,1)S(1)}, bf16[512,128]{1,0:T(8,128)(2,1)S(1)}, u32[]{:S(2)}, u32[]{:S(2)}) collective-permute-start(bf16[512,128]{1,0:T(8,128)(2,1)S(1)} %get-tuple-element.80), channel_id=1, source_target_pairs={{40,8},{44,12},{48,16},{52,20},{56,24},{60,28},{64,32},{68,36},{10... | collective-permute-start | bytes 393224 | tf_op jit(solution)/shard_map/ppermute | solution.py:425
  64.7 28.5 %collective-permute-start.12 = (bf16[768,128]{1,0:T(8,128)(2,1)S(1)}, bf16[768,128]{1,0:T(8,128)(2,1)S(1)}, u32[]{:S(2)}, u32[]{:S(2)}) collective-permute-start(bf16[768,128]{1,0:T(8,128)(2,1)S(1)} %get-tuple-element.76), channel_id=1, source_target_pairs={{8,12},{12,16},{16,20},{20,8},{24,28},{28,32},{32,36},{36,24},{40,... | collective-permute-start | bytes 589832 | tf_op jit(solution)/shard_map/ppermute | solution.py:415
  66.0 27.2 %collective-permute-start.13 = (bf16[768,128]{1,0:T(8,128)(2,1)S(1)}, bf16[768,128]{1,0:T(8,128)(2,1)S(1)}, u32[]{:S(2)}, u32[]{:S(2)}) collective-permute-start(bf16[768,128]{1,0:T(8,128)(2,1)S(1)} %get-tuple-element.77), channel_id=1, source_target_pairs={{8,16},{12,20},{16,8},{20,12},{24,32},{28,36},{32,24},{36,28},{40,... | collective-permute-start | bytes 589832 | tf_op jit(solution)/shard_map/ppermute | solution.py:415
  81.4 20.3 %collective-permute-start.16 = (bf16[768,128]{1,0:T(8,128)(2,1)S(1)}, bf16[768,128]{1,0:T(8,128)(2,1)S(1)}, u32[]{:S(2)}, u32[]{:S(2)}) collective-permute-start(bf16[768,128]{1,0:T(8,128)(2,1)S(1)} %get-tuple-element.81), channel_id=1, source_target_pairs={{8,20},{12,8},{16,12},{20,16},{24,36},{28,24},{32,28},{36,32},{40,... | collective-permute-start | bytes 589832 | tf_op jit(solution)/shard_map/ppermute | solution.py:415
  93.3 9.5 %collective-permute-start.18 = (bf16[384,128]{1,0:T(8,128)(2,1)S(1)}, bf16[384,128]{1,0:T(8,128)(2,1)S(1)}, u32[]{:S(2)}, u32[]{:S(2)}) collective-permute-start(bf16[384,128]{1,0:T(8,128)(2,1)S(1)} %get-tuple-element.85), channel_id=1, source_target_pairs={{8,12},{12,16},{16,20},{20,8},{24,28},{28,32},{32,36},{36,24},{40,... | collective-permute-start | bytes 294920 | tf_op jit(solution)/shard_map/ppermute | solution.py:415
  95.2 10.7 %collective-permute-start.19 = (bf16[384,128]{1,0:T(8,128)(2,1)S(1)}, bf16[384,128]{1,0:T(8,128)(2,1)S(1)}, u32[]{:S(2)}, u32[]{:S(2)}) collective-permute-start(bf16[384,128]{1,0:T(8,128)(2,1)S(1)} %get-tuple-element.87), channel_id=1, source_target_pairs={{8,16},{12,20},{16,8},{20,12},{24,32},{28,36},{32,24},{36,28},{40,... | collective-permute-start | bytes 294920 | tf_op jit(solution)/shard_map/ppermute | solution.py:415
  99.8 9.5 %collective-permute-start.20 = (bf16[384,128]{1,0:T(8,128)(2,1)S(1)}, bf16[384,128]{1,0:T(8,128)(2,1)S(1)}, u32[]{:S(2)}, u32[]{:S(2)}) collective-permute-start(bf16[384,128]{1,0:T(8,128)(2,1)S(1)} %get-tuple-element.88), channel_id=1, source_target_pairs={{8,20},{12,8},{16,12},{20,16},{24,36},{28,24},{32,28},{36,32},{40,... | collective-permute-start | bytes 294920 | tf_op jit(solution)/shard_map/ppermute | solution.py:415

commit v4 on v3

--- a/solution.py
+++ b/solution.py
@@ -61,7 +61,9 @@
     return jnp.broadcast_to(jnp.max(scores, axis=1, keepdims=True), (scores.shape[0], DIM))
 
 
-def call(kernel, outs, scratch=(), name=None, flops=0, bytes_accessed=0, far=()):
+def call(
+    kernel, outs, scratch=(), name=None, flops=0, bytes_accessed=0, far=(), outs_far=False
+):
     def run(*args):
         args = [
             pltpu.with_memory_space_constraint(arg, pltpu.HBM) if i in far else arg
@@ -80,7 +82,8 @@
                 )
                 for i, arg in enumerate(args)
             ],
-            out_specs=[pl.BlockSpec(memory_space=pltpu.VMEM)] * len(outs),
+            out_specs=[pl.BlockSpec(memory_space=pltpu.HBM if outs_far else pltpu.VMEM)]
+            * len(outs),
             scratch_shapes=list(scratch),
             compiler_params=pltpu.CompilerParams(vmem_limit_bytes=16 << 20),
             cost_estimate=pl.CostEstimate(
@@ -120,10 +123,10 @@
     sort = sort_matrix()
     for i, copy in enumerate(copies):
         copy.wait()
+        held[i] = dot_nn(sort, held[i]).astype(BF16)
         for s, target in enumerate((o0, o1, o2, o3)):
-            head = head_at((place + s) & 3, block)
             rows = held.at[i]
-            target[i * TOK : (i + 1) * TOK] = dot_nn(sort, rows[:, cols_at(head)]).astype(BF16)
+            target[i * TOK : (i + 1) * TOK] = rows[:, cols_at(head_at((place + s) & 3, block))]
 
 
 def gather_kernel(offsets, p0, p1, p2, p3, qa, kv, both, kv2):
@@ -375,29 +378,36 @@
             ).astype(BF16)
 
 
-def finish_query_kernel(p0, p1, p2, p3, dq):
+def finish_own_kernel(p0, p1, p2, p3, dq, dk, dv, held):
+    place, block = place_and_block()
+    for s, piece in enumerate((p0, p1, p2, p3)):
+        cols = cols_at(head_at((place - s) & 3, block))
+        dk[:, cols] = piece[:TOK].astype(F32)
+        dv[:, cols] = piece[TOK : 2 * TOK].astype(F32)
+        held[:, cols] = piece[2 * TOK :]
+    dq[...] = dot_nn(unsort_matrix(), held[...]).astype(BF16)
+
+
+def finish_kernel(offsets, in_k, in_v, c0, c1, c2, c3, dk, dv, total, low_k, low_v, sem):
     place, block = place_and_block()
     unsort = unsort_matrix()
-    for s, piece in enumerate((p0, p1, p2, p3)):
-        cols = cols_at(head_at((place - s) & 3, block))
-        dq[:, cols] = dot_nn(unsort, piece[2 * TOK :]).astype(BF16)
-
-
-def finish_kernel(offsets, p0, p1, p2, p3, c0, c1, c2, c3, dk, dv, total):
-    place, block = place_and_block()
-    unsort = unsort_matrix()
-    for s, (piece, cross) in enumerate(((p0, c0), (p1, c1), (p2, c2), (p3, c3))):
-        head = head_at((place - s) & 3, block)
-        off1, off2 = offsets[head, 1], offsets[head, 2]
-        group2 = ((off2 & 1) << 1) | (off2 >> 1)
-        cols = cols_at(head)
-        for part, out in enumerate((dk, dv)):
-            both = total.at[2 * s + part]
-            both[...] = piece[part * TOK : (part + 1) * TOK].astype(F32)
+    copies = []
+    for part, (own, low, out) in enumerate(((in_k, low_k, dk), (in_v, low_v, dv))):
+        total[part] = own[...]
+        for s, cross in enumerate((c0, c1, c2, c3)):
+            head = head_at((place - s) & 3, block)
+            off1, off2 = offsets[head, 1], offsets[head, 2]
+            group2 = ((off2 & 1) << 1) | (off2 >> 1)
+            cols = cols_at(head)
             rows1, rows2 = rows_at(off1 * 128, 128), rows_at(group2 * 64, 64)
-            both[rows1] += cross[part * 128 : (part + 1) * 128].astype(F32)
-            both[rows2] += cross[256 + part * 64 : 256 + (part + 1) * 64].astype(F32)
-            out[:, cols] = dot_nn(unsort, both[...].astype(BF16)).astype(BF16)
+            sums = total.at[part]
+            sums[rows1, cols] += cross[part * 128 : (part + 1) * 128].astype(F32)
+            sums[rows2, cols] += cross[256 + part * 64 : 256 + (part + 1) * 64].astype(F32)
+        low[...] = dot_nn(unsort, total[part].astype(BF16)).astype(BF16)
+        copies.append(pltpu.make_async_copy(low, out, sem.at[part]))
+        copies[part].start()
+    for copy in copies:
+        copy.wait()
 
 
 def local(queries, keys, values, out_grad, w_out, offsets):
@@ -559,16 +569,28 @@
     cross_parts = [cross_parts[0]] + [
         exchange(cross_parts[s], s, (0, 1, 2)) for s in (1, 2, 3)
     ]
-    query_grad = call(finish_query_kernel, [((TOK, 4 * DIM), BF16)], name="finish_query")(
-        *own_parts
-    )[0]
+    wide = (TOK, 4 * DIM)
+    query_grad, own_k, own_v = call(
+        finish_own_kernel,
+        [(wide, BF16), (wide, F32), (wide, F32)],
+        [pltpu.VMEM(wide, BF16)],
+        name="finish_own",
+    )(*own_parts)
     cross_parts[1] = after(cross_parts[1], query_grad)
     key_value_grads = call(
         finish_kernel,
-        [((TOK, 4 * DIM), BF16)] * 2,
-        [pltpu.VMEM((8, TOK, DIM), F32)],
+        [(wide, BF16)] * 2,
+        [
+            pltpu.VMEM((2, *wide), F32),
+            pltpu.VMEM(wide, BF16),
+            pltpu.VMEM(wide, BF16),
+            pltpu.SemaphoreType.DMA((2,)),
+        ],
         name="finish",
-    )(offsets, *own_parts, *cross_parts)
+        outs_far=True,
+    )(
+        offsets, own_k, own_v, *cross_parts
+    )
     return (query_grad, *key_value_grads)
 
 

time: 112 us -> 112 us (level)
  no operation moved by 1% of the time
where the time goes in v4:
time: 112 us; the launch traced here: 111 us
  starting transfers between devices  55.2 us (49%)
  waiting for transfers between devices  36.1 us (32%)
  Pallas kernels  18 us (16%)
    ppermute x12, starting transfers between devices, exchange(): return lax.ppermute(part, 'ctx', route)  36.3 us
    ppermute x12, waiting for transfers between devices, exchange(): return lax.ppermute(part, 'ctx', route)  19.4 us
    pallas_call x10, Pallas kernels, run(): pl.pallas_call(kernel, out_shape=[jax.ShapeDtypeStruct(shape, dtype) for...  18 us
    ppermute x6, starting transfers between devices, to_blocks(): return lax.ppermute(part, 'ctx', route)  17 us
    ppermute x6, waiting for transfers between devices, to_blocks(): return lax.ppermute(part, 'ctx', route)  15.4 us
  transfers between devices with their start and end apart: 21, of which 6 were waited for; matrix products, arithmetic and copies ran while one was open for 0% of the time, Pallas kernels for 11%

profile of v4, /device:TPU:166, one launch (start us, length us, event | category | flops | bytes accessed | tf_op | source)
XLA Modules:
  0.0 111.3 jit_solution(18198388539671630073)
XLA Ops:
  0.6 1.8 %pack.1 = (bf16[768,128]{1,0:T(8,128)(2,1)S(1)}, bf16[768,128]{1,0:T(8,128)(2,1)S(1)}, bf16[768,128]{1,0:T(8,128)(2,1)S(1)}, bf16[768,128]{1,0:T(8,128)(2,1)S(1)}) custom-call(bf16[256,512]{1,0:T(8,128)(2,1)} %q.1, bf16[256,512]{1,0:T(8,128)(2,1)} %k.1, bf16[256,512]{1,0:T(8,128)(2,1)} %v.1), custom_call_target="tpu_custom_call" | custom-call | flops 200000000 | bytes 2097152 | tf_op jit(solution)/shard_map/pack/pallas_call | solution.py:72
  2.6 1.7 %collective-permute-start.4 = (bf16[256,1024]{1,0:T(8,128)(2,1)}, bf16[256,1024]{1,0:T(8,128)(2,1)S(1)}, u32[]{:S(2)}, u32[]{:S(2)}) collective-permute-start(bf16[256,1024]{1,0:T(8,128)(2,1)} %g0.1), channel_id=1, source_target_pairs={{0,2},{1,3},{2,0},{3,1},{4,6},{5,7},{6,4},{7,5},{8,10},{9,11},{10,... | collective-permute-start | bytes 1572872 | tf_op jit(solution)/shard_map/ppermute | solution.py:438
  4.2 0.6 collective-permute-start.2
  5.3 4.6 %collective-permute-start = (bf16[768,128]{1,0:T(8,128)(2,1)S(1)}, bf16[768,128]{1,0:T(8,128)(2,1)S(1)}, u32[]{:S(2)}, u32[]{:S(2)}) collective-permute-start(bf16[768,128]{1,0:T(8,128)(2,1)S(1)} %get-tuple-element.51), channel_id=1, source_target_pairs={{8,12},{12,16},{16,20},{20,8},{24,28},{28,32},{32,36},{36,24},{40,... | collective-permute-start | bytes 589832 | tf_op jit(solution)/shard_map/ppermute | solution.py:425
  9.8 1.0 copy-done
  10.9 2.2 %grad_near.1 = (f32[256,512]{1,0:T(8,128)S(1)}, bf16[2,512,1024]{2,1,0:T(8,128)(2,1)S(1)}) custom-call(bf16[256,1024]{1,0:T(8,128)(2,1)S(1)} %copy-done, bf16[256,1024]{1,0:T(8,128)(2,1)S(1)} %collective-permute-done.1.g1, bf16[512,4096]{1,0:T(8,128)(2,1)} %w.1), custom_call_target="tpu_custom_call" | custom-call | tf_op jit(solution)/shard_map/grad_near/pallas_call | solution.py:72
  13.1 9.1 %collective-permute-done.2.p2 = bf16[768,128]{1,0:T(8,128)(2,1)S(1)} collective-permute-done((bf16[768,128]{1,0:T(8,128)(2,1)S(1)}, bf16[768,128]{1,0:T(8,128)(2,1)S(1)}, u32[]{:S(2)}, u32[]{:S(2)}) %collective-permute-start.2) | collective-permute-done | bytes 196640 | tf_op jit(solution)/shard_map/ppermute | solution.py:425
  22.4 0.7 gather.1
  23.1 1.2 %collective-permute-done.5.g3 = bf16[256,1024]{1,0:T(8,128)(2,1)S(1)} collective-permute-done((bf16[256,1024]{1,0:T(8,128)(2,1)S(1)}, bf16[256,1024]{1,0:T(8,128)(2,1)S(1)}, u32[]{:S(2)}, u32[]{:S(2)}) %collective-permute-start.5) | collective-permute-done | bytes 524320 | tf_op jit(solution)/shard_map/ppermute | solution.py:438
  24.3 1.0 grad_far.1
  25.3 5.4 %collective-permute-start.6 = (bf16[1536,128]{1,0:T(8,128)(2,1)S(1)}, bf16[1536,128]{1,0:T(8,128)(2,1)S(1)}, u32[]{:S(2)}, u32[]{:S(2)}) collective-permute-start(bf16[1536,128]{1,0:T(8,128)(2,1)S(1)} %get-tuple-element.66.both), channel_id=1, source_target_pairs={{8,36},{12,32},{16,28},{20,24},{40,68},{44,64},{48,60},{52,56},{72... | collective-permute-start | bytes 1179656 | tf_op jit(solution)/shard_map/ppermute | solution.py:435
  30.7 4.9 %collective-permute-start.10 = (bf16[256,128]{1,0:T(8,128)(2,1)S(1)}, bf16[256,128]{1,0:T(8,128)(2,1)S(1)}, u32[]{:S(2)}, u32[]{:S(2)}) collective-permute-start(bf16[256,128]{1,0:T(8,128)(2,1)S(1)} %get-tuple-element.72), channel_id=1, source_target_pairs={{8,16},{12,20},{16,8},{20,12},{24,32},{28,36},{32,24},{36,28},{40,... | collective-permute-start | bytes 196616 | tf_op jit(solution)/shard_map/ppermute | solution.py:425
  35.5 6.5 %collective-permute-start.8 = (bf16[512,128]{1,0:T(8,128)(2,1)S(1)}, bf16[512,128]{1,0:T(8,128)(2,1)S(1)}, u32[]{:S(2)}, u32[]{:S(2)}) collective-permute-start(bf16[512,128]{1,0:T(8,128)(2,1)S(1)} %get-tuple-element.68), channel_id=1, source_target_pairs={{8,40},{12,44},{16,48},{20,52},{24,56},{28,60},{32,64},{36,68},{72... | collective-permute-start | bytes 393224 | tf_op jit(solution)/shard_map/ppermute | solution.py:435
  42.0 1.3 %collective-permute-start.7 = (bf16[512,128]{1,0:T(8,128)(2,1)S(1)}, bf16[512,128]{1,0:T(8,128)(2,1)S(1)}, u32[]{:S(2)}, u32[]{:S(2)}) collective-permute-start(bf16[512,128]{1,0:T(8,128)(2,1)S(1)} %get-tuple-element.68), channel_id=1, source_target_pairs={{24,52},{28,48},{32,44},{36,40},{8,68},{12,64},{16,60},{20,56},{88... | collective-permute-start | bytes 393224 | tf_op jit(solution)/shard_map/ppermute | solution.py:435
  43.3 4.3 %collective-permute-start.9 = (bf16[256,128]{1,0:T(8,128)(2,1)S(1)}, bf16[256,128]{1,0:T(8,128)(2,1)S(1)}, u32[]{:S(2)}, u32[]{:S(2)}) collective-permute-start(bf16[256,128]{1,0:T(8,128)(2,1)S(1)} %get-tuple-element.65), channel_id=1, source_target_pairs={{8,12},{12,16},{16,20},{20,8},{24,28},{28,32},{32,36},{36,24},{40,... | collective-permute-start | bytes 196616 | tf_op jit(solution)/shard_map/ppermute | solution.py:425
  47.7 3.4 %own_forward.1 = (bf16[1024,1024]{1,0:T(8,128)(2,1)S(1)}, bf16[512,512]{1,0:T(8,128)(2,1)S(1)}, bf16[256,256]{1,0:T(8,128)(2,1)S(1)}, f32[1024,128]{1,0:T(8,128)S(1)}, f32[1024,256]{1,0:T(8,128)S(1)}) custom-call(s32[4,3]{1,0:T(4,128)S(1)} %copy-done.1, bf16[1024,128]{1,0:T(8,128)(2,1)S(1)} %get-tuple-element.57.qa, ...), custom_call_target="tpu_custom_call" | custom-call | flops 1000000000 | bytes 6291456 | tf_op jit(solution)/shard_map/own_forward/pallas_call | solution.py:72
  51.1 3.8 %collective-permute-done.11.p3 = bf16[256,128]{1,0:T(8,128)(2,1)S(1)} collective-permute-done((bf16[256,128]{1,0:T(8,128)(2,1)S(1)}, bf16[256,128]{1,0:T(8,128)(2,1)S(1)}, u32[]{:S(2)}, u32[]{:S(2)}) %collective-permute-start.11) | collective-permute-done | bytes 65568 | tf_op jit(solution)/shard_map/ppermute | solution.py:425
  55.0 1.3 %cross.1 = (bf16[1024,128]{1,0:T(8,128)(2,1)S(1)}, f32[1024,128]{1,0:T(8,128)S(1)}, f32[1024,128]{1,0:T(8,128)S(1)}, f32[1024,128]{1,0:T(8,128)S(1)}, bf16[1536,...) custom-call(s32[4,3]{1,0:T(4,128)S(1)} %copy-done.1, ...), custom_call_target="tpu_custom_call" | custom-call | flops 1000000000 | bytes 6291456 | tf_op jit(solution)/shard_map/cross/pallas_call | solution.py:72
  56.2 1.3 %collective-permute-start.17 = (bf16[1536,128]{1,0:T(8,128)(2,1)S(1)}, bf16[1536,128]{1,0:T(8,128)(2,1)S(1)}, u32[]{:S(2)}, u32[]{:S(2)}) collective-permute-start(bf16[1536,128]{1,0:T(8,128)(2,1)S(1)} %get-tuple-element.88), channel_id=1, source_target_pairs={{36,8},{32,12},{28,16},{24,20},{68,40},{64,44},{60,48},{56,52},{10... | collective-permute-start | bytes 1179656 | tf_op jit(solution)/shard_map/ppermute | solution.py:435
  57.5 1.3 %collective-permute-start.14 = (bf16[512,128]{1,0:T(8,128)(2,1)S(1)}, bf16[512,128]{1,0:T(8,128)(2,1)S(1)}, u32[]{:S(2)}, u32[]{:S(2)}) collective-permute-start(bf16[512,128]{1,0:T(8,128)(2,1)S(1)} %get-tuple-element.82), channel_id=1, source_target_pairs={{52,24},{48,28},{44,32},{40,36},{68,8},{64,12},{60,16},{56,20},{11... | collective-permute-start | bytes 393224 | tf_op jit(solution)/shard_map/ppermute | solution.py:435
  58.8 1.3 %collective-permute-start.15 = (bf16[512,128]{1,0:T(8,128)(2,1)S(1)}, bf16[512,128]{1,0:T(8,128)(2,1)S(1)}, u32[]{:S(2)}, u32[]{:S(2)}) collective-permute-start(bf16[512,128]{1,0:T(8,128)(2,1)S(1)} %get-tuple-element.83), channel_id=1, source_target_pairs={{40,8},{44,12},{48,16},{52,20},{56,24},{60,28},{64,32},{68,36},{10... | collective-permute-start | bytes 393224 | tf_op jit(solution)/shard_map/ppermute | solution.py:435
  60.1 4.5 %own_backward.1 = (bf16[768,128]{1,0:T(8,128)(2,1)S(1)}, bf16[768,128]{1,0:T(8,128)(2,1)S(1)}, bf16[768,128]{1,0:T(8,128)(2,1)S(1)}, bf16[768,128]{1,0:T(8,128)(2,1)S(1)}) custom-call(s32[4,3]{1,0:T(4,128)S(1)} %copy-done.1, bf16[1024,1024]{1,0:T(8,128)(2,1)S(1)} %get-tuple-element.60.e0, bf16[512,512]{1,0:T(8,128)(2,1)S(1)} %get-tuple-element.61.e1, ...), custom_call_target="tpu_custom_call" | custom-call | flops 2000000000 | bytes 8388608 | tf_op jit(solution)/shard_map/own_backward/pallas_call | solution.py:72
  64.7 1.3 %collective-permute-start.12 = (bf16[768,128]{1,0:T(8,128)(2,1)S(1)}, bf16[768,128]{1,0:T(8,128)(2,1)S(1)}, u32[]{:S(2)}, u32[]{:S(2)}) collective-permute-start(bf16[768,128]{1,0:T(8,128)(2,1)S(1)} %get-tuple-element.79), channel_id=1, source_target_pairs={{8,12},{12,16},{16,20},{20,8},{24,28},{28,32},{32,36},{36,24},{40,... | collective-permute-start | bytes 589832 | tf_op jit(solution)/shard_map/ppermute | solution.py:425
  66.0 15.4 %collective-permute-done.14.yb = bf16[512,128]{1,0:T(8,128)(2,1)S(1)} collective-permute-done((bf16[512,128]{1,0:T(8,128)(2,1)S(1)}, bf16[512,128]{1,0:T(8,128)(2,1)S(1)}, u32[]{:S(2)}, u32[]{:S(2)}) %collective-permute-start.14) | collective-permute-done | bytes 131104 | tf_op jit(solution)/shard_map/ppermute | solution.py:435
  81.5 11.7 %collective-permute-start.16 = (bf16[768,128]{1,0:T(8,128)(2,1)S(1)}, bf16[768,128]{1,0:T(8,128)(2,1)S(1)}, u32[]{:S(2)}, u32[]{:S(2)}) collective-permute-start(bf16[768,128]{1,0:T(8,128)(2,1)S(1)} %get-tuple-element.84), channel_id=1, source_target_pairs={{8,20},{12,8},{16,12},{20,16},{24,36},{28,24},{32,28},{36,32},{40,... | collective-permute-start | bytes 589832 | tf_op jit(solution)/shard_map/ppermute | solution.py:425
  93.3 1.9 %collective-permute-start.18 = (bf16[384,128]{1,0:T(8,128)(2,1)S(1)}, bf16[384,128]{1,0:T(8,128)(2,1)S(1)}, u32[]{:S(2)}, u32[]{:S(2)}) collective-permute-start(bf16[384,128]{1,0:T(8,128)(2,1)S(1)} %get-tuple-element.91), channel_id=1, source_target_pairs={{8,12},{12,16},{16,20},{20,8},{24,28},{28,32},{32,36},{36,24},{40,... | collective-permute-start | bytes 294920 | tf_op jit(solution)/shard_map/ppermute | solution.py:425
  95.2 4.6 %collective-permute-start.19 = (bf16[384,128]{1,0:T(8,128)(2,1)S(1)}, bf16[384,128]{1,0:T(8,128)(2,1)S(1)}, u32[]{:S(2)}, u32[]{:S(2)}) collective-permute-start(bf16[384,128]{1,0:T(8,128)(2,1)S(1)} %get-tuple-element.93), channel_id=1, source_target_pairs={{8,16},{12,20},{16,8},{20,12},{24,32},{28,36},{32,24},{36,28},{40,... | collective-permute-start | bytes 294920 | tf_op jit(solution)/shard_map/ppermute | solution.py:425
  99.8 1.9 %collective-permute-start.20 = (bf16[384,128]{1,0:T(8,128)(2,1)S(1)}, bf16[384,128]{1,0:T(8,128)(2,1)S(1)}, u32[]{:S(2)}, u32[]{:S(2)}) collective-permute-start(bf16[384,128]{1,0:T(8,128)(2,1)S(1)} %get-tuple-element.94), channel_id=1, source_target_pairs={{8,20},{12,8},{16,12},{20,16},{24,36},{28,24},{32,28},{36,32},{40,... | collective-permute-start | bytes 294920 | tf_op jit(solution)/shard_map/ppermute | solution.py:425
  101.8 1.1 %finish_own.1 = (bf16[256,512]{1,0:T(8,128)(2,1)}, f32[256,512]{1,0:T(8,128)S(1)}, f32[256,512]{1,0:T(8,128)S(1)}) custom-call(bf16[768,128]{1,0:T(8,128)(2,1)S(1)} %get-tuple-element.78.p0, bf16[768,128]{1,0:T(8,128)(2,1)S(1)} %collective-permute-done.12.p1, bf16[768,128]{1,0:T(8,128)(2,1)S(1)} %collective-permute-done.13.p2, ...), custom_call_target="tpu_custom_call" | custom-call | tf_op jit(solution)/shard_map/finish_own/pallas_call | solution.py:72
  102.9 3.1 %collective-permute-done.19.c2 = bf16[384,128]{1,0:T(8,128)(2,1)S(1)} collective-permute-done((bf16[384,128]{1,0:T(8,128)(2,1)S(1)}, bf16[384,128]{1,0:T(8,128)(2,1)S(1)}, u32[]{:S(2)}, u32[]{:S(2)}) %collective-permute-start.19) | collective-permute-done | bytes 98336 | tf_op jit(solution)/shard_map/ppermute | solution.py:425
  105.9 3.4 %collective-permute-done.20.c3 = bf16[384,128]{1,0:T(8,128)(2,1)S(1)} collective-permute-done((bf16[384,128]{1,0:T(8,128)(2,1)S(1)}, bf16[384,128]{1,0:T(8,128)(2,1)S(1)}, u32[]{:S(2)}, u32[]{:S(2)}) %collective-permute-start.20) | collective-permute-done | bytes 98336 | tf_op jit(solution)/shard_map/ppermute | solution.py:425
  109.3 1.8 %finish.1 = (bf16[256,512]{1,0:T(8,128)(2,1)}, bf16[256,512]{1,0:T(8,128)(2,1)}) custom-call(s32[4,3]{1,0:T(4,128)S(1)} %copy-done.1, f32[256,512]{1,0:T(8,128)S(1)} %get-tuple-element.86.in_k, f32[256,512]{1,0:T(8,128)S(1)} %get-tuple-element.87.in_v, bf16[384,128]{1,0:T(8,128)(2,1)S(1)} %get-tuple-element.90.c0, ...), custom_call_target="tpu_custom_call" | custom-call | tf_op jit(solution)/shard_map/finish/pallas_call | solution.py:72
  (24 shorter events, 0.8 us)
Async XLA Ops:
  2.5 7.4 %collective-permute-start.1 = (bf16[256,1024]{1,0:T(8,128)(2,1)}, bf16[256,1024]{1,0:T(8,128)(2,1)S(1)}, u32[]{:S(2)}, u32[]{:S(2)}) collective-permute-start(bf16[256,1024]{1,0:T(8,128)(2,1)} %g0.1), channel_id=1, source_target_pairs={{0,1},{1,0},{2,3},{3,2},{4,5},{5,4},{6,7},{7,6},{8,9},{9,8},{10,11... | collective-permute-start | bytes 1572872 | tf_op jit(solution)/shard_map/ppermute | solution.py:438
  2.6 19.7 %collective-permute-start.4 = (bf16[256,1024]{1,0:T(8,128)(2,1)}, bf16[256,1024]{1,0:T(8,128)(2,1)S(1)}, u32[]{:S(2)}, u32[]{:S(2)}) collective-permute-start(bf16[256,1024]{1,0:T(8,128)(2,1)} %g0.1), channel_id=1, source_target_pairs={{0,2},{1,3},{2,0},{3,1},{4,6},{5,7},{6,4},{7,5},{8,10},{9,11},{10,... | collective-permute-start | bytes 1572872 | tf_op jit(solution)/shard_map/ppermute | solution.py:438
  4.2 18.0 %collective-permute-start.2 = (bf16[768,128]{1,0:T(8,128)(2,1)S(1)}, bf16[768,128]{1,0:T(8,128)(2,1)S(1)}, u32[]{:S(2)}, u32[]{:S(2)}) collective-permute-start(bf16[768,128]{1,0:T(8,128)(2,1)S(1)} %get-tuple-element.55), channel_id=1, source_target_pairs={{8,16},{12,20},{16,8},{20,12},{24,32},{28,36},{32,24},{36,28},{40,... | collective-permute-start | bytes 589832 | tf_op jit(solution)/shard_map/ppermute | solution.py:425
  4.8 17.5 %collective-permute-start.3 = (bf16[768,128]{1,0:T(8,128)(2,1)S(1)}, bf16[768,128]{1,0:T(8,128)(2,1)S(1)}, u32[]{:S(2)}, u32[]{:S(2)}) collective-permute-start(bf16[768,128]{1,0:T(8,128)(2,1)S(1)} %get-tuple-element.56), channel_id=1, source_target_pairs={{8,20},{12,8},{16,12},{20,16},{24,36},{28,24},{32,28},{36,32},{40,... | collective-permute-start | bytes 589832 | tf_op jit(solution)/shard_map/ppermute | solution.py:425
  5.3 17.0 %collective-permute-start = (bf16[768,128]{1,0:T(8,128)(2,1)S(1)}, bf16[768,128]{1,0:T(8,128)(2,1)S(1)}, u32[]{:S(2)}, u32[]{:S(2)}) collective-permute-start(bf16[768,128]{1,0:T(8,128)(2,1)S(1)} %get-tuple-element.51), channel_id=1, source_target_pairs={{8,12},{12,16},{16,20},{20,8},{24,28},{28,32},{32,36},{36,24},{40,... | collective-permute-start | bytes 589832 | tf_op jit(solution)/shard_map/ppermute | solution.py:425
  9.8 1.0 copy-start
  10.9 11.5 %copy-start.1 = (s32[4,3]{1,0:T(4,128)S(1)}, s32[4,3]{1,0:T(4,128)}, u32[]{:S(2)}) copy-start(s32[4,3]{1,0:T(4,128)} %offsets.9) | copy-start | bytes 148
  22.3 2.0 %collective-permute-start.5 = (bf16[256,1024]{1,0:T(8,128)(2,1)S(1)}, bf16[256,1024]{1,0:T(8,128)(2,1)S(1)}, u32[]{:S(2)}, u32[]{:S(2)}) collective-permute-start(bf16[256,1024]{1,0:T(8,128)(2,1)S(1)} %collective-permute-done.4.g2), channel_id=1, source_target_pairs={{0,1},{1,0},{2,3},{3,2},{4,5},{5,4},{6,7},{7,6},{8,9},{9,8},{10,11... | collective-permute-start | bytes 1572872 | tf_op jit(solution)/shard_map/ppermute | solution.py:438
  25.3 29.7 %collective-permute-start.6 = (bf16[1536,128]{1,0:T(8,128)(2,1)S(1)}, bf16[1536,128]{1,0:T(8,128)(2,1)S(1)}, u32[]{:S(2)}, u32[]{:S(2)}) collective-permute-start(bf16[1536,128]{1,0:T(8,128)(2,1)S(1)} %get-tuple-element.66.both), channel_id=1, source_target_pairs={{8,36},{12,32},{16,28},{20,24},{40,68},{44,64},{48,60},{52,56},{72... | collective-permute-start | bytes 1179656 | tf_op jit(solution)/shard_map/ppermute | solution.py:435
  30.7 17.0 %collective-permute-start.10 = (bf16[256,128]{1,0:T(8,128)(2,1)S(1)}, bf16[256,128]{1,0:T(8,128)(2,1)S(1)}, u32[]{:S(2)}, u32[]{:S(2)}) collective-permute-start(bf16[256,128]{1,0:T(8,128)(2,1)S(1)} %get-tuple-element.72), channel_id=1, source_target_pairs={{8,16},{12,20},{16,8},{20,12},{24,32},{28,36},{32,24},{36,28},{40,... | collective-permute-start | bytes 196616 | tf_op jit(solution)/shard_map/ppermute | solution.py:425
  35.5 19.4 %collective-permute-start.8 = (bf16[512,128]{1,0:T(8,128)(2,1)S(1)}, bf16[512,128]{1,0:T(8,128)(2,1)S(1)}, u32[]{:S(2)}, u32[]{:S(2)}) collective-permute-start(bf16[512,128]{1,0:T(8,128)(2,1)S(1)} %get-tuple-element.68), channel_id=1, source_target_pairs={{8,40},{12,44},{16,48},{20,52},{24,56},{28,60},{32,64},{36,68},{72... | collective-permute-start | bytes 393224 | tf_op jit(solution)/shard_map/ppermute | solution.py:435
  42.0 12.9 %collective-permute-start.7 = (bf16[512,128]{1,0:T(8,128)(2,1)S(1)}, bf16[512,128]{1,0:T(8,128)(2,1)S(1)}, u32[]{:S(2)}, u32[]{:S(2)}) collective-permute-start(bf16[512,128]{1,0:T(8,128)(2,1)S(1)} %get-tuple-element.68), channel_id=1, source_target_pairs={{24,52},{28,48},{32,44},{36,40},{8,68},{12,64},{16,60},{20,56},{88... | collective-permute-start | bytes 393224 | tf_op jit(solution)/shard_map/ppermute | solution.py:435
  43.3 11.6 %collective-permute-start.9 = (bf16[256,128]{1,0:T(8,128)(2,1)S(1)}, bf16[256,128]{1,0:T(8,128)(2,1)S(1)}, u32[]{:S(2)}, u32[]{:S(2)}) collective-permute-start(bf16[256,128]{1,0:T(8,128)(2,1)S(1)} %get-tuple-element.65), channel_id=1, source_target_pairs={{8,12},{12,16},{16,20},{20,8},{24,28},{28,32},{32,36},{36,24},{40,... | collective-permute-start | bytes 196616 | tf_op jit(solution)/shard_map/ppermute | solution.py:425
  47.7 7.3 %collective-permute-start.11 = (bf16[256,128]{1,0:T(8,128)(2,1)S(1)}, bf16[256,128]{1,0:T(8,128)(2,1)S(1)}, u32[]{:S(2)}, u32[]{:S(2)}) collective-permute-start(bf16[256,128]{1,0:T(8,128)(2,1)S(1)} %get-tuple-element.73), channel_id=1, source_target_pairs={{8,20},{12,8},{16,12},{20,16},{24,36},{28,24},{32,28},{36,32},{40,... | collective-permute-start | bytes 196616 | tf_op jit(solution)/shard_map/ppermute | solution.py:425
  56.2 37.0 %collective-permute-start.17 = (bf16[1536,128]{1,0:T(8,128)(2,1)S(1)}, bf16[1536,128]{1,0:T(8,128)(2,1)S(1)}, u32[]{:S(2)}, u32[]{:S(2)}) collective-permute-start(bf16[1536,128]{1,0:T(8,128)(2,1)S(1)} %get-tuple-element.88), channel_id=1, source_target_pairs={{36,8},{32,12},{28,16},{24,20},{68,40},{64,44},{60,48},{56,52},{10... | collective-permute-start | bytes 1179656 | tf_op jit(solution)/shard_map/ppermute | solution.py:435
  57.5 23.9 %collective-permute-start.14 = (bf16[512,128]{1,0:T(8,128)(2,1)S(1)}, bf16[512,128]{1,0:T(8,128)(2,1)S(1)}, u32[]{:S(2)}, u32[]{:S(2)}) collective-permute-start(bf16[512,128]{1,0:T(8,128)(2,1)S(1)} %get-tuple-element.82), channel_id=1, source_target_pairs={{52,24},{48,28},{44,32},{40,36},{68,8},{64,12},{60,16},{56,20},{11... | collective-permute-start | bytes 393224 | tf_op jit(solution)/shard_map/ppermute | solution.py:435
  58.8 22.6 %collective-permute-start.15 = (bf16[512,128]{1,0:T(8,128)(2,1)S(1)}, bf16[512,128]{1,0:T(8,128)(2,1)S(1)}, u32[]{:S(2)}, u32[]{:S(2)}) collective-permute-start(bf16[512,128]{1,0:T(8,128)(2,1)S(1)} %get-tuple-element.83), channel_id=1, source_target_pairs={{40,8},{44,12},{48,16},{52,20},{56,24},{60,28},{64,32},{68,36},{10... | collective-permute-start | bytes 393224 | tf_op jit(solution)/shard_map/ppermute | solution.py:435
  64.7 28.5 %collective-permute-start.12 = (bf16[768,128]{1,0:T(8,128)(2,1)S(1)}, bf16[768,128]{1,0:T(8,128)(2,1)S(1)}, u32[]{:S(2)}, u32[]{:S(2)}) collective-permute-start(bf16[768,128]{1,0:T(8,128)(2,1)S(1)} %get-tuple-element.79), channel_id=1, source_target_pairs={{8,12},{12,16},{16,20},{20,8},{24,28},{28,32},{32,36},{36,24},{40,... | collective-permute-start | bytes 589832 | tf_op jit(solution)/shard_map/ppermute | solution.py:425
  66.0 27.2 %collective-permute-start.13 = (bf16[768,128]{1,0:T(8,128)(2,1)S(1)}, bf16[768,128]{1,0:T(8,128)(2,1)S(1)}, u32[]{:S(2)}, u32[]{:S(2)}) collective-permute-start(bf16[768,128]{1,0:T(8,128)(2,1)S(1)} %get-tuple-element.80), channel_id=1, source_target_pairs={{8,16},{12,20},{16,8},{20,12},{24,32},{28,36},{32,24},{36,28},{40,... | collective-permute-start | bytes 589832 | tf_op jit(solution)/shard_map/ppermute | solution.py:425
  81.5 20.3 %collective-permute-start.16 = (bf16[768,128]{1,0:T(8,128)(2,1)S(1)}, bf16[768,128]{1,0:T(8,128)(2,1)S(1)}, u32[]{:S(2)}, u32[]{:S(2)}) collective-permute-start(bf16[768,128]{1,0:T(8,128)(2,1)S(1)} %get-tuple-element.84), channel_id=1, source_target_pairs={{8,20},{12,8},{16,12},{20,16},{24,36},{28,24},{32,28},{36,32},{40,... | collective-permute-start | bytes 589832 | tf_op jit(solution)/shard_map/ppermute | solution.py:425
  93.3 9.6 %collective-permute-start.18 = (bf16[384,128]{1,0:T(8,128)(2,1)S(1)}, bf16[384,128]{1,0:T(8,128)(2,1)S(1)}, u32[]{:S(2)}, u32[]{:S(2)}) collective-permute-start(bf16[384,128]{1,0:T(8,128)(2,1)S(1)} %get-tuple-element.91), channel_id=1, source_target_pairs={{8,12},{12,16},{16,20},{20,8},{24,28},{28,32},{32,36},{36,24},{40,... | collective-permute-start | bytes 294920 | tf_op jit(solution)/shard_map/ppermute | solution.py:425
  95.2 10.7 %collective-permute-start.19 = (bf16[384,128]{1,0:T(8,128)(2,1)S(1)}, bf16[384,128]{1,0:T(8,128)(2,1)S(1)}, u32[]{:S(2)}, u32[]{:S(2)}) collective-permute-start(bf16[384,128]{1,0:T(8,128)(2,1)S(1)} %get-tuple-element.93), channel_id=1, source_target_pairs={{8,16},{12,20},{16,8},{20,12},{24,32},{28,36},{32,24},{36,28},{40,... | collective-permute-start | bytes 294920 | tf_op jit(solution)/shard_map/ppermute | solution.py:425
  99.8 9.5 %collective-permute-start.20 = (bf16[384,128]{1,0:T(8,128)(2,1)S(1)}, bf16[384,128]{1,0:T(8,128)(2,1)S(1)}, u32[]{:S(2)}, u32[]{:S(2)}) collective-permute-start(bf16[384,128]{1,0:T(8,128)(2,1)S(1)} %get-tuple-element.94), channel_id=1, source_target_pairs={{8,20},{12,8},{16,12},{20,16},{24,36},{28,24},{32,28},{36,32},{40,... | collective-permute-start | bytes 294920 | tf_op jit(solution)/shard_map/ppermute | solution.py:425

commit v5 on v4

--- a/solution.py
+++ b/solution.py
@@ -565,7 +565,7 @@
         name="combine",
         flops=10**7,
         bytes_accessed=1 << 20,
-    )(after(ys[0], *own_parts[:3]), *ys[1:])
+    )(after(ys[0], own_parts[1]), *ys[1:])
     cross_parts = [cross_parts[0]] + [
         exchange(cross_parts[s], s, (0, 1, 2)) for s in (1, 2, 3)
     ]

time: 112 us -> 116 us (1.036)
  starting transfers between devices: 55.2 us -> 59.4 us
    ppermute x12, starting transfers between devices: 36.3 us -> 40.5 us  [exchange(): return lax.ppermute(part, 'ctx', route)]
  transfers between devices with their start and end apart: 21 -> 21, of which waited for: 6 -> 6; matrix products, arithmetic and copies ran while one was open for 0% -> 0% of each run, Pallas kernels for 11% -> 10%
where the time goes in v5:
time: 116 us; the launch traced here: 115 us
  starting transfers between devices  59.4 us (51%)
  waiting for transfers between devices  36.1 us (31%)
  Pallas kernels  18 us (16%)
    ppermute x12, starting transfers between devices, exchange(): return lax.ppermute(part, 'ctx', route)  40.5 us
    ppermute x12, waiting for transfers between devices, exchange(): return lax.ppermute(part, 'ctx', route)  19.4 us
    pallas_call x10, Pallas kernels, run(): pl.pallas_call(kernel, out_shape=[jax.ShapeDtypeStruct(shape, dtype) for...  18 us
    ppermute x6, starting transfers between devices, to_blocks(): return lax.ppermute(part, 'ctx', route)  17 us
    ppermute x6, waiting for transfers between devices, to_blocks(): return lax.ppermute(part, 'ctx', route)  15.4 us
  transfers between devices with their start and end apart: 21, of which 6 were waited for; matrix products, arithmetic and copies ran while one was open for 0% of the time, Pallas kernels for 10%

profile of v5, /device:TPU:166, one launch (start us, length us, event | category | flops | bytes accessed | tf_op | source)
XLA Modules:
  0.0 115.4 jit_solution(11650564150080697061)
XLA Ops:
  0.6 1.8 %pack.1 = (bf16[768,128]{1,0:T(8,128)(2,1)S(1)}, bf16[768,128]{1,0:T(8,128)(2,1)S(1)}, bf16[768,128]{1,0:T(8,128)(2,1)S(1)}, bf16[768,128]{1,0:T(8,128)(2,1)S(1)}) custom-call(bf16[256,512]{1,0:T(8,128)(2,1)} %q.1, bf16[256,512]{1,0:T(8,128)(2,1)} %k.1, bf16[256,512]{1,0:T(8,128)(2,1)} %v.1), custom_call_target="tpu_custom_call" | custom-call | flops 200000000 | bytes 2097152 | tf_op jit(solution)/shard_map/pack/pallas_call | solution.py:72
  2.6 1.7 %collective-permute-start.4 = (bf16[256,1024]{1,0:T(8,128)(2,1)}, bf16[256,1024]{1,0:T(8,128)(2,1)S(1)}, u32[]{:S(2)}, u32[]{:S(2)}) collective-permute-start(bf16[256,1024]{1,0:T(8,128)(2,1)} %g0.1), channel_id=1, source_target_pairs={{0,2},{1,3},{2,0},{3,1},{4,6},{5,7},{6,4},{7,5},{8,10},{9,11},{10,... | collective-permute-start | bytes 1572872 | tf_op jit(solution)/shard_map/ppermute | solution.py:438
  4.2 0.6 collective-permute-start.2
  5.3 4.6 %collective-permute-start = (bf16[768,128]{1,0:T(8,128)(2,1)S(1)}, bf16[768,128]{1,0:T(8,128)(2,1)S(1)}, u32[]{:S(2)}, u32[]{:S(2)}) collective-permute-start(bf16[768,128]{1,0:T(8,128)(2,1)S(1)} %get-tuple-element.51), channel_id=1, source_target_pairs={{8,12},{12,16},{16,20},{20,8},{24,28},{28,32},{32,36},{36,24},{40,... | collective-permute-start | bytes 589832 | tf_op jit(solution)/shard_map/ppermute | solution.py:425
  9.8 1.0 copy-done
  10.9 2.2 %grad_near.1 = (f32[256,512]{1,0:T(8,128)S(1)}, bf16[2,512,1024]{2,1,0:T(8,128)(2,1)S(1)}) custom-call(bf16[256,1024]{1,0:T(8,128)(2,1)S(1)} %copy-done, bf16[256,1024]{1,0:T(8,128)(2,1)S(1)} %collective-permute-done.1.g1, bf16[512,4096]{1,0:T(8,128)(2,1)} %w.1), custom_call_target="tpu_custom_call" | custom-call | tf_op jit(solution)/shard_map/grad_near/pallas_call | solution.py:72
  13.1 9.1 %collective-permute-done.2.p2 = bf16[768,128]{1,0:T(8,128)(2,1)S(1)} collective-permute-done((bf16[768,128]{1,0:T(8,128)(2,1)S(1)}, bf16[768,128]{1,0:T(8,128)(2,1)S(1)}, u32[]{:S(2)}, u32[]{:S(2)}) %collective-permute-start.2) | collective-permute-done | bytes 196640 | tf_op jit(solution)/shard_map/ppermute | solution.py:425
  22.4 0.7 gather.1
  23.1 1.2 %collective-permute-done.5.g3 = bf16[256,1024]{1,0:T(8,128)(2,1)S(1)} collective-permute-done((bf16[256,1024]{1,0:T(8,128)(2,1)S(1)}, bf16[256,1024]{1,0:T(8,128)(2,1)S(1)}, u32[]{:S(2)}, u32[]{:S(2)}) %collective-permute-start.5) | collective-permute-done | bytes 524320 | tf_op jit(solution)/shard_map/ppermute | solution.py:438
  24.3 1.0 grad_far.1
  25.3 5.4 %collective-permute-start.6 = (bf16[1536,128]{1,0:T(8,128)(2,1)S(1)}, bf16[1536,128]{1,0:T(8,128)(2,1)S(1)}, u32[]{:S(2)}, u32[]{:S(2)}) collective-permute-start(bf16[1536,128]{1,0:T(8,128)(2,1)S(1)} %get-tuple-element.66.both), channel_id=1, source_target_pairs={{8,36},{12,32},{16,28},{20,24},{40,68},{44,64},{48,60},{52,56},{72... | collective-permute-start | bytes 1179656 | tf_op jit(solution)/shard_map/ppermute | solution.py:435
  30.7 4.9 %collective-permute-start.10 = (bf16[256,128]{1,0:T(8,128)(2,1)S(1)}, bf16[256,128]{1,0:T(8,128)(2,1)S(1)}, u32[]{:S(2)}, u32[]{:S(2)}) collective-permute-start(bf16[256,128]{1,0:T(8,128)(2,1)S(1)} %get-tuple-element.72), channel_id=1, source_target_pairs={{8,16},{12,20},{16,8},{20,12},{24,32},{28,36},{32,24},{36,28},{40,... | collective-permute-start | bytes 196616 | tf_op jit(solution)/shard_map/ppermute | solution.py:425
  35.5 6.5 %collective-permute-start.8 = (bf16[512,128]{1,0:T(8,128)(2,1)S(1)}, bf16[512,128]{1,0:T(8,128)(2,1)S(1)}, u32[]{:S(2)}, u32[]{:S(2)}) collective-permute-start(bf16[512,128]{1,0:T(8,128)(2,1)S(1)} %get-tuple-element.68), channel_id=1, source_target_pairs={{8,40},{12,44},{16,48},{20,52},{24,56},{28,60},{32,64},{36,68},{72... | collective-permute-start | bytes 393224 | tf_op jit(solution)/shard_map/ppermute | solution.py:435
  42.0 1.3 %collective-permute-start.7 = (bf16[512,128]{1,0:T(8,128)(2,1)S(1)}, bf16[512,128]{1,0:T(8,128)(2,1)S(1)}, u32[]{:S(2)}, u32[]{:S(2)}) collective-permute-start(bf16[512,128]{1,0:T(8,128)(2,1)S(1)} %get-tuple-element.68), channel_id=1, source_target_pairs={{24,52},{28,48},{32,44},{36,40},{8,68},{12,64},{16,60},{20,56},{88... | collective-permute-start | bytes 393224 | tf_op jit(solution)/shard_map/ppermute | solution.py:435
  43.3 4.3 %collective-permute-start.9 = (bf16[256,128]{1,0:T(8,128)(2,1)S(1)}, bf16[256,128]{1,0:T(8,128)(2,1)S(1)}, u32[]{:S(2)}, u32[]{:S(2)}) collective-permute-start(bf16[256,128]{1,0:T(8,128)(2,1)S(1)} %get-tuple-element.65), channel_id=1, source_target_pairs={{8,12},{12,16},{16,20},{20,8},{24,28},{28,32},{32,36},{36,24},{40,... | collective-permute-start | bytes 196616 | tf_op jit(solution)/shard_map/ppermute | solution.py:425
  47.7 3.4 %own_forward.1 = (bf16[1024,1024]{1,0:T(8,128)(2,1)S(1)}, bf16[512,512]{1,0:T(8,128)(2,1)S(1)}, bf16[256,256]{1,0:T(8,128)(2,1)S(1)}, f32[1024,128]{1,0:T(8,128)S(1)}, f32[1024,256]{1,0:T(8,128)S(1)}) custom-call(s32[4,3]{1,0:T(4,128)S(1)} %copy-done.1, bf16[1024,128]{1,0:T(8,128)(2,1)S(1)} %get-tuple-element.57.qa, ...), custom_call_target="tpu_custom_call" | custom-call | flops 1000000000 | bytes 6291456 | tf_op jit(solution)/shard_map/own_forward/pallas_call | solution.py:72
  51.1 3.8 %collective-permute-done.11.p3 = bf16[256,128]{1,0:T(8,128)(2,1)S(1)} collective-permute-done((bf16[256,128]{1,0:T(8,128)(2,1)S(1)}, bf16[256,128]{1,0:T(8,128)(2,1)S(1)}, u32[]{:S(2)}, u32[]{:S(2)}) %collective-permute-start.11) | collective-permute-done | bytes 65568 | tf_op jit(solution)/shard_map/ppermute | solution.py:425
  55.0 1.3 %cross.1 = (bf16[1024,128]{1,0:T(8,128)(2,1)S(1)}, f32[1024,128]{1,0:T(8,128)S(1)}, f32[1024,128]{1,0:T(8,128)S(1)}, f32[1024,128]{1,0:T(8,128)S(1)}, bf16[1536,...) custom-call(s32[4,3]{1,0:T(4,128)S(1)} %copy-done.1, ...), custom_call_target="tpu_custom_call" | custom-call | flops 1000000000 | bytes 6291456 | tf_op jit(solution)/shard_map/cross/pallas_call | solution.py:72
  56.2 1.3 %collective-permute-start.17 = (bf16[1536,128]{1,0:T(8,128)(2,1)S(1)}, bf16[1536,128]{1,0:T(8,128)(2,1)S(1)}, u32[]{:S(2)}, u32[]{:S(2)}) collective-permute-start(bf16[1536,128]{1,0:T(8,128)(2,1)S(1)} %get-tuple-element.88), channel_id=1, source_target_pairs={{36,8},{32,12},{28,16},{24,20},{68,40},{64,44},{60,48},{56,52},{10... | collective-permute-start | bytes 1179656 | tf_op jit(solution)/shard_map/ppermute | solution.py:435
  57.5 1.3 %collective-permute-start.14 = (bf16[512,128]{1,0:T(8,128)(2,1)S(1)}, bf16[512,128]{1,0:T(8,128)(2,1)S(1)}, u32[]{:S(2)}, u32[]{:S(2)}) collective-permute-start(bf16[512,128]{1,0:T(8,128)(2,1)S(1)} %get-tuple-element.82), channel_id=1, source_target_pairs={{52,24},{48,28},{44,32},{40,36},{68,8},{64,12},{60,16},{56,20},{11... | collective-permute-start | bytes 393224 | tf_op jit(solution)/shard_map/ppermute | solution.py:435
  58.8 1.3 %collective-permute-start.15 = (bf16[512,128]{1,0:T(8,128)(2,1)S(1)}, bf16[512,128]{1,0:T(8,128)(2,1)S(1)}, u32[]{:S(2)}, u32[]{:S(2)}) collective-permute-start(bf16[512,128]{1,0:T(8,128)(2,1)S(1)} %get-tuple-element.83), channel_id=1, source_target_pairs={{40,8},{44,12},{48,16},{52,20},{56,24},{60,28},{64,32},{68,36},{10... | collective-permute-start | bytes 393224 | tf_op jit(solution)/shard_map/ppermute | solution.py:435
  60.1 4.5 %own_backward.1 = (bf16[768,128]{1,0:T(8,128)(2,1)S(1)}, bf16[768,128]{1,0:T(8,128)(2,1)S(1)}, bf16[768,128]{1,0:T(8,128)(2,1)S(1)}, bf16[768,128]{1,0:T(8,128)(2,1)S(1)}) custom-call(s32[4,3]{1,0:T(4,128)S(1)} %copy-done.1, bf16[1024,1024]{1,0:T(8,128)(2,1)S(1)} %get-tuple-element.60.e0, bf16[512,512]{1,0:T(8,128)(2,1)S(1)} %get-tuple-element.61.e1, ...), custom_call_target="tpu_custom_call" | custom-call | flops 2000000000 | bytes 8388608 | tf_op jit(solution)/shard_map/own_backward/pallas_call | solution.py:72
  64.7 1.3 %collective-permute-start.12 = (bf16[768,128]{1,0:T(8,128)(2,1)S(1)}, bf16[768,128]{1,0:T(8,128)(2,1)S(1)}, u32[]{:S(2)}, u32[]{:S(2)}) collective-permute-start(bf16[768,128]{1,0:T(8,128)(2,1)S(1)} %get-tuple-element.79), channel_id=1, source_target_pairs={{8,12},{12,16},{16,20},{20,8},{24,28},{28,32},{32,36},{36,24},{40,... | collective-permute-start | bytes 589832 | tf_op jit(solution)/shard_map/ppermute | solution.py:425
  66.0 15.4 %collective-permute-done.14.yb = bf16[512,128]{1,0:T(8,128)(2,1)S(1)} collective-permute-done((bf16[512,128]{1,0:T(8,128)(2,1)S(1)}, bf16[512,128]{1,0:T(8,128)(2,1)S(1)}, u32[]{:S(2)}, u32[]{:S(2)}) %collective-permute-start.14) | collective-permute-done | bytes 131104 | tf_op jit(solution)/shard_map/ppermute | solution.py:435
  81.5 15.9 %collective-permute-start.16 = (bf16[768,128]{1,0:T(8,128)(2,1)S(1)}, bf16[768,128]{1,0:T(8,128)(2,1)S(1)}, u32[]{:S(2)}, u32[]{:S(2)}) collective-permute-start(bf16[768,128]{1,0:T(8,128)(2,1)S(1)} %get-tuple-element.84), channel_id=1, source_target_pairs={{8,20},{12,8},{16,12},{20,16},{24,36},{28,24},{32,28},{36,32},{40,... | collective-permute-start | bytes 589832 | tf_op jit(solution)/shard_map/ppermute | solution.py:425
  97.4 1.9 %collective-permute-start.18 = (bf16[384,128]{1,0:T(8,128)(2,1)S(1)}, bf16[384,128]{1,0:T(8,128)(2,1)S(1)}, u32[]{:S(2)}, u32[]{:S(2)}) collective-permute-start(bf16[384,128]{1,0:T(8,128)(2,1)S(1)} %get-tuple-element.91), channel_id=1, source_target_pairs={{8,12},{12,16},{16,20},{20,8},{24,28},{28,32},{32,36},{36,24},{40,... | collective-permute-start | bytes 294920 | tf_op jit(solution)/shard_map/ppermute | solution.py:425
  99.3 4.6 %collective-permute-start.19 = (bf16[384,128]{1,0:T(8,128)(2,1)S(1)}, bf16[384,128]{1,0:T(8,128)(2,1)S(1)}, u32[]{:S(2)}, u32[]{:S(2)}) collective-permute-start(bf16[384,128]{1,0:T(8,128)(2,1)S(1)} %get-tuple-element.93), channel_id=1, source_target_pairs={{8,16},{12,20},{16,8},{20,12},{24,32},{28,36},{32,24},{36,28},{40,... | collective-permute-start | bytes 294920 | tf_op jit(solution)/shard_map/ppermute | solution.py:425
  103.9 1.9 %collective-permute-start.20 = (bf16[384,128]{1,0:T(8,128)(2,1)S(1)}, bf16[384,128]{1,0:T(8,128)(2,1)S(1)}, u32[]{:S(2)}, u32[]{:S(2)}) collective-permute-start(bf16[384,128]{1,0:T(8,128)(2,1)S(1)} %get-tuple-element.94), channel_id=1, source_target_pairs={{8,20},{12,8},{16,12},{20,16},{24,36},{28,24},{32,28},{36,32},{40,... | collective-permute-start | bytes 294920 | tf_op jit(solution)/shard_map/ppermute | solution.py:425
  105.9 1.1 finish_own.1
  107.0 0.9 collective-permute-done.19.c2
  107.9 5.5 %collective-permute-done.20.c3 = bf16[384,128]{1,0:T(8,128)(2,1)S(1)} collective-permute-done((bf16[384,128]{1,0:T(8,128)(2,1)S(1)}, bf16[384,128]{1,0:T(8,128)(2,1)S(1)}, u32[]{:S(2)}, u32[]{:S(2)}) %collective-permute-start.20) | collective-permute-done | bytes 98336 | tf_op jit(solution)/shard_map/ppermute | solution.py:425
  113.5 1.8 %finish.1 = (bf16[256,512]{1,0:T(8,128)(2,1)}, bf16[256,512]{1,0:T(8,128)(2,1)}) custom-call(s32[4,3]{1,0:T(4,128)S(1)} %copy-done.1, f32[256,512]{1,0:T(8,128)S(1)} %get-tuple-element.86.in_k, f32[256,512]{1,0:T(8,128)S(1)} %get-tuple-element.87.in_v, bf16[384,128]{1,0:T(8,128)(2,1)S(1)} %get-tuple-element.90.c0, ...), custom_call_target="tpu_custom_call" | custom-call | tf_op jit(solution)/shard_map/finish/pallas_call | solution.py:72
  (24 shorter events, 0.8 us)
Async XLA Ops:
  2.5 7.4 %collective-permute-start.1 = (bf16[256,1024]{1,0:T(8,128)(2,1)}, bf16[256,1024]{1,0:T(8,128)(2,1)S(1)}, u32[]{:S(2)}, u32[]{:S(2)}) collective-permute-start(bf16[256,1024]{1,0:T(8,128)(2,1)} %g0.1), channel_id=1, source_target_pairs={{0,1},{1,0},{2,3},{3,2},{4,5},{5,4},{6,7},{7,6},{8,9},{9,8},{10,11... | collective-permute-start | bytes 1572872 | tf_op jit(solution)/shard_map/ppermute | solution.py:438
  2.6 19.7 %collective-permute-start.4 = (bf16[256,1024]{1,0:T(8,128)(2,1)}, bf16[256,1024]{1,0:T(8,128)(2,1)S(1)}, u32[]{:S(2)}, u32[]{:S(2)}) collective-permute-start(bf16[256,1024]{1,0:T(8,128)(2,1)} %g0.1), channel_id=1, source_target_pairs={{0,2},{1,3},{2,0},{3,1},{4,6},{5,7},{6,4},{7,5},{8,10},{9,11},{10,... | collective-permute-start | bytes 1572872 | tf_op jit(solution)/shard_map/ppermute | solution.py:438
  4.2 18.0 %collective-permute-start.2 = (bf16[768,128]{1,0:T(8,128)(2,1)S(1)}, bf16[768,128]{1,0:T(8,128)(2,1)S(1)}, u32[]{:S(2)}, u32[]{:S(2)}) collective-permute-start(bf16[768,128]{1,0:T(8,128)(2,1)S(1)} %get-tuple-element.55), channel_id=1, source_target_pairs={{8,16},{12,20},{16,8},{20,12},{24,32},{28,36},{32,24},{36,28},{40,... | collective-permute-start | bytes 589832 | tf_op jit(solution)/shard_map/ppermute | solution.py:425
  4.8 17.5 %collective-permute-start.3 = (bf16[768,128]{1,0:T(8,128)(2,1)S(1)}, bf16[768,128]{1,0:T(8,128)(2,1)S(1)}, u32[]{:S(2)}, u32[]{:S(2)}) collective-permute-start(bf16[768,128]{1,0:T(8,128)(2,1)S(1)} %get-tuple-element.56), channel_id=1, source_target_pairs={{8,20},{12,8},{16,12},{20,16},{24,36},{28,24},{32,28},{36,32},{40,... | collective-permute-start | bytes 589832 | tf_op jit(solution)/shard_map/ppermute | solution.py:425
  5.3 17.0 %collective-permute-start = (bf16[768,128]{1,0:T(8,128)(2,1)S(1)}, bf16[768,128]{1,0:T(8,128)(2,1)S(1)}, u32[]{:S(2)}, u32[]{:S(2)}) collective-permute-start(bf16[768,128]{1,0:T(8,128)(2,1)S(1)} %get-tuple-element.51), channel_id=1, source_target_pairs={{8,12},{12,16},{16,20},{20,8},{24,28},{28,32},{32,36},{36,24},{40,... | collective-permute-start | bytes 589832 | tf_op jit(solution)/shard_map/ppermute | solution.py:425
  9.8 1.0 copy-start
  10.9 11.5 %copy-start.1 = (s32[4,3]{1,0:T(4,128)S(1)}, s32[4,3]{1,0:T(4,128)}, u32[]{:S(2)}) copy-start(s32[4,3]{1,0:T(4,128)} %offsets.9) | copy-start | bytes 148
  22.3 2.0 %collective-permute-start.5 = (bf16[256,1024]{1,0:T(8,128)(2,1)S(1)}, bf16[256,1024]{1,0:T(8,128)(2,1)S(1)}, u32[]{:S(2)}, u32[]{:S(2)}) collective-permute-start(bf16[256,1024]{1,0:T(8,128)(2,1)S(1)} %collective-permute-done.4.g2), channel_id=1, source_target_pairs={{0,1},{1,0},{2,3},{3,2},{4,5},{5,4},{6,7},{7,6},{8,9},{9,8},{10,11... | collective-permute-start | bytes 1572872 | tf_op jit(solution)/shard_map/ppermute | solution.py:438
  25.3 29.7 %collective-permute-start.6 = (bf16[1536,128]{1,0:T(8,128)(2,1)S(1)}, bf16[1536,128]{1,0:T(8,128)(2,1)S(1)}, u32[]{:S(2)}, u32[]{:S(2)}) collective-permute-start(bf16[1536,128]{1,0:T(8,128)(2,1)S(1)} %get-tuple-element.66.both), channel_id=1, source_target_pairs={{8,36},{12,32},{16,28},{20,24},{40,68},{44,64},{48,60},{52,56},{72... | collective-permute-start | bytes 1179656 | tf_op jit(solution)/shard_map/ppermute | solution.py:435
  30.7 17.0 %collective-permute-start.10 = (bf16[256,128]{1,0:T(8,128)(2,1)S(1)}, bf16[256,128]{1,0:T(8,128)(2,1)S(1)}, u32[]{:S(2)}, u32[]{:S(2)}) collective-permute-start(bf16[256,128]{1,0:T(8,128)(2,1)S(1)} %get-tuple-element.72), channel_id=1, source_target_pairs={{8,16},{12,20},{16,8},{20,12},{24,32},{28,36},{32,24},{36,28},{40,... | collective-permute-start | bytes 196616 | tf_op jit(solution)/shard_map/ppermute | solution.py:425
  35.5 19.4 %collective-permute-start.8 = (bf16[512,128]{1,0:T(8,128)(2,1)S(1)}, bf16[512,128]{1,0:T(8,128)(2,1)S(1)}, u32[]{:S(2)}, u32[]{:S(2)}) collective-permute-start(bf16[512,128]{1,0:T(8,128)(2,1)S(1)} %get-tuple-element.68), channel_id=1, source_target_pairs={{8,40},{12,44},{16,48},{20,52},{24,56},{28,60},{32,64},{36,68},{72... | collective-permute-start | bytes 393224 | tf_op jit(solution)/shard_map/ppermute | solution.py:435
  42.0 12.9 %collective-permute-start.7 = (bf16[512,128]{1,0:T(8,128)(2,1)S(1)}, bf16[512,128]{1,0:T(8,128)(2,1)S(1)}, u32[]{:S(2)}, u32[]{:S(2)}) collective-permute-start(bf16[512,128]{1,0:T(8,128)(2,1)S(1)} %get-tuple-element.68), channel_id=1, source_target_pairs={{24,52},{28,48},{32,44},{36,40},{8,68},{12,64},{16,60},{20,56},{88... | collective-permute-start | bytes 393224 | tf_op jit(solution)/shard_map/ppermute | solution.py:435
  43.3 11.6 %collective-permute-start.9 = (bf16[256,128]{1,0:T(8,128)(2,1)S(1)}, bf16[256,128]{1,0:T(8,128)(2,1)S(1)}, u32[]{:S(2)}, u32[]{:S(2)}) collective-permute-start(bf16[256,128]{1,0:T(8,128)(2,1)S(1)} %get-tuple-element.65), channel_id=1, source_target_pairs={{8,12},{12,16},{16,20},{20,8},{24,28},{28,32},{32,36},{36,24},{40,... | collective-permute-start | bytes 196616 | tf_op jit(solution)/shard_map/ppermute | solution.py:425
  47.7 7.3 %collective-permute-start.11 = (bf16[256,128]{1,0:T(8,128)(2,1)S(1)}, bf16[256,128]{1,0:T(8,128)(2,1)S(1)}, u32[]{:S(2)}, u32[]{:S(2)}) collective-permute-start(bf16[256,128]{1,0:T(8,128)(2,1)S(1)} %get-tuple-element.73), channel_id=1, source_target_pairs={{8,20},{12,8},{16,12},{20,16},{24,36},{28,24},{32,28},{36,32},{40,... | collective-permute-start | bytes 196616 | tf_op jit(solution)/shard_map/ppermute | solution.py:425
  56.2 41.1 %collective-permute-start.17 = (bf16[1536,128]{1,0:T(8,128)(2,1)S(1)}, bf16[1536,128]{1,0:T(8,128)(2,1)S(1)}, u32[]{:S(2)}, u32[]{:S(2)}) collective-permute-start(bf16[1536,128]{1,0:T(8,128)(2,1)S(1)} %get-tuple-element.88), channel_id=1, source_target_pairs={{36,8},{32,12},{28,16},{24,20},{68,40},{64,44},{60,48},{56,52},{10... | collective-permute-start | bytes 1179656 | tf_op jit(solution)/shard_map/ppermute | solution.py:435
  57.5 23.9 %collective-permute-start.14 = (bf16[512,128]{1,0:T(8,128)(2,1)S(1)}, bf16[512,128]{1,0:T(8,128)(2,1)S(1)}, u32[]{:S(2)}, u32[]{:S(2)}) collective-permute-start(bf16[512,128]{1,0:T(8,128)(2,1)S(1)} %get-tuple-element.82), channel_id=1, source_target_pairs={{52,24},{48,28},{44,32},{40,36},{68,8},{64,12},{60,16},{56,20},{11... | collective-permute-start | bytes 393224 | tf_op jit(solution)/shard_map/ppermute | solution.py:435
  58.8 22.6 %collective-permute-start.15 = (bf16[512,128]{1,0:T(8,128)(2,1)S(1)}, bf16[512,128]{1,0:T(8,128)(2,1)S(1)}, u32[]{:S(2)}, u32[]{:S(2)}) collective-permute-start(bf16[512,128]{1,0:T(8,128)(2,1)S(1)} %get-tuple-element.83), channel_id=1, source_target_pairs={{40,8},{44,12},{48,16},{52,20},{56,24},{60,28},{64,32},{68,36},{10... | collective-permute-start | bytes 393224 | tf_op jit(solution)/shard_map/ppermute | solution.py:435
  64.7 32.7 %collective-permute-start.12 = (bf16[768,128]{1,0:T(8,128)(2,1)S(1)}, bf16[768,128]{1,0:T(8,128)(2,1)S(1)}, u32[]{:S(2)}, u32[]{:S(2)}) collective-permute-start(bf16[768,128]{1,0:T(8,128)(2,1)S(1)} %get-tuple-element.79), channel_id=1, source_target_pairs={{8,12},{12,16},{16,20},{20,8},{24,28},{28,32},{32,36},{36,24},{40,... | collective-permute-start | bytes 589832 | tf_op jit(solution)/shard_map/ppermute | solution.py:425
  66.0 39.9 %collective-permute-start.13 = (bf16[768,128]{1,0:T(8,128)(2,1)S(1)}, bf16[768,128]{1,0:T(8,128)(2,1)S(1)}, u32[]{:S(2)}, u32[]{:S(2)}) collective-permute-start(bf16[768,128]{1,0:T(8,128)(2,1)S(1)} %get-tuple-element.80), channel_id=1, source_target_pairs={{8,16},{12,20},{16,8},{20,12},{24,32},{28,36},{32,24},{36,28},{40,... | collective-permute-start | bytes 589832 | tf_op jit(solution)/shard_map/ppermute | solution.py:425
  81.5 24.4 %collective-permute-start.16 = (bf16[768,128]{1,0:T(8,128)(2,1)S(1)}, bf16[768,128]{1,0:T(8,128)(2,1)S(1)}, u32[]{:S(2)}, u32[]{:S(2)}) collective-permute-start(bf16[768,128]{1,0:T(8,128)(2,1)S(1)} %get-tuple-element.84), channel_id=1, source_target_pairs={{8,20},{12,8},{16,12},{20,16},{24,36},{28,24},{32,28},{36,32},{40,... | collective-permute-start | bytes 589832 | tf_op jit(solution)/shard_map/ppermute | solution.py:425
  97.4 9.6 %collective-permute-start.18 = (bf16[384,128]{1,0:T(8,128)(2,1)S(1)}, bf16[384,128]{1,0:T(8,128)(2,1)S(1)}, u32[]{:S(2)}, u32[]{:S(2)}) collective-permute-start(bf16[384,128]{1,0:T(8,128)(2,1)S(1)} %get-tuple-element.91), channel_id=1, source_target_pairs={{8,12},{12,16},{16,20},{20,8},{24,28},{28,32},{32,36},{36,24},{40,... | collective-permute-start | bytes 294920 | tf_op jit(solution)/shard_map/ppermute | solution.py:425
  99.3 8.6 %collective-permute-start.19 = (bf16[384,128]{1,0:T(8,128)(2,1)S(1)}, bf16[384,128]{1,0:T(8,128)(2,1)S(1)}, u32[]{:S(2)}, u32[]{:S(2)}) collective-permute-start(bf16[384,128]{1,0:T(8,128)(2,1)S(1)} %get-tuple-element.93), channel_id=1, source_target_pairs={{8,16},{12,20},{16,8},{20,12},{24,32},{28,36},{32,24},{36,28},{40,... | collective-permute-start | bytes 294920 | tf_op jit(solution)/shard_map/ppermute | solution.py:425
  103.9 9.5 %collective-permute-start.20 = (bf16[384,128]{1,0:T(8,128)(2,1)S(1)}, bf16[384,128]{1,0:T(8,128)(2,1)S(1)}, u32[]{:S(2)}, u32[]{:S(2)}) collective-permute-start(bf16[384,128]{1,0:T(8,128)(2,1)S(1)} %get-tuple-element.94), channel_id=1, source_target_pairs={{8,20},{12,8},{16,12},{20,16},{24,36},{28,24},{32,28},{36,32},{40,... | collective-permute-start | bytes 294920 | tf_op jit(solution)/shard_map/ppermute | solution.py:425
